TPU v7x, 512 devices: a whole 4x8x8 slice. The times are simulated.
512 devices in a mesh: section: 4 (over x), rep: 128 (over y, z, core).
Axes of the slice: x: 4, y: 8, z: 8, core: 2. Of those that a mesh axis runs over, the one named last changes fastest.
Arguments:
- tile_features: bfloat16 [256, 16, 16, 512], P('rep'), may hold values from -6 to 6
- patches: bfloat16 [256, 16, 16, 768], P('rep'), may hold values from -6 to 6
- det_kernel: float32 [4, 7, 7, 512], P('section'), may hold values from -0.875 to 0.875
- det_gain: float32 [4, 512], P('section'), may hold values from 0.1 to 1.9
- det_in: bfloat16 [4, 512, 2048], P('section', None, 'rep'), may hold values from -0.25 to 0.25
- det_out: bfloat16 [4, 2048, 512], P('section', 'rep'), may hold values from -0.125 to 0.125
- det_scale: float32 [4, 512], P('section'), may hold values from 0.3 to 1.5
- cls_embed: bfloat16 [768, 1024], P(None, 'section'), may hold values from -0.21875 to 0.21875
- cls_merge: bfloat16 [512, 1024], P(None, 'section'), may hold values from -0.25 to 0.25
- cls_pos: bfloat16 [196, 1024], P(None, 'section'), may hold values from -3 to 3
- cls_qkv: bfloat16 [1024, 3, 512], P(None, None, 'section'), may hold values from -1.5 to 1.5
- cls_out: bfloat16 [512, 1024], P('section'), may hold values from -0.25 to 0.25
- cls_gain: float32 [2, 1024], replicated, may hold values from 0.1 to 1.9
- crop_plan: int32 [128, 4, 3, 3], P('rep'), may hold values from 0 to 2, as said below
- slot_from: int32 [128, 4], P('rep'), may hold values from 0 to 3, as said below
Outputs:
- crop_class: float32 [128, 4, 1024], P('rep', 'section')
Inputs may be any that keep to these rules, and one draw needn't show every extreme that they name: `crop_plan`: each entry is a micro-batch below 2 followed by a top and a left patch offset of 0 to 2; records that no slot names are arbitrary. `slot_from`: 0 marks an empty slot, 1 a crop from the replica one index lower, 2 the replica's own, 3 one from the replica one index higher; the first replica never has 1 and the last never has 3.
All inputs are finite; a program needn't handle non-finite values.
Results may differ from a plain program's by a relative error of at most 0.004.
Values may be sent and summed in bfloat16 or wider, within the bound.
No kernel may reach another device: no remote copies, remote signals or barrier semaphores. Data moves between devices by JAX's collectives and lax.ppermute only.
A program may use at most 64 MiB of HBM per device.

v0:
```python
import math

import jax
import jax.numpy as jnp
from jax import lax
from jax.sharding import PartitionSpec as P

HEAD_DIM = 64
TILE = 16
CROP = 14


epsilon = 1e-06


def passed_along(block, axis, distance):
    devices = range(lax.axis_size(axis))
    route = [(i - distance, i) for i in devices if i - distance in devices]
    return lax.ppermute(block, axis, route)


def spread(value, axis, source):
    kept = jnp.where(lax.axis_index(axis) == source, value, 0).astype(value.dtype)
    return lax.psum(kept, axis)


def padded_2(block, sides, width):
    for axis, dim in sides:
        count = lax.axis_size(axis)
        forward = [(i, i + 1) for i in range(count - 1)]
        backward = [(target, source) for source, target in forward]
        low = lax.ppermute(
            lax.slice_in_dim(block, block.shape[dim] - width, None, axis=dim), axis, forward
        )
        high = lax.ppermute(lax.slice_in_dim(block, 0, width, axis=dim), axis, backward)
        block = jnp.concatenate([low, block, high], axis=dim)
    return block


def layer_norm(values, gain_row):
    row_mean = jnp.mean(values, axis=-1, keepdims=True)
    centred = values - row_mean
    row_var = jnp.mean(centred * centred, axis=-1, keepdims=True)
    return centred * lax.rsqrt(row_var + epsilon) * gain_row


def detector_block(tile_rows, kernel, gain_row, in_weight, out_weight, scale_row):
    widened = tile_rows.astype(jnp.float32)
    padded = jnp.pad(widened, ((3, 3), (3, 3), (0, 0)))
    conv = jnp.zeros_like(widened)
    for row_shift in range(7):
        for col_shift in range(7):
            conv = (
                conv
                + padded[row_shift : row_shift + TILE, col_shift : col_shift + TILE]
                * kernel[row_shift, col_shift]
            )
    normed = layer_norm(conv, gain_row).astype(jnp.bfloat16).reshape(TILE * TILE, -1)
    hidden = jax.nn.gelu(jnp.dot(normed, in_weight, preferred_element_type=jnp.float32)).astype(
        jnp.bfloat16
    )
    update = jnp.dot(hidden, out_weight, preferred_element_type=jnp.float32).reshape(widened.shape)
    return (widened + scale_row * update).astype(jnp.bfloat16)


def per_device(
    tile_features,
    patches,
    det_kernel,
    det_gain,
    det_in,
    det_out,
    det_scale,
    cls_embed,
    cls_merge,
    cls_pos,
    cls_qkv,
    cls_out,
    cls_gain,
    crop_plan,
    slot_from,
):
    sections = lax.axis_size("section")
    section_num = lax.axis_index("section")
    micro_count = tile_features.shape[0]
    in_whole, out_whole = (
        lax.all_gather(det_in, "rep", axis=2, tiled=True),
        lax.all_gather(det_out, "rep", axis=1, tiled=True),
    )
    kernel = det_kernel[0]
    gain_row = det_gain[0]
    scale_row = det_scale[0]
    in_weight = in_whole[0]
    out_weight = out_whole[0]

    def run_block(operand_tile):
        return detector_block(operand_tile, kernel, gain_row, in_weight, out_weight, scale_row)

    def skip_block(operand_tile):
        return jnp.zeros_like(operand_tile)

    def tick(tick_index, loop_state):
        incoming, finals = loop_state
        micro_num = tick_index - section_num
        is_valid = (micro_num >= 0) & (micro_num < micro_count)
        clipped = jnp.clip(micro_num, 0, micro_count - 1)
        fresh_tile = lax.dynamic_index_in_dim(tile_features, clipped, 0, keepdims=False)
        operand = jnp.where(section_num == 0, fresh_tile, incoming)
        result = lax.cond(is_valid, run_block, skip_block, operand)
        stored = lax.dynamic_update_index_in_dim(finals, result, clipped, 0)
        finals = jnp.where(is_valid & (section_num == sections - 1), stored, finals)
        incoming = passed_along(result, "section", 1)
        return (incoming, finals)

    start_state = (
        jnp.zeros(tile_features.shape[1:], jnp.bfloat16),
        jnp.zeros(tile_features.shape, jnp.bfloat16),
    )
    unused_tile, finals = lax.fori_loop(0, micro_count + sections - 1, tick, start_state)
    finals = spread(finals, "section", sections - 1)
    pixel_width = patches.shape[3]
    feat_width = finals.shape[3]
    full_width = cls_gain.shape[1]
    local_width = cls_embed.shape[1]
    local_heads = cls_qkv.shape[2] // HEAD_DIM
    qkv_flat = cls_qkv.reshape(cls_qkv.shape[0], -1)
    gain_first = lax.dynamic_slice_in_dim(cls_gain[0], section_num * local_width, local_width)
    slot_plan = crop_plan[0]
    source = lax.dynamic_index_in_dim(slot_from[0], section_num, 0, keepdims=False)
    zero_index = jnp.int32(0)

    def cut_crop(record):
        pixel_rows = lax.dynamic_slice(
            patches, (record[0], record[1], record[2], zero_index), (1, CROP, CROP, pixel_width)
        ).reshape(CROP * CROP, pixel_width)
        feat_rows = lax.dynamic_slice(
            finals, (record[0], record[1], record[2], zero_index), (1, CROP, CROP, feat_width)
        ).reshape(CROP * CROP, feat_width)
        return (pixel_rows, feat_rows)

    pixel_rows, feat_rows = jax.vmap(cut_crop)(slot_plan.reshape(-1, 3))
    count = pixel_rows.shape[0]
    widened = (
        jnp.einsum("crp,pd->crd", pixel_rows, cls_embed, preferred_element_type=jnp.float32)
        + jnp.einsum("crp,pd->crd", feat_rows, cls_merge, preferred_element_type=jnp.float32)
        + cls_pos.astype(jnp.float32)[None]
    )
    row_sum, row_square = lax.psum(
        (jnp.sum(widened, axis=-1), jnp.sum(widened * widened, axis=-1)), "section"
    )
    row_mean = row_sum / full_width
    row_var = row_square / full_width - row_mean * row_mean
    attn_part = (
        (widened - row_mean[..., None]) * lax.rsqrt(row_var[..., None] + epsilon) * gain_first
    ).astype(jnp.bfloat16)
    attn_in = lax.all_gather(attn_part, "section", axis=2, tiled=True)
    qkv = jnp.einsum("crd,de->cre", attn_in, qkv_flat, preferred_element_type=jnp.float32).astype(
        jnp.bfloat16
    )
    qkv = qkv.reshape(count, CROP * CROP, 3, local_heads, HEAD_DIM)
    query_rows = qkv[:, :, 0]
    key_rows = qkv[:, :, 1]
    value_rows = qkv[:, :, 2]
    scores = jnp.einsum(
        "cqhd,ckhd->chqk", query_rows, key_rows, preferred_element_type=jnp.float32
    ) * (1.0 / math.sqrt(HEAD_DIM))
    top_score = jnp.max(scores, axis=-1, keepdims=True)
    weights = jnp.exp(scores - top_score)
    probs = (weights / jnp.sum(weights, axis=-1, keepdims=True)).astype(jnp.bfloat16)
    context = jnp.einsum(
        "chqk,ckhd->cqhd", probs, value_rows, preferred_element_type=jnp.float32
    ).astype(jnp.bfloat16)
    context_mean = jnp.mean(context.reshape(count, CROP * CROP, -1).astype(jnp.float32), axis=1)
    context_term = jnp.dot(
        context_mean, cls_out.astype(jnp.float32), precision=lax.Precision.HIGHEST
    )
    token_mean = jnp.mean(widened, axis=1)
    placed = lax.dynamic_update_slice_in_dim(
        jnp.zeros((count, full_width), jnp.float32), token_mean, section_num * local_width, 1
    )
    terms = (placed + context_term).reshape(sections, -1)
    pooled = lax.psum_scatter(terms, "section", scatter_dimension=0, tiled=True).reshape(
        -1, full_width
    )
    results = layer_norm(pooled, cls_gain[1])
    outgoing_results = jnp.stack([results[0], results[2]], axis=0)
    extended_results = padded_2(outgoing_results, (("rep", 0),), 1)
    result = jnp.where(
        source == 1, extended_results[0], jnp.where(source == 3, extended_results[3], results[1])
    )
    result = jnp.where(source == 0, jnp.zeros_like(result), result)
    return result[None, None, :]


def solution(mesh):
    return jax.shard_map(
        per_device,
        mesh=mesh,
        in_specs=(
            P("rep", None, None, None),
            P("rep", None, None, None),
            P("section", None, None, None),
            P("section", None),
            P("section", None, "rep"),
            P("section", "rep", None),
            P("section", None),
            P(None, "section"),
            P(None, "section"),
            P(None, "section"),
            P(None, None, "section"),
            P("section", None),
            P(),
            P("rep", None, None, None),
            P("rep", None),
        ),
        out_specs=P("rep", "section", None),
        check_vma=False,
    )
```

profile of v0, /device:TPU:32, one launch (start us, length us, event | category | flops | bytes accessed | tf_op | source)
XLA Modules:
  0.0 480.9 jit_solution(15910834706224890067)
XLA Ops:
  8.1 0.8 copy.37
  9.0 0.9 copy.64
  9.9 52.1 %while.18 = (s32[]{:T(128)}, bf16[2,16,16,768]{3,2,1,0:T(8,128)(2,1)}, s32[12,4]{0,1:T(4,128)S(1)}, bf16[12,1,14,14,768]{4,3,2,1,0:T(8,128)(2,1)}, s32[]{:T(128)}) while((s32[]{:T(128)}, bf16[2,16,16,768]{3,2,1,0:T(8,128)(2,1)}, s32[12,4]{0,1:T(4,128)S(1)}, bf16[12,1,14,14,768]{4,3,2,1,0:T(8,128)(2,1)}, s32[]{:T(128)}) %tuple.126), condition=%wide.while_cond, body=%wide.while_body.sunk | while | flops 2 | bytes 690297 | solution.py:133
  10.6 3.7 bitcast_dynamic-update-slice_fusion.2
  14.9 3.7 bitcast_dynamic-update-slice_fusion.2
  19.2 3.7 bitcast_dynamic-update-slice_fusion.2
  23.6 3.7 bitcast_dynamic-update-slice_fusion.2
  27.9 3.7 bitcast_dynamic-update-slice_fusion.2
  32.3 3.7 bitcast_dynamic-update-slice_fusion.2
  36.6 3.7 bitcast_dynamic-update-slice_fusion.2
  41.0 3.7 bitcast_dynamic-update-slice_fusion.2
  45.3 3.7 bitcast_dynamic-update-slice_fusion.2
  49.6 3.7 bitcast_dynamic-update-slice_fusion.2
  54.0 3.7 bitcast_dynamic-update-slice_fusion.2
  58.3 3.7 bitcast_dynamic-update-slice_fusion.2
  62.0 34.7 %all-gather.4.cloned.1.call-done = bf16[1,512,2048]{1,2,0:T(8,128)(2,1)} async-done(((bf16[1,512,16]{1,2,0:T(8,128)(2,1)}), bf16[1,512,2048]{1,2,0:T(8,128)(2,1)}) %all-gather.4.cloned.1.call-update) | async-done | bytes 2097168 | tf_op jit(solution)/shard_map/all_gather | solution.py:87
  96.7 4.0 copy.39
  100.7 79.0 %all-gather.6.cloned.1.call-done = bf16[1,2048,512]{2,1,0:T(8,128)(2,1)} async-done(((bf16[1,16,512]{2,1,0:T(8,128)(2,1)}), bf16[1,2048,512]{2,1,0:T(8,128)(2,1)}) %all-gather.6.cloned.1.call-update) | async-done | bytes 2097168 | tf_op jit(solution)/shard_map/all_gather | solution.py:88
  179.7 84.6 %while.17 = (s32[]{:T(128)}, bf16[16,16,512]{2,1,0:T(8,128)(2,1)S(1)}, bf16[2,16,16,512]{3,2,1,0:T(8,128)(2,1)S(1)}, s32[]{:T(128)}, pred[]{:T(512)}, /*index=5*...) while((s32[]{:T(128)}, ...), condition=%wide.region_5.6_spmd, body=%wide.region_0.5_spmd.sunk | while | flops 1093009664 | bytes 12373336 | solution.py:119
  179.8 10.3 %conditional.2 = (bf16[16,16,512]{2,1,0:T(8,128)(2,1)}, bf16[1,16,16,512]{3,2,1,0:T(8,128)(2,1)S(1)}) conditional(s32[]{:T(128)} %convert_element_type.74, () %tuple.120, (pred[]{:T(512)}, bf16[2,16,16,512]{3,2,1,0:T(8,128)(2,1)S(1)}, s32[]{:T(128)}, bf16[16,16,512]{2,1,0:T(8,128)(2,1)S(1)}, f32[1,512]{1,0:T(1,128)S(1)}, ...), branch_computations={%region_1.1_spmd, %region_2.4_spmd} | conditional | flops 1092878592 | bytes 10538005 | solution.py:109
  180.0 4.2 fusion.129
  184.6 3.8 fusion.8
  188.4 0.8 add_convert_fusion
  189.2 0.9 copy.68
  190.1 1.3 collective-permute-start
  191.5 6.5 %collective-permute-done = bf16[16,16,512]{2,1,0:T(8,128)(2,1)S(1)} collective-permute-done((bf16[16,16,512]{2,1,0:T(8,128)(2,1)}, bf16[16,16,512]{2,1,0:T(8,128)(2,1)S(1)}, u32[]{:S(2)}, u32[]{:S(2)}) %collective-permute-start) | collective-permute-done | bytes 262176 | tf_op jit(solution)/shard_map/while/body/eval_jaxpr/ppermute | solution.py:19
  198.0 10.3 %conditional.2 = (bf16[16,16,512]{2,1,0:T(8,128)(2,1)}, bf16[1,16,16,512]{3,2,1,0:T(8,128)(2,1)S(1)}) conditional(s32[]{:T(128)} %convert_element_type.74, () %tuple.120, (pred[]{:T(512)}, bf16[2,16,16,512]{3,2,1,0:T(8,128)(2,1)S(1)}, s32[]{:T(128)}, bf16[16,16,512]{2,1,0:T(8,128)(2,1)S(1)}, f32[1,512]{1,0:T(1,128)S(1)}, ...), branch_computations={%region_1.1_spmd, %region_2.4_spmd} | conditional | flops 1092878592 | bytes 10538005 | solution.py:109
  198.1 4.2 fusion.129
  202.8 3.8 fusion.8
  206.6 0.8 add_convert_fusion
  207.4 0.9 copy.68
  208.3 4.3 collective-permute-start
  212.7 5.7 %collective-permute-done = bf16[16,16,512]{2,1,0:T(8,128)(2,1)S(1)} collective-permute-done((bf16[16,16,512]{2,1,0:T(8,128)(2,1)}, bf16[16,16,512]{2,1,0:T(8,128)(2,1)S(1)}, u32[]{:S(2)}, u32[]{:S(2)}) %collective-permute-start) | collective-permute-done | bytes 262176 | tf_op jit(solution)/shard_map/while/body/eval_jaxpr/ppermute | solution.py:19
  218.4 0.7 conditional.2
  218.4 0.7 broadcast.139
  219.2 13.9 %collective-permute-start = (bf16[16,16,512]{2,1,0:T(8,128)(2,1)}, bf16[16,16,512]{2,1,0:T(8,128)(2,1)S(1)}, u32[]{:S(2)}, u32[]{:S(2)}) collective-permute-start(bf16[16,16,512]{2,1,0:T(8,128)(2,1)} %get-tuple-element.531), channel_id=1, source_target_pairs={{0,128},{128,256},{256,384},{1,129},{129,257},{257,385},{2,130},{1... | collective-permute-start | bytes 786440 | tf_op jit(solution)/shard_map/while/body/eval_jaxpr/ppermute | solution.py:19
  233.1 4.8 %collective-permute-done = bf16[16,16,512]{2,1,0:T(8,128)(2,1)S(1)} collective-permute-done((bf16[16,16,512]{2,1,0:T(8,128)(2,1)}, bf16[16,16,512]{2,1,0:T(8,128)(2,1)S(1)}, u32[]{:S(2)}, u32[]{:S(2)}) %collective-permute-start) | collective-permute-done | bytes 262176 | tf_op jit(solution)/shard_map/while/body/eval_jaxpr/ppermute | solution.py:19
  237.9 0.7 conditional.2
  237.9 0.7 broadcast.139
  238.7 4.3 collective-permute-start
  243.1 4.1 collective-permute-done
  247.2 0.7 conditional.2
  247.2 0.7 broadcast.139
  247.9 12.2 %collective-permute-start = (bf16[16,16,512]{2,1,0:T(8,128)(2,1)}, bf16[16,16,512]{2,1,0:T(8,128)(2,1)S(1)}, u32[]{:S(2)}, u32[]{:S(2)}) collective-permute-start(bf16[16,16,512]{2,1,0:T(8,128)(2,1)} %get-tuple-element.531), channel_id=1, source_target_pairs={{0,128},{128,256},{256,384},{1,129},{129,257},{257,385},{2,130},{1... | collective-permute-start | bytes 786440 | tf_op jit(solution)/shard_map/while/body/eval_jaxpr/ppermute | solution.py:19
  260.2 4.1 collective-permute-done
  264.3 1.5 broadcast_select_fusion
  266.1 6.0 %reshape.115 = bf16[12,196,768]{2,1,0:T(8,128)(2,1)} reshape(bf16[12,1,14,14,768]{4,3,2,1,0:T(8,128)(2,1)} %get-tuple-element.289) | data formatting | bytes 7225344 | tf_op jit(solution)/shard_map/vmap()/reshape | solution.py:135
  272.2 3.2 fusion.123
  275.3 52.9 %all-reduce.5.cloned.1.call-done = bf16[2,16,16,512]{3,0,2,1:T(2,128)(2,1)} async-done(((bf16[2,16,16,512]{3,0,2,1:T(2,128)(2,1)}), bf16[2,16,16,512]{3,0,2,1:T(2,128)(2,1)}) %all-reduce.5.cloned.1.call-update) | async-done | bytes 524304 | tf_op jit(solution)/shard_map/psum | solution.py:24
  328.2 12.0 %gather_fusion = bf16[12,14,14,512]{3,0,2,1:T(8,128)(2,1)} fusion(bf16[2,16,16,512]{3,0,2,1:T(2,128)(2,1)} %all-reduce.5.cloned.1.call-done, s32[12]{0:T(128)S(1)} %get-tuple-element.423), kind=kCustom, calls=%fused_computation | custom fusion | bytes 4817088 | tf_op jit(solution)/shard_map/vmap()/gather | solution.py:136
  340.2 6.5 %fusion.128 = (f32[12,256]{1,0:T(8,128)S(1)}, f32[12,196]{1,0:T(8,128)S(1)}, f32[12,196]{1,0:T(8,128)S(1)}, f32[12,196,256]{2,1,0:T(8,128)}) fusion(f32[196,256]{1,0:T(8,128)S(1)} %convert_element_type.50, f32[12,196,256]{2,1,0:T(8,128)S(1)} %fusion.123, bf16[512,256]{1,0:T(8,128)(2,1)S(1)} %copy-done.9, bf16[12,196,512]{2,0,1:T(8,128)(2,1)} %bitcast.131), kind=kOutput, calls=%fused_computation.214 | convolution fusion | flops 620167552 | bytes 7719296 | tf_op jit(solution)/shard_map/crp,pd->crd/dot_general | solution.py:145
  346.7 16.1 %all-reduce.2 = (f32[12,196]{1,0:T(8,128)S(1)}, f32[12,196]{1,0:T(8,128)S(1)}) all-reduce(f32[12,196]{1,0:T(8,128)S(1)} %get-tuple-element.327, f32[12,196]{1,0:T(8,128)S(1)} %get-tuple-element.328), channel_id=1, replica_groups=mesh['section'=4,'rep'=128] {'section'}, use_global_device_ids=true, to_apply=%region_10.11 | all-reduce | flops 4704 | bytes 37632 | tf_op jit(solution)/shard_map/psum | solution.py:148
  362.8 3.0 multiply_convert_fusion.1
  366.2 1.3 dynamic-slice.12
  367.5 61.7 %all-gather.8.cloned.1.call-done = bf16[12,196,1024]{2,1,0:T(8,128)(2,1)} async-done(((bf16[12,196,256]{2,1,0:T(8,128)(2,1)}), bf16[12,196,1024]{2,1,0:T(8,128)(2,1)}) %all-gather.8.cloned.1.call-update) | async-done | bytes 4816912 | tf_op jit(solution)/shard_map/all_gather | solution.py:156
  429.2 6.4 %convolution_convert_fusion = bf16[12,196,384]{2,1,0:T(8,128)(2,1)} fusion(bf16[12,196,1024]{2,1,0:T(8,128)(2,1)} %all-gather.8.cloned.1.call-done, bf16[1024,384,1]{0,1,2:T(8,128)(2,1)S(1)} %bitcast.133), kind=kOutput, calls=%fused_computation.181 | convolution fusion | flops 1850591232 | bytes 7409664 | tf_op jit(solution)/shard_map/crd,de->cre/dot_general | solution.py:157
  435.6 2.7 copy.44
  438.3 0.8 fusion.122
  439.2 4.1 fusion.137
  443.3 0.8 convert_reduce_fusion
  444.5 16.7 %all-reduce.1 = f32[4,3072]{1,0:T(4,128)S(1)} all-reduce(f32[4,3072]{1,0:T(4,128)S(1)} %reshape.119), channel_id=2, replica_groups=mesh['section'=4,'rep'=128] {'section'}, use_global_device_ids=true, to_apply=%region_15.16.clone | all-reduce | flops 12288 | bytes 98304
  462.4 1.9 collective-permute-start.1
  464.3 7.0 %collective-permute-start.2 = (f32[1,1024]{1,0:T(1,128)S(1)}, f32[1,1024]{1,0:T(1,128)S(1)}, u32[]{:S(2)}, u32[]{:S(2)}) collective-permute-start(f32[1,1024]{1,0:T(1,128)S(1)} %get-tuple-element.417), channel_id=1, source_target_pairs={{1,0},{2,1},{3,2},{4,3},{5,4},{6,5},{7,6},{8,7},{9,8},{10,9},{11,1... | collective-permute-start | bytes 12296 | tf_op jit(solution)/shard_map/ppermute | solution.py:35
  473.2 1.2 fusion.126
  (104 shorter events, 14.0 us)
Async XLA Ops:
  6.5 265.6 %copy-start = (bf16[768,256]{1,0:T(8,128)(2,1)S(1)}, bf16[768,256]{1,0:T(8,128)(2,1)}, u32[]{:S(2)}) copy-start(bf16[768,256]{1,0:T(8,128)(2,1)} %param.26) | copy-start | bytes 1179652
  6.5 90.1 %all-gather.4.cloned.1.call-start = ((), (), s32[]{:S(2)}) async-start(), calls=%async_computation | async-start | bytes 2113536 | tf_op jit(solution)/shard_map/all_gather | solution.py:87
  7.3 172.4 %all-gather.6.cloned.1.call-start = ((), (), s32[]{:S(2)}) async-start(), calls=%async_computation.1 | async-start | bytes 2113536 | tf_op jit(solution)/shard_map/all_gather | solution.py:88
  8.0 320.2 %all-reduce.5.cloned.1.call-start = ((), (), s32[]{:S(2)}) async-start(), calls=%async_computation.2 | async-start | bytes 1048576 | tf_op jit(solution)/shard_map/psum | solution.py:24
  96.7 83.1 %copy-start.1 = (bf16[2,16,16,512]{3,2,1,0:T(8,128)(2,1)S(1)}, bf16[2,16,16,512]{3,2,1,0:T(8,128)(2,1)}, u32[]{:S(2)}) copy-start(bf16[2,16,16,512]{3,2,1,0:T(8,128)(2,1)} %param.19) | copy-start | bytes 1572868
  96.7 83.1 %copy-start.5 = (f32[1,512]{1,0:T(1,128)S(1)}, f32[1,512]{1,0:T(1,128)}, u32[]{:S(2)}) copy-start(f32[1,512]{1,0:T(1,128)} %param.25) | copy-start | bytes 6148
  96.7 83.1 %copy-start.6 = (f32[1,512]{1,0:T(1,128)S(1)}, f32[1,512]{1,0:T(1,128)}, u32[]{:S(2)}) copy-start(f32[1,512]{1,0:T(1,128)} %param.22) | copy-start | bytes 6148
  179.7 86.3 %copy-start.7 = (f32[2,1024]{1,0:T(2,128)S(1)}, f32[2,1024]{1,0:T(2,128)}, u32[]{:S(2)}) copy-start(f32[2,1024]{1,0:T(2,128)} %param.31) | copy-start | bytes 24580
  190.1 7.9 %collective-permute-start = (bf16[16,16,512]{2,1,0:T(8,128)(2,1)}, bf16[16,16,512]{2,1,0:T(8,128)(2,1)S(1)}, u32[]{:S(2)}, u32[]{:S(2)}) collective-permute-start(bf16[16,16,512]{2,1,0:T(8,128)(2,1)} %get-tuple-element.531), channel_id=1, source_target_pairs={{0,128},{128,256},{256,384},{1,129},{129,257},{257,385},{2,130},{1... | collective-permute-start | bytes 786440 | tf_op jit(solution)/shard_map/while/body/eval_jaxpr/ppermute | solution.py:19
  208.3 10.1 %collective-permute-start = (bf16[16,16,512]{2,1,0:T(8,128)(2,1)}, bf16[16,16,512]{2,1,0:T(8,128)(2,1)S(1)}, u32[]{:S(2)}, u32[]{:S(2)}) collective-permute-start(bf16[16,16,512]{2,1,0:T(8,128)(2,1)} %get-tuple-element.531), channel_id=1, source_target_pairs={{0,128},{128,256},{256,384},{1,129},{129,257},{257,385},{2,130},{1... | collective-permute-start | bytes 786440 | tf_op jit(solution)/shard_map/while/body/eval_jaxpr/ppermute | solution.py:19
  219.2 18.8 %collective-permute-start = (bf16[16,16,512]{2,1,0:T(8,128)(2,1)}, bf16[16,16,512]{2,1,0:T(8,128)(2,1)S(1)}, u32[]{:S(2)}, u32[]{:S(2)}) collective-permute-start(bf16[16,16,512]{2,1,0:T(8,128)(2,1)} %get-tuple-element.531), channel_id=1, source_target_pairs={{0,128},{128,256},{256,384},{1,129},{129,257},{257,385},{2,130},{1... | collective-permute-start | bytes 786440 | tf_op jit(solution)/shard_map/while/body/eval_jaxpr/ppermute | solution.py:19
  238.7 8.5 %collective-permute-start = (bf16[16,16,512]{2,1,0:T(8,128)(2,1)}, bf16[16,16,512]{2,1,0:T(8,128)(2,1)S(1)}, u32[]{:S(2)}, u32[]{:S(2)}) collective-permute-start(bf16[16,16,512]{2,1,0:T(8,128)(2,1)} %get-tuple-element.531), channel_id=1, source_target_pairs={{0,128},{128,256},{256,384},{1,129},{129,257},{257,385},{2,130},{1... | collective-permute-start | bytes 786440 | tf_op jit(solution)/shard_map/while/body/eval_jaxpr/ppermute | solution.py:19
  247.9 16.4 %collective-permute-start = (bf16[16,16,512]{2,1,0:T(8,128)(2,1)}, bf16[16,16,512]{2,1,0:T(8,128)(2,1)S(1)}, u32[]{:S(2)}, u32[]{:S(2)}) collective-permute-start(bf16[16,16,512]{2,1,0:T(8,128)(2,1)} %get-tuple-element.531), channel_id=1, source_target_pairs={{0,128},{128,256},{256,384},{1,129},{129,257},{257,385},{2,130},{1... | collective-permute-start | bytes 786440 | tf_op jit(solution)/shard_map/while/body/eval_jaxpr/ppermute | solution.py:19
  265.8 163.4 %all-gather.8.cloned.1.call-start = ((), (), s32[]{:S(2)}) async-start(), calls=%async_computation.3 | async-start | bytes 6144000 | tf_op jit(solution)/shard_map/all_gather | solution.py:156
  266.1 6.0 %copy-start.4 = (bf16[196,256]{1,0:T(8,128)(2,1)S(1)}, bf16[196,256]{1,0:T(8,128)(2,1)}, u32[]{:S(2)}) copy-start(bf16[196,256]{1,0:T(8,128)(2,1)} %param.28) | copy-start | bytes 301060
  328.2 12.1 %copy-start.9 = (bf16[512,256]{1,0:T(8,128)(2,1)S(1)}, bf16[512,256]{1,0:T(8,128)(2,1)}, u32[]{:S(2)}) copy-start(bf16[512,256]{1,0:T(8,128)(2,1)} %param.27) | copy-start | bytes 786436
  362.8 3.1 copy-start.2
  443.3 1.0 copy-start.3
  443.3 28.0 %copy-start.8 = (s32[1,4]{1,0:T(1,128)S(1)}, s32[1,4]{1,0:T(1,128)}, u32[]{:S(2)}) copy-start(s32[1,4]{1,0:T(1,128)} %param.33) | copy-start | bytes 52
  462.4 10.8 %collective-permute-start.1 = (f32[1,1024]{1,0:T(1,128)S(1)}, f32[1,1024]{1,0:T(1,128)S(1)}, u32[]{:S(2)}, u32[]{:S(2)}) collective-permute-start(f32[1,1024]{1,0:T(1,128)S(1)} %get-tuple-element.418), channel_id=1, source_target_pairs={{0,1},{1,2},{2,3},{3,4},{4,5},{5,6},{6,7},{7,8},{8,9},{9,10},{10,1... | collective-permute-start | bytes 12296 | tf_op jit(solution)/shard_map/ppermute | solution.py:32
  464.3 8.9 %collective-permute-start.2 = (f32[1,1024]{1,0:T(1,128)S(1)}, f32[1,1024]{1,0:T(1,128)S(1)}, u32[]{:S(2)}, u32[]{:S(2)}) collective-permute-start(f32[1,1024]{1,0:T(1,128)S(1)} %get-tuple-element.417), channel_id=1, source_target_pairs={{1,0},{2,1},{3,2},{4,3},{5,4},{6,5},{7,6},{8,7},{9,8},{10,9},{11,1... | collective-permute-start | bytes 12296 | tf_op jit(solution)/shard_map/ppermute | solution.py:35
Sparse Core Ops, SparseCore 0:
  10.5 86.1 all-gather.3
  99.8 79.7 all-gather.5
  265.9 62.2 all-reduce.4
  366.0 63.1 all-gather.7
where the time goes:
time: 483 us; the launch traced here: 481 us
  waiting for transfers between devices  255 us (53%)
  local copies, waits for them, and re-layouts  85.6 us (18%)
  starting transfers between devices  45.1 us (9%)
  blocking collectives  32.7 us (7%)
  matrix products  25.5 us (5%)
  other arithmetic  22.2 us (5%)
  between operations  14.8 us (3%)
    all_gather x1, waiting for transfers between devices, per_device(): lax.all_gather(det_out, 'rep', axis=1, tiled=True)  79 us
    all_gather x1, waiting for transfers between devices, per_device(): attn_in = lax.all_gather(attn_part, 'section', axis=2, tiled=True)  61.7 us
    psum x1, waiting for transfers between devices, spread(): return lax.psum(kept, axis)  52.9 us
    gather x36, local copies, waits for them, and re-layouts  52 us
    ppermute x5, starting transfers between devices, passed_along(): return lax.ppermute(block, axis, route)  35.9 us
    all_gather x1, waiting for transfers between devices, per_device(): lax.all_gather(det_in, 'rep', axis=2, tiled=True)  34.7 us
    ppermute x5, waiting for transfers between devices, passed_along(): return lax.ppermute(block, axis, route)  25.1 us
    unnamed x1, blocking collectives  16.7 us
  transfers between devices with their start and end apart: 11, of which 9 were waited for; matrix products, arithmetic and copies ran while one was open for 15% of the time, Pallas kernels for 0%

commit v1 on v0

v1 whole, which is shorter than its diff:
```python
import math

import jax
import jax.numpy as jnp
from jax import lax
from jax.experimental import pallas as pl
from jax.experimental.pallas import tpu as pltpu
from jax.sharding import PartitionSpec as P

HEAD_DIM = 64
TILE = 16
CELLS = TILE * TILE
CROP = 14
ROWS = CROP * CROP
PADDED = 208
LANES = 128
SIDE = 8
EPSILON = 1e-06

ANY = pl.BlockSpec(memory_space=pl.ANY)
SMEM = pl.BlockSpec(memory_space=pltpu.SMEM)
VMEM = pl.BlockSpec(memory_space=pltpu.VMEM)


def rep_index(y, z, core):
    return (y * SIDE + z) * 2 + core


def line_groups(first):
    along_z = [[rep_index(y, z, 0 if first else 1) for z in range(SIDE)] for y in range(SIDE)]
    along_y = [[rep_index(y, z, 1 if first else 0) for y in range(SIDE)] for z in range(SIDE)]
    return along_z + along_y


def spread_in_groups(block, groups):
    copies = jnp.broadcast_to(block[None], (SIDE,) + block.shape)
    return lax.all_to_all(copies, "rep", 0, 0, axis_index_groups=groups)


def block_body(flag_ref, tile_ref, param_ref, own_ref, other_ref, out_ref, tile_buf, wide, conv, w_in, w_out, sems):
    @pl.when(flag_ref[0] == 1)
    def _():
        count = own_ref.shape[0]
        copies = [
            pltpu.make_async_copy(own_ref.at[:, 0], w_in.at[pl.ds(0, count)], sems.at[0]),
            pltpu.make_async_copy(other_ref.at[:, 0], w_in.at[pl.ds(count, count)], sems.at[1]),
            pltpu.make_async_copy(own_ref.at[:, 1], w_out.at[pl.ds(0, count)], sems.at[2]),
            pltpu.make_async_copy(other_ref.at[:, 1], w_out.at[pl.ds(count, count)], sems.at[3]),
        ]
        tile_copy = pltpu.make_async_copy(tile_ref, tile_buf, sems.at[4])
        tile_copy.start()
        for copy in copies:
            copy.start()
        slabs = wide.shape[0]
        wide[:, :, 0:8, :] = jnp.zeros((slabs, TILE, 8, LANES), jnp.float32)
        wide[:, :, 24:32, :] = jnp.zeros((slabs, TILE, 8, LANES), jnp.float32)
        tile_copy.wait()
        for slab in range(slabs):
            part = tile_buf[:, slab * LANES : (slab + 1) * LANES].astype(jnp.float32)
            wide[slab, :, 8:24, :] = part.reshape(TILE, TILE, LANES)

        def one_slab(slab, carry):
            sums = [None] * TILE
            for col in range(7):
                taps = [param_ref[slab, pl.ds(row * 7 + col, 1), :] for row in range(7)]
                for source in range(TILE):
                    cells = wide[slab, source, pl.ds(5 + col, TILE), :]
                    for row in range(7):
                        target = source + 3 - row
                        if 0 <= target < TILE:
                            term = cells * taps[row]
                            sums[target] = term if sums[target] is None else sums[target] + term
            for target in range(TILE):
                conv[slab, pl.ds(target * TILE, TILE), :] = sums[target]
            return carry

        lax.fori_loop(0, slabs, one_slab, 0)
        width = slabs * LANES
        total = conv[0]
        for slab in range(1, slabs):
            total = total + conv[slab]
        mean = jnp.sum(total, axis=-1, keepdims=True) / width
        squares = None
        for slab in range(slabs):
            centred = conv[slab] - mean
            squares = centred * centred if squares is None else squares + centred * centred
        scale = lax.rsqrt(jnp.sum(squares, axis=-1, keepdims=True) / width + EPSILON)
        normed = jnp.concatenate(
            [
                ((conv[slab] - mean) * scale * param_ref[slab, pl.ds(49, 1), :]).astype(jnp.bfloat16)
                for slab in range(slabs)
            ],
            axis=1,
        )
        for copy in copies:
            copy.wait()
        update = None
        step = 32
        for chunk in range(0, 2 * count, step):
            into = w_in[pl.ds(chunk, step)].reshape(step * 16, width)
            outof = w_out[pl.ds(chunk, step)].reshape(step * 16, width)
            hidden = lax.dot_general(
                normed, into, (((1,), (1,)), ((), ())), preferred_element_type=jnp.float32
            )
            hidden = jax.nn.gelu(hidden, approximate=True).astype(jnp.bfloat16)
            term = jnp.dot(hidden, outof, preferred_element_type=jnp.float32)
            update = term if update is None else update + term
        for slab in range(slabs):
            part = slice(slab * LANES, (slab + 1) * LANES)
            tile_buf[:, part] = (
                tile_buf[:, part].astype(jnp.float32) + param_ref[slab, pl.ds(50, 1), :] * update[:, part]
            ).astype(jnp.bfloat16)
        result_copy = pltpu.make_async_copy(tile_buf, out_ref, sems.at[4])
        result_copy.start()
        result_copy.wait()


def detector_block(flag, tile, params, own, other):
    cells, width = tile.shape
    slabs = width // LANES
    count = own.shape[0]
    return pl.pallas_call(
        block_body,
        out_shape=jax.ShapeDtypeStruct(tile.shape, jnp.bfloat16),
        in_specs=[SMEM, ANY, VMEM, ANY, ANY],
        out_specs=ANY,
        scratch_shapes=[
            pltpu.VMEM((cells, width), jnp.bfloat16),
            pltpu.VMEM((slabs, TILE, 32, LANES), jnp.float32),
            pltpu.VMEM((slabs, cells, LANES), jnp.float32),
            pltpu.VMEM((2 * count, 16, width), jnp.bfloat16),
            pltpu.VMEM((2 * count, 16, width), jnp.bfloat16),
            pltpu.SemaphoreType.DMA((5,)),
        ],
        name="detector_block",
    )(flag, tile, params, own, other)


def selection(top, left):
    row = lax.broadcasted_iota(jnp.int32, (PADDED, CELLS), 0)
    cell = lax.broadcasted_iota(jnp.int32, (PADDED, CELLS), 1)
    crop_row = (row * 4682) >> 16
    wanted = (top + crop_row) * TILE + left + (row - crop_row * CROP)
    return jnp.where((cell == wanted) & (row < ROWS), 1.0, 0.0).astype(jnp.bfloat16)


def cut_body(plan_ref, *refs):
    groups = (len(refs) - 3) // 2
    out_ref, tiles, sems = refs[2 * groups :]
    place = plan_ref[9]
    for group in range(groups):

        @pl.when(place == group)
        def _(group=group):
            copies = [
                pltpu.make_async_copy(refs[2 * group + micro], tiles.at[micro], sems.at[micro])
                for micro in range(2)
            ]
            for copy in copies:
                copy.start()
            for copy in copies:
                copy.wait()

    for turn in range(3):
        chosen = selection(plan_ref[3 * turn + 1], plan_ref[3 * turn + 2])
        rows = jnp.dot(chosen, tiles[plan_ref[3 * turn]], preferred_element_type=jnp.float32)
        out_ref[turn] = rows.astype(jnp.bfloat16)


def cut_crops(plan, place, tile_pairs):
    cells, width = tile_pairs[0][0].shape
    scalars = jnp.concatenate([plan.reshape(-1), place.reshape(1)]).astype(jnp.int32)
    return pl.pallas_call(
        cut_body,
        out_shape=jax.ShapeDtypeStruct((3, PADDED, width), jnp.bfloat16),
        in_specs=[SMEM] + [ANY] * (2 * len(tile_pairs)),
        out_specs=VMEM,
        scratch_shapes=[pltpu.VMEM((2, cells, width), jnp.bfloat16), pltpu.SemaphoreType.DMA((2,))],
        name="cut_crops",
    )(scalars, *[tile for pair in tile_pairs for tile in pair])


def classify_body(source_ref, pix_own, pix_left, pix_right, feat_own, feat_left, feat_right, weight_ref, gain_ref, out_ref, pix, feat, weights, sems):
    source = source_ref[0]
    sections, rows, lanes = weight_ref.shape
    weight_copies = []
    embed_to, merge_to, pos_to, qkv_to = 1536, 2560, 2976, 6048
    for part, (low, high) in enumerate(((0, pos_to), (pos_to, qkv_to), (qkv_to, rows))):
        weight_copies.append(
            pltpu.make_async_copy(
                weight_ref.at[:, pl.ds(low, high - low)],
                weights.at[:, pl.ds(low, high - low)],
                sems.at[part],
            )
        )
    for copy in weight_copies:
        copy.start()
    for number, (pix_ref, feat_ref) in enumerate(
        ((pix_left, feat_left), (pix_own, feat_own), (pix_right, feat_right))
    ):

        @pl.when((source == number + 1) if number != 1 else ((source == 2) | (source == 0)))
        def _(pix_ref=pix_ref, feat_ref=feat_ref):
            first = pltpu.make_async_copy(pix_ref, pix, sems.at[3])
            second = pltpu.make_async_copy(feat_ref, feat, sems.at[4])
            first.start()
            second.start()
            first.wait()
            second.wait()

    weight_copies[0].wait()
    pixel_rows = pix[...]
    feat_rows = feat[...]

    def columns(section, low, height):
        return jnp.concatenate(
            [weights[section, pl.ds(low, height), :], weights[section, pl.ds(low + height, height), :]],
            axis=1,
        )

    parts = []
    for section in range(sections):
        parts.append(
            jnp.dot(pixel_rows, columns(section, 0, 768), preferred_element_type=jnp.float32)
            + jnp.dot(feat_rows, columns(section, embed_to, 512), preferred_element_type=jnp.float32)
            + columns(section, merge_to, PADDED).astype(jnp.float32)
        )
    tokens = jnp.concatenate(parts, axis=1)
    width = tokens.shape[1]
    mean = jnp.sum(tokens, axis=-1, keepdims=True) / width
    centred = tokens - mean
    var = jnp.sum(centred * centred, axis=-1, keepdims=True) / width
    attn_in = (centred * lax.rsqrt(var + EPSILON) * gain_ref[pl.ds(0, 1), :]).astype(jnp.bfloat16)
    token_sum = jnp.sum(tokens, axis=0, keepdims=True)
    weight_copies[1].wait()
    key_ok = lax.broadcasted_iota(jnp.int32, (PADDED, PADDED), 1) < ROWS
    lane = lax.broadcasted_iota(jnp.int32, (PADDED, 2 * HEAD_DIM), 1)
    row_ok = lax.broadcasted_iota(jnp.int32, (PADDED, 2 * HEAD_DIM), 0) < ROWS
    context_sums = []
    for section in range(sections):
        piece = jnp.concatenate(
            [weights[section, pl.ds(pos_to + 1024 * index, 1024), :] for index in range(3)], axis=1
        )
        qkv = jnp.dot(attn_in, piece, preferred_element_type=jnp.float32).astype(jnp.bfloat16)
        query, key, value = qkv[:, :128], qkv[:, 128:256], qkv[:, 256:]
        contexts = []
        for head in range(2):
            mine = (lane >= HEAD_DIM) if head else (lane < HEAD_DIM)
            scores = lax.dot_general(
                jnp.where(mine, query, jnp.zeros_like(query)),
                key,
                (((1,), (1,)), ((), ())),
                preferred_element_type=jnp.float32,
            ) * (1.0 / math.sqrt(HEAD_DIM))
            scores = jnp.where(key_ok, scores, -jnp.inf)
            top = jnp.max(scores, axis=-1, keepdims=True)
            numer = jnp.exp(scores - top)
            probs = (numer * (1.0 / jnp.sum(numer, axis=-1, keepdims=True))).astype(jnp.bfloat16)
            contexts.append(jnp.dot(probs, value, preferred_element_type=jnp.float32))
        context = jnp.where(lane < HEAD_DIM, contexts[0], contexts[1]).astype(jnp.bfloat16)
        context = jnp.where(row_ok, context.astype(jnp.float32), 0.0)
        context_sums.append(jnp.sum(context, axis=0, keepdims=True))
    context_mean = jnp.concatenate(context_sums, axis=1) / ROWS
    high = context_mean.astype(jnp.bfloat16)
    rest = context_mean - high.astype(jnp.float32)
    middle = rest.astype(jnp.bfloat16)
    low = (rest - middle.astype(jnp.float32)).astype(jnp.bfloat16)
    pieces = jnp.concatenate([high, middle, low, jnp.zeros((13, high.shape[1]), jnp.bfloat16)], axis=0)
    weight_copies[2].wait()
    out_weight = jnp.concatenate(
        [
            jnp.concatenate(
                [weights[section, pl.ds(qkv_to + 128 * column, 128), :] for column in range(8)], axis=1
            )
            for section in range(sections)
        ],
        axis=0,
    )
    mixed = jnp.dot(pieces, out_weight, preferred_element_type=jnp.float32)
    pooled = token_sum / ROWS + jnp.sum(mixed, axis=0, keepdims=True)
    pooled_mean = jnp.sum(pooled, axis=-1, keepdims=True) / width
    centred = pooled - pooled_mean
    var = jnp.sum(centred * centred, axis=-1, keepdims=True) / width
    result = centred * lax.rsqrt(var + EPSILON) * gain_ref[pl.ds(1, 1), :]
    out_ref[...] = jnp.where(source == 0, 0.0, result)


def classify(source, pixels, feats, weights, gain):
    return pl.pallas_call(
        classify_body,
        out_shape=jax.ShapeDtypeStruct((1, gain.shape[1]), jnp.float32),
        in_specs=[SMEM] + [ANY] * 7 + [VMEM],
        out_specs=VMEM,
        scratch_shapes=[
            pltpu.VMEM(pixels[0].shape, jnp.bfloat16),
            pltpu.VMEM(feats[0].shape, jnp.bfloat16),
            pltpu.VMEM(weights.shape, jnp.bfloat16),
            pltpu.SemaphoreType.DMA((5,)),
        ],
        name="classify",
    )(source.reshape(1), *pixels, *feats, weights, gain)


def exchanged(crops):
    count = lax.axis_size("rep")
    upward = [(index, index + 1) for index in range(count - 1)]
    downward = [(target, origin) for origin, target in upward]
    return (
        crops[1],
        lax.ppermute(crops[2], "rep", upward),
        lax.ppermute(crops[0], "rep", downward),
    )


def per_device(
    tile_features,
    patches,
    det_kernel,
    det_gain,
    det_in,
    det_out,
    det_scale,
    cls_embed,
    cls_merge,
    cls_pos,
    cls_qkv,
    cls_out,
    cls_gain,
    crop_plan,
    slot_from,
):
    sections = lax.axis_size("section")
    section = lax.axis_index("section")
    width = tile_features.shape[3]
    slabs = width // LANES

    shard = jnp.stack([det_in[0].T, det_out[0]], axis=0)
    line = spread_in_groups(shard, line_groups(True))
    plane = spread_in_groups(line, line_groups(False))
    own = plane.reshape((SIDE * SIDE,) + shard.shape)
    swap = [(index, index ^ 1) for index in range(lax.axis_size("rep"))]
    other = lax.ppermute(own, "rep", swap)

    pos = jnp.pad(cls_pos, ((0, PADDED - ROWS), (0, 0)))
    packed = jnp.concatenate(
        [
            cls_embed[:, :LANES],
            cls_embed[:, LANES:],
            cls_merge[:, :LANES],
            cls_merge[:, LANES:],
            pos[:, :LANES],
            pos[:, LANES:],
            cls_qkv[:, 0],
            cls_qkv[:, 1],
            cls_qkv[:, 2],
        ]
        + [cls_out[:, column * LANES : (column + 1) * LANES] for column in range(8)],
        axis=0,
    )
    weights = lax.all_gather(packed, "section", axis=0)

    plan = lax.dynamic_index_in_dim(crop_plan[0], section, 0, keepdims=False)
    source = lax.dynamic_index_in_dim(slot_from[0], section, 0, keepdims=False)
    patch_tiles = patches.reshape(2, CELLS, patches.shape[3])
    pixels = exchanged(cut_crops(plan, jnp.int32(0), [(patch_tiles[0], patch_tiles[1])]))

    params = jnp.concatenate(
        [det_kernel[0].reshape(49, width), det_gain, det_scale, jnp.zeros((5, width), jnp.float32)], axis=0
    )
    params = params.reshape(56, slabs, LANES).transpose(1, 0, 2)
    start = tile_features.reshape(2, CELLS, width)
    tiles = [start[0], start[1]]
    for number in range(sections):
        flag = (section == number).astype(jnp.int32).reshape(1)
        tiles = [detector_block(flag, tile, params, own, other) for tile in tiles]
        if number + 1 < sections:
            tiles = [lax.ppermute(tile, "section", [(number, number + 1)]) for tile in tiles]
    last = sections - 1
    pairs = [
        [lax.ppermute(tile, "section", [(last, target)]) for tile in tiles] for target in range(last)
    ]
    feats = exchanged(cut_crops(plan, section, pairs + [tiles]))
    result = classify(source, pixels, feats, weights, cls_gain)
    return result[None]


def solution(mesh):
    return jax.shard_map(
        per_device,
        mesh=mesh,
        in_specs=(
            P("rep", None, None, None),
            P("rep", None, None, None),
            P("section", None, None, None),
            P("section", None),
            P("section", None, "rep"),
            P("section", "rep", None),
            P("section", None),
            P(None, "section"),
            P(None, "section"),
            P(None, "section"),
            P(None, None, "section"),
            P("section", None),
            P(),
            P("rep", None, None, None),
            P("rep", None),
        ),
        out_specs=P("rep", "section", None),
        check_vma=False,
    )
```

time: 483 us -> 204 us (0.42)
  the two profiles are of different devices: /device:TPU:32 before, /device:TPU:14 now
where the time goes in v1:
time: 204 us; the launch traced here: 203 us
  blocking collectives  56.8 us (28%)
  waiting for transfers between devices  44.1 us (22%)
  Pallas kernels  35 us (17%)
  starting transfers between devices  30.6 us (15%)
  local copies, waits for them, and re-layouts  20.7 us (10%)
  between operations  14.1 us (7%)
    all_to_all x2, blocking collectives, spread_in_groups(): return lax.all_to_all(copies, 'rep', 0, 0, axis_index_groups=groups)  56.8 us
    ppermute x6, waiting for transfers between devices, per_device(): lax.ppermute(tile, 'section', [(number, number + 1)])  39 us
    pallas_call x8, Pallas kernels, detector_block(): pl.pallas_call(block_body, out_shape=jax.ShapeDtypeStruct(tile.shape, jnp...  19.7 us
    unnamed x74, local copies, waits for them, and re-layouts  13.7 us
    ppermute x2, starting transfers between devices, exchanged(): lax.ppermute(crops[0], 'rep', downward)  11.7 us
    pallas_call x1, Pallas kernels, classify(): pl.pallas_call(classify_body, out_shape=jax.ShapeDtypeStruct((1, gain.sha...  8.88 us
    ppermute x6, starting transfers between devices, per_device(): lax.ppermute(tile, 'section', [(last, target)])  7.82 us
    pallas_call x2, Pallas kernels, cut_crops(): pl.pallas_call(cut_body, out_shape=jax.ShapeDtypeStruct((3, PADDED, width...  6.35 us
  transfers between devices with their start and end apart: 18, of which 4 were waited for; matrix products, arithmetic and copies ran while one was open for 4% of the time, Pallas kernels for 13%

profile of v1, /device:TPU:14, one launch (start us, length us, event | category | flops | bytes accessed | tf_op | source)
XLA Modules:
  0.0 202.6 jit_solution(17349586850079620327)
XLA Ops:
  6.5 1.0 slice_dynamic-update-slice_fusion.1
  7.6 1.0 slice_dynamic-update-slice_fusion
  8.5 0.9 slice_dynamic-update-slice_fusion.3
  9.5 0.9 slice_dynamic-update-slice_fusion.2
  10.4 0.8 fusion
  11.2 0.8 fusion.1
  12.0 1.0 bitcast_dynamic-update-slice_fusion.2
  13.4 1.3 copy-done.2
  14.7 0.0 all-gather.3.cloned.1.call-update
  14.7 20.6 %all_to_all.10 = bf16[8,2,16,512]{3,2,1,0:T(8,128)(2,1)S(1)} all-to-all(bf16[8,2,16,512]{3,2,1,0:T(8,128)(2,1)S(1)} %broadcast_in_dim.9), channel_id=1, replica_groups={{0,2,4,6,8,10,12,14},{16,18,20,22,24,26,28,30},{32,34,36,38,40,42,44,46..., dimensions={0} | all-to-all | bytes 524288 | tf_op jit(solution)/shard_map/all_to_all | solution.py:37
  35.3 0.2 broadcast_in_dim.20
  35.6 36.2 %all_to_all.11 = bf16[8,8,2,16,512]{4,3,2,1,0:T(8,128)(2,1)S(1)} all-to-all(bf16[8,8,2,16,512]{4,3,2,1,0:T(8,128)(2,1)S(1)} %broadcast_in_dim.20), channel_id=1, replica_groups={{1,3,5,7,9,11,13,15},{17,19,21,23,25,27,29,31},{33,35,37,39,41,43,45,47..., dimensions={0} | all-to-all | bytes 4194304 | tf_op jit(solution)/shard_map/all_to_all | solution.py:37
  71.8 1.9 collective-permute-start.2
  73.8 0.1 pad.10.clone
  73.9 0.7 maximum_bitcast_fusion.param_ref
  74.6 0.8 fusion.3
  75.4 2.6 %collective-permute-done.2.other_ref = bf16[64,2,16,512]{3,2,1,0:T(8,128)(2,1)} collective-permute-done((bf16[64,2,16,512]{3,2,1,0:T(8,128)(2,1)S(1)}, bf16[64,2,16,512]{3,2,1,0:T(8,128)(2,1)}, u32[]{:S(2)}, u32[]{:S(2)}) %collective-permute-start.2) | collective-permute-done | bytes 2097184 | tf_op jit(solution)/shard_map/ppermute | solution.py:342
  78.0 0.9 detector_block.12
  78.9 0.7 collective-permute-start.7
  79.6 1.0 detector_block.8
  80.6 0.7 collective-permute-start.3
  81.3 0.7 copy-done.19
  82.0 0.9 detector_block.13
  82.9 0.7 collective-permute-start.8
  83.7 0.7 copy-done.15
  84.4 0.9 detector_block.9
  85.3 0.7 collective-permute-start.4
  86.0 0.7 copy-done.16
  86.7 0.9 detector_block.14
  87.7 1.3 collective-permute-start.9
  89.0 0.7 copy-done.17
  89.7 0.9 detector_block.10
  90.6 1.3 collective-permute-start.5
  91.9 39.0 %collective-permute-done.9.tile_ref = bf16[256,512]{1,0:T(8,128)(2,1)S(1)} collective-permute-done((bf16[256,512]{1,0:T(8,128)(2,1)}, bf16[256,512]{1,0:T(8,128)(2,1)S(1)}, u32[]{:S(2)}, u32[]{:S(2)}) %collective-permute-start.9) | collective-permute-done | bytes 262176 | tf_op jit(solution)/shard_map/ppermute | solution.py:377
  130.9 0.7 copy-done.18
  131.6 7.1 %detector_block.15.refs_7_ = bf16[256,512]{1,0:T(8,128)(2,1)} custom-call(s32[1]{0:T(128)} %bitcast.7.flag_ref, bf16[256,512]{1,0:T(8,128)(2,1)} %copy-done.18, f32[4,56,128]{2,1,0:T(8,128)} %maximum_bitcast_fusion.param_ref, bf16[64,2,16,512]{3,2,1,0:T(8,128)(2,1)} %bitcast.48, bf16[64,2,16,512]{3,2,1,0:T(8,128)(2,1)} %collective-permute-done.2.other_ref), custom_call_target="tpu_custom_call" | custom-call | tf_op jit(solution)/shard_map/detector_block/pallas_call | solution.py:122
  138.7 1.3 collective-permute-start.10
  140.0 0.3 dynamic-slice_reduce_fusion
  140.4 0.1 reshape.53
  140.5 0.9 fusion.2
  141.4 1.3 collective-permute-start.12
  142.7 1.3 collective-permute-start.14
  144.0 0.7 copy-done.14
  144.7 7.0 %detector_block.11.refs_6_ = bf16[256,512]{1,0:T(8,128)(2,1)} custom-call(s32[1]{0:T(128)} %bitcast.7.flag_ref, bf16[256,512]{1,0:T(8,128)(2,1)} %copy-done.14, f32[4,56,128]{2,1,0:T(8,128)} %maximum_bitcast_fusion.param_ref, bf16[64,2,16,512]{3,2,1,0:T(8,128)(2,1)} %bitcast.49, bf16[64,2,16,512]{3,2,1,0:T(8,128)(2,1)} %collective-permute-done.2.other_ref), custom_call_target="tpu_custom_call" | custom-call | tf_op jit(solution)/shard_map/detector_block/pallas_call | solution.py:122
  151.7 1.3 collective-permute-start.11
  153.0 1.3 collective-permute-start.13
  154.4 1.3 collective-permute-start.6
  155.7 0.7 pad_add_fusion.1
  156.4 3.3 %cut_crops.2 = bf16[3,208,768]{2,1,0:T(8,128)(2,1)} custom-call(s32[10]{0:T(128)} %get-tuple-element.16.plan_ref, bf16[256,768]{1,0:T(8,128)(2,1)} %bitcast.52, bf16[256,768]{1,0:T(8,128)(2,1)} %bitcast.51), custom_call_target="tpu_custom_call" | custom-call | tf_op jit(solution)/shard_map/cut_crops/pallas_call | solution.py:173
  159.6 2.0 slice_bitcast_fusion
  161.6 1.9 collective-permute-start
  163.6 5.8 %collective-permute-start.1 = (bf16[208,768]{1,0:T(8,128)(2,1)S(1)}, bf16[208,768]{1,0:T(8,128)(2,1)S(1)}, u32[]{:S(2)}, u32[]{:S(2)}) collective-permute-start(bf16[208,768]{1,0:T(8,128)(2,1)S(1)} %get-tuple-element.5), channel_id=1, source_target_pairs={{1,0},{2,1},{3,2},{4,3},{5,4},{6,5},{7,6},{8,7},{9,8},{10,9},{11,1... | collective-permute-start | bytes 958472 | tf_op jit(solution)/shard_map/ppermute | solution.py:311
  169.4 0.6 copy-done.11
  170.0 0.1 copy-done.12
  170.1 0.1 copy-done.13
  170.2 3.1 %cut_crops.3 = bf16[3,208,512]{2,1,0:T(8,128)(2,1)} custom-call(s32[10]{0:T(128)} %get-tuple-element.15.plan_ref, bf16[256,512]{1,0:T(8,128)(2,1)} %copy-done.13, bf16[256,512]{1,0:T(8,128)(2,1)} %copy-done.8, bf16[256,512]{1,0:T(8,128)(2,1)} %copy-done.11, bf16[256,512]{1,0:T(8,128)(2,1)} %copy-done.9, bf16[256,512]{1,0:T(8,128)(2,1)} %copy-done.12, ...), custom_call_target="tpu_custom_call" | custom-call | tf_op jit(solution)/shard_map/cut_crops/pallas_call | solution.py:173
  173.3 1.9 slice_bitcast_fusion.3
  175.2 1.9 collective-permute-start.15
  177.1 6.0 %collective-permute-start.16 = (bf16[208,512]{1,0:T(8,128)(2,1)S(1)}, bf16[208,512]{1,0:T(8,128)(2,1)S(1)}, u32[]{:S(2)}, u32[]{:S(2)}) collective-permute-start(bf16[208,512]{1,0:T(8,128)(2,1)S(1)} %get-tuple-element.10), channel_id=1, source_target_pairs={{1,0},{2,1},{3,2},{4,3},{5,4},{6,5},{7,6},{8,7},{9,8},{10,9},{11,1... | collective-permute-start | bytes 638984 | tf_op jit(solution)/shard_map/ppermute | solution.py:311
  183.1 0.6 constant_dynamic-slice_fusion
  183.7 0.7 collective-permute-done.15.feat_left
  184.5 1.8 collective-permute-done.16.feat_right
  186.2 0.6 copy-done.22
  186.9 8.9 %classify.1 = f32[1,1024]{1,0:T(1,128)} custom-call(s32[1]{0:T(128)} %bitcast.source_ref, bf16[208,768]{1,0:T(8,128)(2,1)} %get-tuple-element.7.pix_own, bf16[208,768]{1,0:T(8,128)(2,1)} %copy-done.6, bf16[208,768]{1,0:T(8,128)(2,1)} %copy-done.7, bf16[208,512]{1,0:T(8,128)(2,1)} %get-tuple-element.12.feat_own, bf16[208,512]{1,0:T(8,128)(2,1)} %copy-done.21, ...), custom_call_target="tpu_custom_call" | custom-call | tf_op jit(solution)/shard_map/classify/pallas_call | solution.py:289
  (76 shorter events, 0.4 us)
Async XLA Ops:
  6.5 133.5 %copy-start = (s32[1,4,3,3]{1,0,3,2:T(1,128)S(1)}, s32[1,4,3,3]{1,0,3,2:T(1,128)}, u32[]{:S(2)}) copy-start(s32[1,4,3,3]{1,0,3,2:T(1,128)} %param.28) | copy-start | bytes 436
  6.5 6.5 %copy-start.4 = (bf16[1024,3,128]{2,0,1:T(8,128)(2,1)S(1)}, bf16[1024,3,128]{2,0,1:T(8,128)(2,1)}, u32[]{:S(2)}) copy-start(bf16[1024,3,128]{2,0,1:T(8,128)(2,1)} %param.25) | copy-start | bytes 2359300
  6.5 6.6 %copy-start.20 = (bf16[128,1024]{1,0:T(8,128)(2,1)S(1)}, bf16[128,1024]{1,0:T(8,128)(2,1)}, u32[]{:S(2)}) copy-start(bf16[128,1024]{1,0:T(8,128)(2,1)} %param.26) | copy-start | bytes 786436
  6.5 179.7 %all-gather.3.cloned.1.call-start = ((), (), s32[]{:S(2)}) async-start(), calls=%async_computation.2 | async-start | bytes 9052160 | tf_op jit(solution)/shard_map/all_gather | solution.py:360
  13.0 1.6 copy-start.24
  13.0 1.6 copy-start.25
  13.4 1.3 copy-start.2
  35.6 38.1 %copy-start.23 = (f32[1,7,7,512]{3,0,2,1:T(1,128)S(1)}, f32[1,7,7,512]{3,0,2,1:T(1,128)}, u32[]{:S(2)}) copy-start(f32[1,7,7,512]{3,0,2,1:T(1,128)} %param.17) | copy-start | bytes 301060
  35.6 38.2 %copy-start.26 = (f32[1,512]{1,0:T(1,128)S(1)}, f32[1,512]{1,0:T(1,128)}, u32[]{:S(2)}) copy-start(f32[1,512]{1,0:T(1,128)} %param.21) | copy-start | bytes 6148
  35.6 38.2 %copy-start.27 = (f32[1,512]{1,0:T(1,128)S(1)}, f32[1,512]{1,0:T(1,128)}, u32[]{:S(2)}) copy-start(f32[1,512]{1,0:T(1,128)} %param.18) | copy-start | bytes 6148
  35.6 39.0 %copy-start.5 = (bf16[2,16,16,512]{3,2,1,0:T(8,128)(2,1)S(1)}, bf16[2,16,16,512]{3,2,1,0:T(8,128)(2,1)}, u32[]{:S(2)}) copy-start(bf16[2,16,16,512]{3,2,1,0:T(8,128)(2,1)} %param.15) | copy-start | bytes 1572868
  71.8 6.2 %copy-start.1 = (bf16[8,8,2,16,512]{4,3,2,1,0:T(8,128)(2,1)}, bf16[8,8,2,16,512]{4,3,2,1,0:T(8,128)(2,1)S(1)}, u32[]{:S(2)}) copy-start(bf16[8,8,2,16,512]{4,3,2,1,0:T(8,128)(2,1)S(1)} %all_to_all.11) | copy-start | bytes 6291460
  71.8 6.2 %collective-permute-start.2 = (bf16[64,2,16,512]{3,2,1,0:T(8,128)(2,1)S(1)}, bf16[64,2,16,512]{3,2,1,0:T(8,128)(2,1)}, u32[]{:S(2)}, u32[]{:S(2)}) collective-permute-start(bf16[64,2,16,512]{3,2,1,0:T(8,128)(2,1)S(1)} %bitcast.41), channel_id=1, source_target_pairs={{0,1},{1,0},{2,3},{3,2},{4,5},{5,4},{6,7},{7,6},{8,9},{9,8},{10,11... | collective-permute-start | bytes 6291464 | tf_op jit(solution)/shard_map/ppermute | solution.py:342
  78.9 2.3 %collective-permute-start.7 = (bf16[256,512]{1,0:T(8,128)(2,1)}, bf16[256,512]{1,0:T(8,128)(2,1)S(1)}, u32[]{:S(2)}, u32[]{:S(2)}) collective-permute-start(bf16[256,512]{1,0:T(8,128)(2,1)} %detector_block.12), channel_id=1, source_target_pairs={{0,128},{1,129},{2,130},{3,131},{4,132},{5,133},{6,134},{7,135},{8... | collective-permute-start | bytes 786440 | tf_op jit(solution)/shard_map/ppermute | solution.py:377
  80.6 3.0 %collective-permute-start.3 = (bf16[256,512]{1,0:T(8,128)(2,1)}, bf16[256,512]{1,0:T(8,128)(2,1)S(1)}, u32[]{:S(2)}, u32[]{:S(2)}) collective-permute-start(bf16[256,512]{1,0:T(8,128)(2,1)} %detector_block.8), channel_id=1, source_target_pairs={{0,128},{1,129},{2,130},{3,131},{4,132},{5,133},{6,134},{7,135},{8... | collective-permute-start | bytes 786440 | tf_op jit(solution)/shard_map/ppermute | solution.py:377
  81.3 0.7 copy-start.19
  82.9 3.0 %collective-permute-start.8 = (bf16[256,512]{1,0:T(8,128)(2,1)}, bf16[256,512]{1,0:T(8,128)(2,1)S(1)}, u32[]{:S(2)}, u32[]{:S(2)}) collective-permute-start(bf16[256,512]{1,0:T(8,128)(2,1)} %detector_block.13), channel_id=1, source_target_pairs={{128,256},{129,257},{130,258},{131,259},{132,260},{133,261},{134,2... | collective-permute-start | bytes 786440 | tf_op jit(solution)/shard_map/ppermute | solution.py:377
  83.6 0.7 copy-start.15
  85.3 3.7 %collective-permute-start.4 = (bf16[256,512]{1,0:T(8,128)(2,1)}, bf16[256,512]{1,0:T(8,128)(2,1)S(1)}, u32[]{:S(2)}, u32[]{:S(2)}) collective-permute-start(bf16[256,512]{1,0:T(8,128)(2,1)} %detector_block.9), channel_id=1, source_target_pairs={{128,256},{129,257},{130,258},{131,259},{132,260},{133,261},{134,2... | collective-permute-start | bytes 786440 | tf_op jit(solution)/shard_map/ppermute | solution.py:377
  86.0 0.7 copy-start.16
  87.7 43.3 %collective-permute-start.9 = (bf16[256,512]{1,0:T(8,128)(2,1)}, bf16[256,512]{1,0:T(8,128)(2,1)S(1)}, u32[]{:S(2)}, u32[]{:S(2)}) collective-permute-start(bf16[256,512]{1,0:T(8,128)(2,1)} %detector_block.14), channel_id=1, source_target_pairs={{256,384},{257,385},{258,386},{259,387},{260,388},{261,389},{262,3... | collective-permute-start | bytes 786440 | tf_op jit(solution)/shard_map/ppermute | solution.py:377
  89.0 0.7 copy-start.17
  90.6 53.4 %collective-permute-start.5 = (bf16[256,512]{1,0:T(8,128)(2,1)}, bf16[256,512]{1,0:T(8,128)(2,1)S(1)}, u32[]{:S(2)}, u32[]{:S(2)}) collective-permute-start(bf16[256,512]{1,0:T(8,128)(2,1)} %detector_block.10), channel_id=1, source_target_pairs={{256,384},{257,385},{258,386},{259,387},{260,388},{261,389},{262,3... | collective-permute-start | bytes 786440 | tf_op jit(solution)/shard_map/ppermute | solution.py:377
  130.9 0.7 copy-start.18
  131.6 8.8 %copy-start.3 = (bf16[2,16,16,768]{3,2,1,0:T(8,128)(2,1)S(1)}, bf16[2,16,16,768]{3,2,1,0:T(8,128)(2,1)}, u32[]{:S(2)}) copy-start(bf16[2,16,16,768]{3,2,1,0:T(8,128)(2,1)} %param.16) | copy-start | bytes 2359300
  138.7 15.6 %collective-permute-start.10 = (bf16[256,512]{1,0:T(8,128)(2,1)}, bf16[256,512]{1,0:T(8,128)(2,1)S(1)}, u32[]{:S(2)}, u32[]{:S(2)}) collective-permute-start(bf16[256,512]{1,0:T(8,128)(2,1)} %detector_block.15.refs_7_), channel_id=1, source_target_pairs={{384,0},{385,1},{386,2},{387,3},{388,4},{389,5},{390,6},{391,7},{3... | collective-permute-start | bytes 786440 | tf_op jit(solution)/shard_map/ppermute | solution.py:380
  141.4 20.2 %collective-permute-start.12 = (bf16[256,512]{1,0:T(8,128)(2,1)}, bf16[256,512]{1,0:T(8,128)(2,1)S(1)}, u32[]{:S(2)}, u32[]{:S(2)}) collective-permute-start(bf16[256,512]{1,0:T(8,128)(2,1)} %detector_block.15.refs_7_), channel_id=1, source_target_pairs={{384,128},{385,129},{386,130},{387,131},{388,132},{389,133},{390,1... | collective-permute-start | bytes 786440 | tf_op jit(solution)/shard_map/ppermute | solution.py:380
  142.7 20.9 %collective-permute-start.14 = (bf16[256,512]{1,0:T(8,128)(2,1)}, bf16[256,512]{1,0:T(8,128)(2,1)S(1)}, u32[]{:S(2)}, u32[]{:S(2)}) collective-permute-start(bf16[256,512]{1,0:T(8,128)(2,1)} %detector_block.15.refs_7_), channel_id=1, source_target_pairs={{384,256},{385,257},{386,258},{387,259},{388,260},{389,261},{390,2... | collective-permute-start | bytes 786440 | tf_op jit(solution)/shard_map/ppermute | solution.py:380
  144.0 0.7 copy-start.14
  151.7 17.6 %collective-permute-start.11 = (bf16[256,512]{1,0:T(8,128)(2,1)}, bf16[256,512]{1,0:T(8,128)(2,1)S(1)}, u32[]{:S(2)}, u32[]{:S(2)}) collective-permute-start(bf16[256,512]{1,0:T(8,128)(2,1)} %detector_block.11.refs_6_), channel_id=1, source_target_pairs={{384,128},{385,129},{386,130},{387,131},{388,132},{389,133},{390,1... | collective-permute-start | bytes 786440 | tf_op jit(solution)/shard_map/ppermute | solution.py:380
  153.0 16.3 %collective-permute-start.13 = (bf16[256,512]{1,0:T(8,128)(2,1)}, bf16[256,512]{1,0:T(8,128)(2,1)S(1)}, u32[]{:S(2)}, u32[]{:S(2)}) collective-permute-start(bf16[256,512]{1,0:T(8,128)(2,1)} %detector_block.11.refs_6_), channel_id=1, source_target_pairs={{384,256},{385,257},{386,258},{387,259},{388,260},{389,261},{390,2... | collective-permute-start | bytes 786440 | tf_op jit(solution)/shard_map/ppermute | solution.py:380
  154.4 7.2 %copy-start.8 = (bf16[256,512]{1,0:T(8,128)(2,1)}, bf16[256,512]{1,0:T(8,128)(2,1)S(1)}, u32[]{:S(2)}) copy-start(bf16[256,512]{1,0:T(8,128)(2,1)S(1)} %collective-permute-done.10.refs_1_) | copy-start | bytes 786436
  154.4 15.0 %collective-permute-start.6 = (bf16[256,512]{1,0:T(8,128)(2,1)}, bf16[256,512]{1,0:T(8,128)(2,1)S(1)}, u32[]{:S(2)}, u32[]{:S(2)}) collective-permute-start(bf16[256,512]{1,0:T(8,128)(2,1)} %detector_block.11.refs_6_), channel_id=1, source_target_pairs={{384,0},{385,1},{386,2},{387,3},{388,4},{389,5},{390,6},{391,7},{3... | collective-permute-start | bytes 786440 | tf_op jit(solution)/shard_map/ppermute | solution.py:380
  161.6 7.8 %copy-start.9 = (bf16[256,512]{1,0:T(8,128)(2,1)}, bf16[256,512]{1,0:T(8,128)(2,1)S(1)}, u32[]{:S(2)}) copy-start(bf16[256,512]{1,0:T(8,128)(2,1)S(1)} %collective-permute-done.12.refs_3_) | copy-start | bytes 786436
  161.6 22.1 %collective-permute-start = (bf16[208,768]{1,0:T(8,128)(2,1)S(1)}, bf16[208,768]{1,0:T(8,128)(2,1)S(1)}, u32[]{:S(2)}, u32[]{:S(2)}) collective-permute-start(bf16[208,768]{1,0:T(8,128)(2,1)S(1)} %get-tuple-element.6), channel_id=1, source_target_pairs={{0,1},{1,2},{2,3},{3,4},{4,5},{5,6},{6,7},{7,8},{8,9},{9,10},{10,1... | collective-permute-start | bytes 958472 | tf_op jit(solution)/shard_map/ppermute | solution.py:310
  163.6 5.8 %copy-start.10 = (bf16[256,512]{1,0:T(8,128)(2,1)}, bf16[256,512]{1,0:T(8,128)(2,1)S(1)}, u32[]{:S(2)}) copy-start(bf16[256,512]{1,0:T(8,128)(2,1)S(1)} %collective-permute-done.14.refs_5_) | copy-start | bytes 786436
  163.6 20.2 %collective-permute-start.1 = (bf16[208,768]{1,0:T(8,128)(2,1)S(1)}, bf16[208,768]{1,0:T(8,128)(2,1)S(1)}, u32[]{:S(2)}, u32[]{:S(2)}) collective-permute-start(bf16[208,768]{1,0:T(8,128)(2,1)S(1)} %get-tuple-element.5), channel_id=1, source_target_pairs={{1,0},{2,1},{3,2},{4,3},{5,4},{6,5},{7,6},{8,7},{9,8},{10,9},{11,1... | collective-permute-start | bytes 958472 | tf_op jit(solution)/shard_map/ppermute | solution.py:311
  169.3 0.7 copy-start.11
  169.4 0.8 copy-start.12
  169.4 0.9 copy-start.13
  170.2 12.9 %copy-start.28 = (s32[1,4]{1,0:T(1,128)S(1)}, s32[1,4]{1,0:T(1,128)}, u32[]{:S(2)}) copy-start(s32[1,4]{1,0:T(1,128)} %param.29) | copy-start | bytes 52
  175.2 9.3 %collective-permute-start.15 = (bf16[208,512]{1,0:T(8,128)(2,1)S(1)}, bf16[208,512]{1,0:T(8,128)(2,1)S(1)}, u32[]{:S(2)}, u32[]{:S(2)}) collective-permute-start(bf16[208,512]{1,0:T(8,128)(2,1)S(1)} %get-tuple-element.11), channel_id=1, source_target_pairs={{0,1},{1,2},{2,3},{3,4},{4,5},{5,6},{6,7},{7,8},{8,9},{9,10},{10,1... | collective-permute-start | bytes 638984 | tf_op jit(solution)/shard_map/ppermute | solution.py:310
  177.1 9.1 %collective-permute-start.16 = (bf16[208,512]{1,0:T(8,128)(2,1)S(1)}, bf16[208,512]{1,0:T(8,128)(2,1)S(1)}, u32[]{:S(2)}, u32[]{:S(2)}) collective-permute-start(bf16[208,512]{1,0:T(8,128)(2,1)S(1)} %get-tuple-element.10), channel_id=1, source_target_pairs={{1,0},{2,1},{3,2},{4,3},{5,4},{6,5},{7,6},{8,7},{9,8},{10,9},{11,1... | collective-permute-start | bytes 638984 | tf_op jit(solution)/shard_map/ppermute | solution.py:311
  183.7 2.5 %copy-start.6 = (bf16[208,768]{1,0:T(8,128)(2,1)}, bf16[208,768]{1,0:T(8,128)(2,1)S(1)}, u32[]{:S(2)}) copy-start(bf16[208,768]{1,0:T(8,128)(2,1)S(1)} %collective-permute-done.pix_left) | copy-start | bytes 958468
  183.7 2.5 %copy-start.7 = (bf16[208,768]{1,0:T(8,128)(2,1)}, bf16[208,768]{1,0:T(8,128)(2,1)S(1)}, u32[]{:S(2)}) copy-start(bf16[208,768]{1,0:T(8,128)(2,1)S(1)} %collective-permute-done.1.pix_right) | copy-start | bytes 958468
  184.5 1.8 copy-start.21
  186.2 0.7 copy-start.22
Sparse Core Ops, SparseCore 0:
  14.8 82.3 all-gather.2

commit v2 on v1

v2 whole, which is shorter than its diff:
```python
import functools
import math

import jax
import jax.numpy as jnp
from jax import lax
from jax.experimental import pallas as pl
from jax.experimental.pallas import tpu as pltpu
from jax.sharding import PartitionSpec as P

HEAD_DIM = 64
TILE = 16
CELLS = TILE * TILE
CROP = 14
ROWS = CROP * CROP
PADDED = 208
LANES = 128
SIDE = 8
REP = ("y", "z", "core")
EPSILON = 1e-06
SLOT_AT = 36
SECTION_AT = 40

ANY = pl.BlockSpec(memory_space=pl.ANY)
SMEM = pl.BlockSpec(memory_space=pltpu.SMEM)
VMEM = pl.BlockSpec(memory_space=pltpu.VMEM)
LIMITED = pltpu.CompilerParams(vmem_limit_bytes=16 << 20)


def rep_index(y, z, core):
    return (y * SIDE + z) * 2 + core


def line_groups(first):
    along_z = [[rep_index(y, z, 0 if first else 1) for z in range(SIDE)] for y in range(SIDE)]
    along_y = [[rep_index(y, z, 1 if first else 0) for y in range(SIDE)] for z in range(SIDE)]
    return along_z + along_y


def spread_in_groups(block, groups):
    copies = jnp.broadcast_to(block[None], (SIDE,) + block.shape)
    return lax.all_to_all(copies, REP, 0, 0, axis_index_groups=groups)


def resident(array):
    return pltpu.with_memory_space_constraint(array, pltpu.VMEM)


def in_hbm(array):
    return pltpu.with_memory_space_constraint(array, pltpu.HBM)


def active(ints_ref, number):
    return ints_ref[SECTION_AT] == number


def block_body(ints_ref, tile_ref, param_ref, own_ref, other_ref, out_ref, wide, conv, *, number):
    @pl.when(active(ints_ref, number))
    def _():
        slabs = wide.shape[0]
        wide[:, :, 0:8, :] = jnp.zeros((slabs, TILE, 8, LANES), jnp.float32)
        wide[:, :, 24:32, :] = jnp.zeros((slabs, TILE, 8, LANES), jnp.float32)
        for slab in range(slabs):
            part = tile_ref[:, slab * LANES : (slab + 1) * LANES].astype(jnp.float32)
            wide[slab, :, 8:24, :] = part.reshape(TILE, TILE, LANES)

        def one_slab(slab, carry):
            sums = [None] * TILE
            for col in range(7):
                taps = [param_ref[slab, pl.ds(row * 7 + col, 1), :] for row in range(7)]
                for source in range(TILE):
                    cells = wide[slab, source, pl.ds(5 + col, TILE), :]
                    for row in range(7):
                        target = source + 3 - row
                        if 0 <= target < TILE:
                            term = cells * taps[row]
                            sums[target] = term if sums[target] is None else sums[target] + term
            for target in range(TILE):
                conv[slab, pl.ds(target * TILE, TILE), :] = sums[target]
            return carry

        lax.fori_loop(0, slabs, one_slab, 0)
        width = slabs * LANES
        total = conv[0]
        for slab in range(1, slabs):
            total = total + conv[slab]
        mean = jnp.sum(total, axis=-1, keepdims=True) / width
        squares = None
        for slab in range(slabs):
            centred = conv[slab] - mean
            squares = centred * centred if squares is None else squares + centred * centred
        scale = lax.rsqrt(jnp.sum(squares, axis=-1, keepdims=True) / width + EPSILON)
        normed = jnp.concatenate(
            [
                ((conv[slab] - mean) * scale * param_ref[slab, pl.ds(49, 1), :]).astype(jnp.bfloat16)
                for slab in range(slabs)
            ],
            axis=1,
        )
        update = None
        step = 32
        for ref in (own_ref, other_ref):
            for chunk in range(0, ref.shape[0], step):
                into = ref[pl.ds(chunk, step), 0].reshape(step * 16, width)
                outof = ref[pl.ds(chunk, step), 1].reshape(step * 16, width)
                hidden = lax.dot_general(
                    normed, into, (((1,), (1,)), ((), ())), preferred_element_type=jnp.float32
                )
                hidden = jax.nn.gelu(hidden, approximate=True).astype(jnp.bfloat16)
                term = jnp.dot(hidden, outof, preferred_element_type=jnp.float32)
                update = term if update is None else update + term
        for slab in range(slabs):
            part = slice(slab * LANES, (slab + 1) * LANES)
            out_ref[:, part] = (
                tile_ref[:, part].astype(jnp.float32) + param_ref[slab, pl.ds(50, 1), :] * update[:, part]
            ).astype(jnp.bfloat16)


def detector_block(number, ints, tile, params, own, other):
    cells, width = tile.shape
    slabs = width // LANES
    return pl.pallas_call(
        functools.partial(block_body, number=number),
        out_shape=pltpu.VMEM(tile.shape, jnp.bfloat16),
        in_specs=[SMEM, VMEM, VMEM, VMEM, VMEM],
        out_specs=VMEM,
        scratch_shapes=[
            pltpu.VMEM((slabs, TILE, 32, LANES), jnp.float32),
            pltpu.VMEM((slabs, cells, LANES), jnp.float32),
        ],
        compiler_params=LIMITED,
        name="detector_block",
    )(ints, *map(resident, (tile, params, own, other)))


def selection(top, left):
    row = lax.broadcasted_iota(jnp.int32, (PADDED, CELLS), 0)
    cell = lax.broadcasted_iota(jnp.int32, (PADDED, CELLS), 1)
    crop_row = (row * 4682) >> 16
    wanted = (top + crop_row) * TILE + left + (row - crop_row * CROP)
    return jnp.where((cell == wanted) & (row < ROWS), 1.0, 0.0).astype(jnp.bfloat16)


def cut_body(ints_ref, tile_ref, *refs):
    out_refs, buffer, sems = refs[:3], refs[3], refs[4]
    base = ints_ref[SECTION_AT] * 9
    copies = []
    for turn in range(3):
        copies.append(
            pltpu.make_async_copy(tile_ref.at[ints_ref[base + 3 * turn]], buffer.at[turn], sems.at[turn])
        )
        copies[-1].start()
    for turn in range(3):
        chosen = selection(ints_ref[base + 3 * turn + 1], ints_ref[base + 3 * turn + 2])
        copies[turn].wait()
        rows = jnp.dot(chosen, buffer[turn], preferred_element_type=jnp.float32)
        out_refs[turn][...] = rows.astype(jnp.bfloat16)


def cut_pixels(ints, tiles):
    micro, cells, width = tiles.shape
    return pl.pallas_call(
        cut_body,
        out_shape=[pltpu.VMEM((PADDED, width), jnp.bfloat16)] * 3,
        in_specs=[SMEM, ANY],
        out_specs=[VMEM] * 3,
        scratch_shapes=[pltpu.VMEM((3, cells, width), jnp.bfloat16), pltpu.SemaphoreType.DMA((3,))],
        compiler_params=LIMITED,
        name="cut_pixels",
    )(ints, tiles)


def pick_body(ints_ref, below_ref, above_ref, *refs):
    tiles, out_refs = refs[:6], refs[6:]

    @pl.when(active(ints_ref, len(out_refs) - 1))
    def _():
        for slot, out_ref in enumerate(out_refs):
            source = ints_ref[SLOT_AT + slot]
            for number, (plan_ref, turn) in enumerate(((below_ref, 2), (ints_ref, 1), (above_ref, 0))):
                base = slot * 9 + turn * 3
                wanted = (source == number + 1) if number != 1 else ((source == 2) | (source == 0))
                for micro in range(2):

                    @pl.when(wanted & (plan_ref[base] == micro))
                    def _(plan_ref=plan_ref, base=base, tile=tiles[2 * number + micro], out_ref=out_ref):
                        chosen = selection(plan_ref[base + 1], plan_ref[base + 2])
                        rows = jnp.dot(chosen, tile[...], preferred_element_type=jnp.float32)
                        out_ref[...] = rows.astype(jnp.bfloat16)


def pick_crops(ints, below, above, tiles, slots):
    width = tiles[0].shape[1]
    return pl.pallas_call(
        pick_body,
        out_shape=[pltpu.VMEM((PADDED, width), jnp.bfloat16)] * slots,
        in_specs=[SMEM] * 3 + [VMEM] * len(tiles),
        out_specs=[VMEM] * slots,
        compiler_params=LIMITED,
        name="pick_crops",
    )(ints, below, above, *map(resident, tiles))


EMBED, MERGE, QUERY = 0, 1536, 2560
KEY, VALUE, OUT, POS, HALF = 0, 1024, 2048, 3072, 3584


def pack_body(parity_ref, embed, merge, pos, qkv, out, packed, buffer, sems):
    first = [
        (embed.at[:, pl.ds(0, LANES)], EMBED),
        (embed.at[:, pl.ds(LANES, LANES)], EMBED + 768),
        (merge.at[:, pl.ds(0, LANES)], MERGE),
        (merge.at[:, pl.ds(LANES, LANES)], MERGE + 512),
        (qkv.at[0], QUERY),
    ]
    second = [(qkv.at[1], KEY), (qkv.at[2], VALUE)]
    second += [(out.at[:, pl.ds(column * LANES, LANES)], OUT + column * LANES) for column in range(8)]
    second += [
        (pos.at[:, pl.ds(0, LANES)], POS),
        (pos.at[:, pl.ds(LANES, LANES)], POS + PADDED),
    ]
    for parity, pieces in enumerate((first, second)):

        @pl.when(parity_ref[0] == parity)
        def _(pieces=pieces):
            copies = [
                pltpu.make_async_copy(piece, buffer.at[pl.ds(at, piece.shape[0])], sems.at[number])
                for number, (piece, at) in enumerate(pieces)
            ]
            for copy in copies:
                copy.start()
            for copy in copies:
                copy.wait()

    result = pltpu.make_async_copy(buffer, packed, sems.at[12])
    result.start()
    result.wait()


def packed_half(parity, embed, merge, pos, qkv, out):
    return pl.pallas_call(
        pack_body,
        out_shape=jax.ShapeDtypeStruct((HALF, LANES), jnp.bfloat16),
        in_specs=[SMEM] + [ANY] * 5,
        out_specs=ANY,
        scratch_shapes=[pltpu.VMEM((HALF, LANES), jnp.bfloat16), pltpu.SemaphoreType.DMA((13,))],
        compiler_params=LIMITED,
        name="pack_weights",
    )(parity, *map(in_hbm, (embed, merge, pos, qkv, out)))


def columns(ref, section, low, height):
    return jnp.concatenate(
        [ref[section, pl.ds(low, height), :], ref[section, pl.ds(low + height, height), :]], axis=1
    )


def stage_body(ints_ref, pix_below, pix_own, pix_above, packed, weights, base_ref, pix, sems):
    source = ints_ref[SLOT_AT + ints_ref[SECTION_AT]]
    sections = packed.shape[0] // 2
    spans = [(0, EMBED, MERGE), (1, POS, HALF), (0, MERGE, HALF), (1, KEY, POS)]
    copies = []
    for part, low, high in spans:
        for section in range(sections):
            place = (2 * section + part, pl.ds(low, high - low))
            copies.append(
                pltpu.make_async_copy(packed.at[place], weights.at[place], sems.at[1 + len(copies)])
            )
    for number, pix_ref in enumerate((pix_below, pix_own, pix_above)):

        @pl.when((source == number + 1) if number != 1 else ((source == 2) | (source == 0)))
        def _(pix_ref=pix_ref):
            copy = pltpu.make_async_copy(pix_ref, pix, sems.at[0])
            copy.start()
            copy.wait()

    for copy in copies:
        copy.start()
    for copy in copies[: 2 * sections]:
        copy.wait()
    rows = pix[...]
    row_ok = lax.broadcasted_iota(jnp.int32, (PADDED, 2 * LANES), 0) < ROWS
    for section in range(sections):
        pos = jnp.where(row_ok, columns(weights, 2 * section + 1, POS, PADDED).astype(jnp.float32), 0.0)
        base_ref[:, pl.ds(section * 2 * LANES, 2 * LANES)] = pos + jnp.dot(
            rows, columns(weights, 2 * section, EMBED, 768), preferred_element_type=jnp.float32
        )
    for copy in copies[2 * sections :]:
        copy.wait()


def staged(ints, pixels, packed):
    width = LANES * packed.shape[0]
    return pl.pallas_call(
        stage_body,
        out_shape=[pltpu.VMEM(packed.shape, jnp.bfloat16), pltpu.VMEM((PADDED, width), jnp.float32)],
        in_specs=[SMEM] + [ANY] * 4,
        out_specs=[VMEM] * 2,
        scratch_shapes=[
            pltpu.VMEM(pixels[0].shape, jnp.bfloat16),
            pltpu.SemaphoreType.DMA((1 + 2 * packed.shape[0],)),
        ],
        compiler_params=LIMITED,
        name="stage_weights",
    )(ints, *map(in_hbm, (*pixels, packed)))


def classify_body(ints_ref, *refs):
    feat_refs = refs[:4]
    base_ref, weights, gain_ref, out_ref, feat = refs[4:]
    place = ints_ref[SECTION_AT]
    source = ints_ref[SLOT_AT + place]
    sections = weights.shape[0] // 2
    for number, feat_ref in enumerate(feat_refs):

        @pl.when(place == number)
        def _(feat_ref=feat_ref):
            feat[...] = feat_ref[...]

    feat_rows = feat[...]
    tokens = base_ref[...] + jnp.concatenate(
        [
            jnp.dot(feat_rows, columns(weights, 2 * section, MERGE, 512), preferred_element_type=jnp.float32)
            for section in range(sections)
        ],
        axis=1,
    )
    width = tokens.shape[1]
    mean = jnp.sum(tokens, axis=-1, keepdims=True) / width
    centred = tokens - mean
    var = jnp.sum(centred * centred, axis=-1, keepdims=True) / width
    attn_in = (centred * lax.rsqrt(var + EPSILON) * gain_ref[pl.ds(0, 1), :]).astype(jnp.bfloat16)
    token_sum = jnp.sum(tokens, axis=0, keepdims=True)
    key_ok = lax.broadcasted_iota(jnp.int32, (PADDED, PADDED), 1) < ROWS
    lane = lax.broadcasted_iota(jnp.int32, (PADDED, 2 * HEAD_DIM), 1)
    row_ok = lax.broadcasted_iota(jnp.int32, (PADDED, 2 * HEAD_DIM), 0) < ROWS
    context_sums = []
    for section in range(sections):
        first, second = 2 * section, 2 * section + 1
        piece = jnp.concatenate(
            [
                weights[first, pl.ds(QUERY, 1024), :],
                weights[second, pl.ds(KEY, 1024), :],
                weights[second, pl.ds(VALUE, 1024), :],
            ],
            axis=1,
        )
        qkv = jnp.dot(attn_in, piece, preferred_element_type=jnp.float32).astype(jnp.bfloat16)
        query, key, value = qkv[:, :128], qkv[:, 128:256], qkv[:, 256:]
        contexts = []
        for head in range(2):
            mine = (lane >= HEAD_DIM) if head else (lane < HEAD_DIM)
            scores = lax.dot_general(
                jnp.where(mine, query, jnp.zeros_like(query)),
                key,
                (((1,), (1,)), ((), ())),
                preferred_element_type=jnp.float32,
            ) * (1.0 / math.sqrt(HEAD_DIM))
            scores = jnp.where(key_ok, scores, -jnp.inf)
            top = jnp.max(scores, axis=-1, keepdims=True)
            numer = jnp.exp(scores - top)
            probs = (numer * (1.0 / jnp.sum(numer, axis=-1, keepdims=True))).astype(jnp.bfloat16)
            contexts.append(jnp.dot(probs, value, preferred_element_type=jnp.float32))
        context = jnp.where(lane < HEAD_DIM, contexts[0], contexts[1]).astype(jnp.bfloat16)
        context = jnp.where(row_ok, context.astype(jnp.float32), 0.0)
        context_sums.append(jnp.sum(context, axis=0, keepdims=True))
    context_mean = jnp.concatenate(context_sums, axis=1) / ROWS
    high = context_mean.astype(jnp.bfloat16)
    rest = context_mean - high.astype(jnp.float32)
    middle = rest.astype(jnp.bfloat16)
    low = (rest - middle.astype(jnp.float32)).astype(jnp.bfloat16)
    pieces = jnp.concatenate([high, middle, low, jnp.zeros((13, high.shape[1]), jnp.bfloat16)], axis=0)
    out_weight = jnp.concatenate(
        [
            jnp.concatenate(
                [weights[2 * section + 1, pl.ds(OUT + LANES * column, LANES), :] for column in range(8)], axis=1
            )
            for section in range(sections)
        ],
        axis=0,
    )
    mixed = jnp.dot(pieces, out_weight, preferred_element_type=jnp.float32)
    pooled = token_sum / ROWS + jnp.sum(mixed, axis=0, keepdims=True)
    pooled_mean = jnp.sum(pooled, axis=-1, keepdims=True) / width
    centred = pooled - pooled_mean
    var = jnp.sum(centred * centred, axis=-1, keepdims=True) / width
    result = centred * lax.rsqrt(var + EPSILON) * gain_ref[pl.ds(1, 1), :]
    out_ref[...] = jnp.where(source == 0, 0.0, result)


def classify(ints, feats, base, weights, gain):
    return pl.pallas_call(
        classify_body,
        out_shape=jax.ShapeDtypeStruct((1, gain.shape[1]), jnp.float32),
        in_specs=[SMEM] + [VMEM] * 7,
        out_specs=VMEM,
        scratch_shapes=[pltpu.VMEM(feats[0].shape, jnp.bfloat16)],
        compiler_params=LIMITED,
        name="classify",
    )(ints, *map(resident, (*feats, base, weights, gain)))


def after(value, *others):
    return lax.optimization_barrier((value,) + others)[0]


def per_device(
    tile_features,
    patches,
    det_kernel,
    det_gain,
    det_in,
    det_out,
    det_scale,
    cls_embed,
    cls_merge,
    cls_pos,
    cls_qkv,
    cls_out,
    cls_gain,
    crop_plan,
    slot_from,
):
    sections = lax.axis_size("section")
    count = lax.axis_size(REP)
    section = lax.axis_index("section").astype(jnp.int32)
    parity = (lax.axis_index(REP) % 2).astype(jnp.int32).reshape(1)
    width = tile_features.shape[3]
    slabs = width // LANES
    last = sections - 1
    upward = [(index, index + 1) for index in range(count - 1)]
    downward = [(target, origin) for origin, target in upward]
    swap = [(index, index ^ 1) for index in range(count)]
    ints = jnp.concatenate([crop_plan.reshape(-1), slot_from.reshape(-1), section.reshape(1)])

    half = packed_half(parity, cls_embed, cls_merge, cls_pos, cls_qkv.transpose(1, 0, 2), cls_out)
    weights = lax.all_gather(half, ("section", "core"), axis=0)

    shard = jnp.stack([det_in[0].T, det_out[0]], axis=0)
    line = spread_in_groups(shard, line_groups(True))
    plane = spread_in_groups(after(line, half), line_groups(False))
    cut = cut_pixels(ints, patches.reshape(2, CELLS, patches.shape[3]))
    pixels = (lax.ppermute(cut[2], REP, upward), cut[1], lax.ppermute(cut[0], REP, downward))
    below = lax.ppermute(ints, REP, upward)
    above = lax.ppermute(ints, REP, downward)
    params = jnp.concatenate(
        [det_kernel[0].reshape(49, width), det_gain, det_scale, jnp.zeros((5, width), jnp.float32)], axis=0
    )
    params = params.reshape(56, slabs, LANES).transpose(1, 0, 2)
    plane = after(plane, below, above, params, *pixels)
    own = plane.reshape((SIDE * SIDE,) + shard.shape)
    other = lax.ppermute(own, REP, swap)

    start = tile_features.reshape(2, CELLS, width)
    tiles = [start[0], start[1]]
    for number in range(sections):
        done = [detector_block(number, ints, tile, params, own, other) for tile in tiles]
        if number < last:
            tiles = [lax.ppermute(tile, "section", [(number, number + 1)]) for tile in done]

    along = [(last * count + origin, last * count + target) for origin, target in upward]
    back = [(target, origin) for origin, target in along]
    from_below = [lax.ppermute(tile, ("section",) + REP, along) for tile in done]
    from_above = [lax.ppermute(tile, ("section",) + REP, back) for tile in done]
    crops = pick_crops(after(ints, weights), below, above, from_below + done + from_above, sections)
    feats = [lax.ppermute(crops[slot], "section", [(last, slot)]) for slot in range(last)] + [crops[last]]
    weights, base = staged(after(ints, *crops), pixels, weights)
    result = classify(ints, feats, base, weights, cls_gain)
    return result[None]


def solution(mesh):
    sections = mesh.shape["section"]
    fine = jax.sharding.Mesh(mesh.devices.reshape(sections, SIDE, SIDE, 2), ("section",) + REP)
    return jax.shard_map(
        per_device,
        mesh=fine,
        in_specs=(
            P(REP, None, None, None),
            P(REP, None, None, None),
            P("section", None, None, None),
            P("section", None),
            P("section", None, REP),
            P("section", REP, None),
            P("section", None),
            P(None, "section"),
            P(None, "section"),
            P(None, "section"),
            P(None, None, "section"),
            P("section", None),
            P(),
            P(REP, None, None, None),
            P(REP, None),
        ),
        out_specs=P(REP, "section", None),
        check_vma=False,
    )
```

time: 204 us -> 168 us (0.82)
  the two profiles are of different devices: /device:TPU:14 before, /device:TPU:36 now
where the time goes in v2:
time: 168 us
  waiting for transfers between devices  69.7 us (41%)
  starting transfers between devices  34.6 us (21%)
  Pallas kernels  26.7 us (16%)
  blocking collectives  20.6 us (12%)
  between operations  13.9 us (8%)
  local copies, waits for them, and re-layouts  2.06 us (1%)
    ppermute x3, waiting for transfers between devices, per_device(): lax.ppermute(crops[slot], 'section', [(last, slot)])  31.7 us
    ppermute x6, waiting for transfers between devices, per_device(): lax.ppermute(tile, 'section', [(number, number + 1)])  22.3 us
    all_to_all x1, blocking collectives, spread_in_groups(): return lax.all_to_all(copies, REP, 0, 0, axis_index_groups=groups)  20.6 us
    pallas_call x8, Pallas kernels, detector_block(): pl.pallas_call(functools.partial(block_body, number=number), out_shape=pl...  12.6 us
    ppermute x1, waiting for transfers between devices, per_device(): above = lax.ppermute(ints, REP, downward)  11.5 us
    all_to_all x1, starting transfers between devices, spread_in_groups(): return lax.all_to_all(copies, REP, 0, 0, axis_index_groups=groups)  7.35 us
    ppermute x1, starting transfers between devices, per_device(): lax.ppermute(cut[0], REP, downward)  6.96 us
    ppermute x6, starting transfers between devices, per_device(): lax.ppermute(tile, 'section', [(number, number + 1)])  6.55 us
  transfers between devices with their start and end apart: 20, of which 5 were waited for; matrix products, arithmetic and copies ran while one was open for 1% of the time, Pallas kernels for 12%

profile of v2, /device:TPU:36, one launch (start us, length us, event | category | flops | bytes accessed | tf_op | source)
XLA Modules:
  0.0 167.7 jit_solution(6978630170933430934)
XLA Ops:
  6.5 2.3 %pack_weights.1 = bf16[3584,128]{1,0:T(8,128)(2,1)} custom-call(s32[1]{0:T(128)} %bitcast.2.parity_ref, bf16[768,256]{1,0:T(8,128)(2,1)} %embed.1, bf16[512,256]{1,0:T(8,128)(2,1)} %merge.1, bf16[196,256]{1,0:T(8,128)(2,1)} %pos.1, bf16[3,1024,128]{2,1,0:T(8,128)(2,1)} %bitcast.33, bf16[128,1024]{1,0:T(8,128)(2,1)} %out.1), custom_call_target="tpu_custom_call" | custom-call | tf_op jit(solution)/shard_map/pack_weights/pallas_call | solution.py:241
  8.9 0.0 all-gather.3.cloned.1.call-update
  9.0 20.6 %all_to_all.10 = bf16[8,2,16,512]{3,2,1,0:T(8,128)(2,1)S(1)} all-to-all(bf16[8,2,16,512]{3,2,1,0:T(8,128)(2,1)S(1)} %broadcast_in_dim.9), channel_id=1, replica_groups={{0,2,4,6,8,10,12,14},{16,18,20,22,24,26,28,30},{32,34,36,38,40,42,44,46..., dimensions={0} | all-to-all | bytes 524288 | tf_op jit(solution)/shard_map/all_to_all | solution.py:42
  29.6 1.7 broadcast_in_dim.20
  31.2 0.0 copy-start.9
  31.2 0.0 copy-start.10
  31.3 0.0 copy-start.3
  31.3 7.3 %all-to-all-start.1 = ((bf16[8,8,2,16,512]{4,3,2,1,0:T(8,128)(2,1)}), bf16[8,8,2,16,512]{4,3,2,1,0:T(8,128)(2,1)S(1)}, u32[]{:S(2)}, u32[]{:S(2)}) async-start(bf16[8,8,2,16,512]{4,3,2,1,0:T(8,128)(2,1)} %broadcast_in_dim.20), calls=%async_computation.1 | async-start | bytes 4194304 | tf_op jit(solution)/shard_map/all_to_all | solution.py:42
  38.6 0.1 copy.17
  38.7 0.1 reshape.31
  38.8 0.1 pad_add_fusion.ints_ref
  38.9 2.0 %cut_pixels.1 = (bf16[208,768]{1,0:T(8,128)(2,1)S(1)}, bf16[208,768]{1,0:T(8,128)(2,1)S(1)}, bf16[208,768]{1,0:T(8,128)(2,1)S(1)}) custom-call(s32[41]{0:T(128)S(1)} %pad_add_fusion.ints_ref, bf16[2,256,768]{2,1,0:T(8,128)(2,1)S(1)} %bitcast.31), custom_call_target="tpu_custom_call" | custom-call | tf_op jit(solution)/shard_map/cut_pixels/pallas_call | solution.py:162
  40.9 1.9 %collective-permute-start.2 = (bf16[208,768]{1,0:T(8,128)(2,1)S(1)}, bf16[208,768]{1,0:T(8,128)(2,1)S(1)}, u32[]{:S(2)}, u32[]{:S(2)}) collective-permute-start(bf16[208,768]{1,0:T(8,128)(2,1)S(1)} %get-tuple-element.20), channel_id=1, source_target_pairs={{0,1},{1,2},{2,3},{3,4},{4,5},{5,6},{6,7},{7,8},{8,9},{9,10},{10,1... | collective-permute-start | bytes 958472 | tf_op jit(solution)/shard_map/ppermute | solution.py:443
  42.9 7.0 %collective-permute-start.3 = (bf16[208,768]{1,0:T(8,128)(2,1)S(1)}, bf16[208,768]{1,0:T(8,128)(2,1)}, u32[]{:S(2)}, u32[]{:S(2)}) collective-permute-start(bf16[208,768]{1,0:T(8,128)(2,1)S(1)} %get-tuple-element.22), channel_id=1, source_target_pairs={{1,0},{2,1},{3,2},{4,3},{5,4},{6,5},{7,6},{8,7},{9,8},{10,9},{11,1... | collective-permute-start | bytes 958472 | tf_op jit(solution)/shard_map/ppermute | solution.py:443
  49.8 1.9 %collective-permute-start.1 = (s32[41]{0:T(128)S(1)}, s32[41]{0:T(128)S(1)}, u32[]{:S(2)}, u32[]{:S(2)}) collective-permute-start(s32[41]{0:T(128)S(1)} %pad_add_fusion.ints_ref), channel_id=1, source_target_pairs={{1,0},{2,1},{3,2},{4,3},{5,4},{6,5},{7,6},{8,7},{9,8},{10,9},{11,1... | collective-permute-start | bytes 500 | tf_op jit(solution)/shard_map/ppermute | solution.py:445
  51.8 2.4 %collective-permute-start = (s32[41]{0:T(128)S(1)}, s32[41]{0:T(128)S(1)}, u32[]{:S(2)}, u32[]{:S(2)}) collective-permute-start(s32[41]{0:T(128)S(1)} %pad_add_fusion.ints_ref), channel_id=1, source_target_pairs={{0,1},{1,2},{2,3},{3,4},{4,5},{5,6},{6,7},{7,8},{8,9},{9,10},{10,1... | collective-permute-start | bytes 500 | tf_op jit(solution)/shard_map/ppermute | solution.py:444
  54.2 0.1 pad.5.clone
  54.3 0.1 maximum_bitcast_fusion.param_ref
  54.4 11.5 %collective-permute-done.1.above_ref = s32[41]{0:T(128)S(1)} collective-permute-done((s32[41]{0:T(128)S(1)}, s32[41]{0:T(128)S(1)}, u32[]{:S(2)}, u32[]{:S(2)}) %collective-permute-start.1) | collective-permute-done | bytes 196 | tf_op jit(solution)/shard_map/ppermute | solution.py:445
  65.9 0.0 collective-permute-done.below_ref
  65.9 0.0 collective-permute-done.2.pix_below
  65.9 0.0 collective-permute-done.3.pix_above
  65.9 0.0 all-to-all-done.1
  65.9 1.9 %collective-permute-start.4 = (bf16[64,2,16,512]{3,2,1,0:T(8,128)(2,1)S(1)}, bf16[64,2,16,512]{3,2,1,0:T(8,128)(2,1)S(1)}, u32[]{:S(2)}, u32[]{:S(2)}) collective-permute-start(bf16[64,2,16,512]{3,2,1,0:T(8,128)(2,1)S(1)} %bitcast.20), channel_id=1, source_target_pairs={{0,1},{1,0},{2,3},{3,2},{4,5},{5,4},{6,7},{7,6},{8,9},{9,8},{10,11... | collective-permute-start | bytes 6291464 | tf_op jit(solution)/shard_map/ppermute | solution.py:452
  67.9 4.1 %collective-permute-done.4.other_ref = bf16[64,2,16,512]{3,2,1,0:T(8,128)(2,1)S(1)} collective-permute-done((bf16[64,2,16,512]{3,2,1,0:T(8,128)(2,1)S(1)}, bf16[64,2,16,512]{3,2,1,0:T(8,128)(2,1)S(1)}, u32[]{:S(2)}, u32[]{:S(2)}) %collective-permute-start.4) | collective-permute-done | bytes 2097184 | tf_op jit(solution)/shard_map/ppermute | solution.py:452
  72.0 0.5 detector_block.8
  72.5 0.7 collective-permute-start.5
  73.2 0.6 detector_block.12
  73.8 0.7 collective-permute-start.9
  74.5 0.0 collective-permute-done.5.tile_ref
  74.5 0.6 detector_block.9
  75.0 1.3 collective-permute-start.6
  76.3 0.0 collective-permute-done.9.tile_ref
  76.4 0.6 detector_block.13
  76.9 1.3 collective-permute-start.10
  78.2 19.2 %collective-permute-done.6.tile_ref = bf16[256,512]{1,0:T(8,128)(2,1)S(1)} collective-permute-done((bf16[256,512]{1,0:T(8,128)(2,1)S(1)}, bf16[256,512]{1,0:T(8,128)(2,1)S(1)}, u32[]{:S(2)}, u32[]{:S(2)}) %collective-permute-start.6) | collective-permute-done | bytes 262176 | tf_op jit(solution)/shard_map/ppermute | solution.py:459
  97.5 4.7 %detector_block.10 = bf16[256,512]{1,0:T(8,128)(2,1)S(1)} custom-call(s32[41]{0:T(128)S(1)} %pad_add_fusion.ints_ref, bf16[256,512]{1,0:T(8,128)(2,1)S(1)} %collective-permute-done.6.tile_ref, f32[4,56,128]{2,1,0:T(8,128)S(1)} %maximum_bitcast_fusion.param_ref, bf16[64,2,16,512]{3,2,1,0:T(8,128)(2,1)S(1)} %bitcast.25, ...), custom_call_target="tpu_custom_call" | custom-call | tf_op jit(solution)/shard_map/detector_block/pallas_call | solution.py:122
  102.2 1.3 collective-permute-start.7
  103.5 0.0 collective-permute-done.10.tile_ref
  103.5 4.6 %detector_block.14 = bf16[256,512]{1,0:T(8,128)(2,1)S(1)} custom-call(s32[41]{0:T(128)S(1)} %pad_add_fusion.ints_ref, bf16[256,512]{1,0:T(8,128)(2,1)S(1)} %collective-permute-done.10.tile_ref, f32[4,56,128]{2,1,0:T(8,128)S(1)} %maximum_bitcast_fusion.param_ref, bf16[64,2,16,512]{3,2,1,0:T(8,128)(2,1)S(1)} %bitcast.26, ...), custom_call_target="tpu_custom_call" | custom-call | tf_op jit(solution)/shard_map/detector_block/pallas_call | solution.py:122
  108.1 1.3 collective-permute-start.11
  109.4 0.0 collective-permute-done.7.tile_ref
  109.4 0.6 detector_block.11.refs_2_
  110.0 0.7 collective-permute-start.13
  110.7 0.7 collective-permute-start.8
  111.4 3.1 %collective-permute-done.11.tile_ref = bf16[256,512]{1,0:T(8,128)(2,1)S(1)} collective-permute-done((bf16[256,512]{1,0:T(8,128)(2,1)S(1)}, bf16[256,512]{1,0:T(8,128)(2,1)S(1)}, u32[]{:S(2)}, u32[]{:S(2)}) %collective-permute-start.11) | collective-permute-done | bytes 262176 | tf_op jit(solution)/shard_map/ppermute | solution.py:459
  114.4 0.5 detector_block.15.refs_3_
  115.0 0.7 collective-permute-start.14
  115.7 0.7 collective-permute-start.12
  116.4 0.0 all-gather.3.cloned.1.call-done
  116.4 0.0 collective-permute-done.13.refs_4_
  116.4 0.0 collective-permute-done.8.refs_0_
  116.4 0.0 collective-permute-done.14.refs_5_
  116.4 0.0 collective-permute-done.12.refs_1_
  116.4 0.6 pick_crops.1
  117.0 0.7 collective-permute-start.15
  117.7 0.7 collective-permute-start.16
  118.4 1.5 collective-permute-start.17
  119.9 0.0 copy-start.2
  119.9 4.8 %stage_weights.1 = (bf16[8,3584,128]{2,1,0:T(8,128)(2,1)S(1)}, f32[208,1024]{1,0:T(8,128)S(1)}) custom-call(s32[41]{0:T(128)S(1)} %pad_add_fusion.ints_ref, bf16[208,768]{1,0:T(8,128)(2,1)} %copy-done.4, bf16[208,768]{1,0:T(8,128)(2,1)} %copy-done.1, bf16[208,768]{1,0:T(8,128)(2,1)} %collective-permute-done.3.pix_above, bf16[8,3584,128]{2,1,0:T(8,128)(2,1)} %bitcast.32), custom_call_target="tpu_custom_call" | custom-call | tf_op jit(solution)/shard_map/stage_weights/pallas_call | solution.py:294
  124.7 0.0 collective-permute-done.15.refs_0_
  124.7 0.0 collective-permute-done.16.refs_1_
  124.7 31.7 %collective-permute-done.17.refs_2_ = bf16[208,512]{1,0:T(8,128)(2,1)S(1)} collective-permute-done((bf16[208,512]{1,0:T(8,128)(2,1)S(1)}, bf16[208,512]{1,0:T(8,128)(2,1)S(1)}, u32[]{:S(2)}, u32[]{:S(2)}) %collective-permute-start.17) | collective-permute-done | bytes 213024 | tf_op jit(solution)/shard_map/ppermute | solution.py:466
  156.4 4.4 %classify.1 = f32[1,1024]{1,0:T(1,128)} custom-call(s32[41]{0:T(128)S(1)} %pad_add_fusion.ints_ref, bf16[208,512]{1,0:T(8,128)(2,1)S(1)} %collective-permute-done.15.refs_0_, bf16[208,512]{1,0:T(8,128)(2,1)S(1)} %collective-permute-done.16.refs_1_, bf16[208,512]{1,0:T(8,128)(2,1)S(1)} %collective-permute-done.17.refs_2_, ...), custom_call_target="tpu_custom_call" | custom-call | tf_op jit(solution)/shard_map/classify/pallas_call | solution.py:392
  (26 shorter events, 0.1 us)
Async XLA Ops:
  6.5 2.4 %copy-start.6 = (bf16[1,16,512]{2,1,0:T(8,128)(2,1)S(1)}, bf16[1,16,512]{2,1,0:T(8,128)(2,1)}, u32[]{:S(2)}) copy-start(bf16[1,16,512]{2,1,0:T(8,128)(2,1)} %param.20) | copy-start | bytes 49156
  6.5 2.4 %copy-start.7 = (bf16[1,512,16]{1,2,0:T(8,128)(2,1)S(1)}, bf16[1,512,16]{1,2,0:T(8,128)(2,1)}, u32[]{:S(2)}) copy-start(bf16[1,512,16]{1,2,0:T(8,128)(2,1)} %param.19) | copy-start | bytes 49156
  6.5 109.8 %all-gather.3.cloned.1.call-start = ((), (), s32[]{:S(2)}) async-start(), calls=%async_computation.2 | async-start | bytes 8257536 | tf_op jit(solution)/shard_map/all_gather | solution.py:437
  31.2 7.4 %copy-start.8 = (s32[1,4,3,3]{1,0,3,2:T(1,128)S(1)}, s32[1,4,3,3]{1,0,3,2:T(1,128)}, u32[]{:S(2)}) copy-start(s32[1,4,3,3]{1,0,3,2:T(1,128)} %param.28) | copy-start | bytes 436
  31.2 7.6 %copy-start.11 = (s32[1,4]{1,0:T(1,128)S(1)}, s32[1,4]{1,0:T(1,128)}, u32[]{:S(2)}) copy-start(s32[1,4]{1,0:T(1,128)} %param.29) | copy-start | bytes 52
  31.2 7.7 %copy-start = (bf16[2,16,16,768]{3,2,1,0:T(8,128)(2,1)S(1)}, bf16[2,16,16,768]{3,2,1,0:T(8,128)(2,1)}, u32[]{:S(2)}) copy-start(bf16[2,16,16,768]{3,2,1,0:T(8,128)(2,1)} %param.16) | copy-start | bytes 2359300
  31.2 23.0 %copy-start.5 = (f32[1,7,7,512]{3,0,2,1:T(1,128)S(1)}, f32[1,7,7,512]{3,0,2,1:T(1,128)}, u32[]{:S(2)}) copy-start(f32[1,7,7,512]{3,0,2,1:T(1,128)} %param.17) | copy-start | bytes 301060
  31.2 23.1 %copy-start.9 = (f32[1,512]{1,0:T(1,128)S(1)}, f32[1,512]{1,0:T(1,128)}, u32[]{:S(2)}) copy-start(f32[1,512]{1,0:T(1,128)} %param.21) | copy-start | bytes 6148
  31.2 23.1 %copy-start.10 = (f32[1,512]{1,0:T(1,128)S(1)}, f32[1,512]{1,0:T(1,128)}, u32[]{:S(2)}) copy-start(f32[1,512]{1,0:T(1,128)} %param.18) | copy-start | bytes 6148
  31.3 36.6 %copy-start.3 = (bf16[2,16,16,512]{3,2,1,0:T(8,128)(2,1)S(1)}, bf16[2,16,16,512]{3,2,1,0:T(8,128)(2,1)}, u32[]{:S(2)}) copy-start(bf16[2,16,16,512]{3,2,1,0:T(8,128)(2,1)} %param.15) | copy-start | bytes 1572868
  31.3 34.7 %all-to-all-start.1 = ((bf16[8,8,2,16,512]{4,3,2,1,0:T(8,128)(2,1)}), bf16[8,8,2,16,512]{4,3,2,1,0:T(8,128)(2,1)S(1)}, u32[]{:S(2)}, u32[]{:S(2)}) async-start(bf16[8,8,2,16,512]{4,3,2,1,0:T(8,128)(2,1)} %broadcast_in_dim.20), calls=%async_computation.1 | async-start | bytes 4194304 | tf_op jit(solution)/shard_map/all_to_all | solution.py:42
  40.9 25.0 %copy-start.1 = (bf16[208,768]{1,0:T(8,128)(2,1)}, bf16[208,768]{1,0:T(8,128)(2,1)S(1)}, u32[]{:S(2)}) copy-start(bf16[208,768]{1,0:T(8,128)(2,1)S(1)} %get-tuple-element.21.pix_own) | copy-start | bytes 958468
  40.9 25.0 %collective-permute-start.2 = (bf16[208,768]{1,0:T(8,128)(2,1)S(1)}, bf16[208,768]{1,0:T(8,128)(2,1)S(1)}, u32[]{:S(2)}, u32[]{:S(2)}) collective-permute-start(bf16[208,768]{1,0:T(8,128)(2,1)S(1)} %get-tuple-element.20), channel_id=1, source_target_pairs={{0,1},{1,2},{2,3},{3,4},{4,5},{5,6},{6,7},{7,8},{8,9},{9,10},{10,1... | collective-permute-start | bytes 958472 | tf_op jit(solution)/shard_map/ppermute | solution.py:443
  42.9 23.0 %collective-permute-start.3 = (bf16[208,768]{1,0:T(8,128)(2,1)S(1)}, bf16[208,768]{1,0:T(8,128)(2,1)}, u32[]{:S(2)}, u32[]{:S(2)}) collective-permute-start(bf16[208,768]{1,0:T(8,128)(2,1)S(1)} %get-tuple-element.22), channel_id=1, source_target_pairs={{1,0},{2,1},{3,2},{4,3},{5,4},{6,5},{7,6},{8,7},{9,8},{10,9},{11,1... | collective-permute-start | bytes 958472 | tf_op jit(solution)/shard_map/ppermute | solution.py:443
  49.8 16.1 %collective-permute-start.1 = (s32[41]{0:T(128)S(1)}, s32[41]{0:T(128)S(1)}, u32[]{:S(2)}, u32[]{:S(2)}) collective-permute-start(s32[41]{0:T(128)S(1)} %pad_add_fusion.ints_ref), channel_id=1, source_target_pairs={{1,0},{2,1},{3,2},{4,3},{5,4},{6,5},{7,6},{8,7},{9,8},{10,9},{11,1... | collective-permute-start | bytes 500 | tf_op jit(solution)/shard_map/ppermute | solution.py:445
  51.8 14.1 %collective-permute-start = (s32[41]{0:T(128)S(1)}, s32[41]{0:T(128)S(1)}, u32[]{:S(2)}, u32[]{:S(2)}) collective-permute-start(s32[41]{0:T(128)S(1)} %pad_add_fusion.ints_ref), channel_id=1, source_target_pairs={{0,1},{1,2},{2,3},{3,4},{4,5},{5,6},{6,7},{7,8},{8,9},{9,10},{10,1... | collective-permute-start | bytes 500 | tf_op jit(solution)/shard_map/ppermute | solution.py:444
  65.9 6.6 %copy-start.4 = (bf16[208,768]{1,0:T(8,128)(2,1)}, bf16[208,768]{1,0:T(8,128)(2,1)S(1)}, u32[]{:S(2)}) copy-start(bf16[208,768]{1,0:T(8,128)(2,1)S(1)} %collective-permute-done.2.pix_below) | copy-start | bytes 958468
  65.9 6.1 %collective-permute-start.4 = (bf16[64,2,16,512]{3,2,1,0:T(8,128)(2,1)S(1)}, bf16[64,2,16,512]{3,2,1,0:T(8,128)(2,1)S(1)}, u32[]{:S(2)}, u32[]{:S(2)}) collective-permute-start(bf16[64,2,16,512]{3,2,1,0:T(8,128)(2,1)S(1)} %bitcast.20), channel_id=1, source_target_pairs={{0,1},{1,0},{2,3},{3,2},{4,5},{5,4},{6,7},{7,6},{8,9},{9,8},{10,11... | collective-permute-start | bytes 6291464 | tf_op jit(solution)/shard_map/ppermute | solution.py:452
  72.5 1.9 %collective-permute-start.5 = (bf16[256,512]{1,0:T(8,128)(2,1)S(1)}, bf16[256,512]{1,0:T(8,128)(2,1)S(1)}, u32[]{:S(2)}, u32[]{:S(2)}) collective-permute-start(bf16[256,512]{1,0:T(8,128)(2,1)S(1)} %detector_block.8), channel_id=1, source_target_pairs={{0,128},{1,129},{2,130},{3,131},{4,132},{5,133},{6,134},{7,135},{8... | collective-permute-start | bytes 786440 | tf_op jit(solution)/shard_map/ppermute | solution.py:459
  73.8 2.6 %collective-permute-start.9 = (bf16[256,512]{1,0:T(8,128)(2,1)S(1)}, bf16[256,512]{1,0:T(8,128)(2,1)S(1)}, u32[]{:S(2)}, u32[]{:S(2)}) collective-permute-start(bf16[256,512]{1,0:T(8,128)(2,1)S(1)} %detector_block.12), channel_id=1, source_target_pairs={{0,128},{1,129},{2,130},{3,131},{4,132},{5,133},{6,134},{7,135},{8... | collective-permute-start | bytes 786440 | tf_op jit(solution)/shard_map/ppermute | solution.py:459
  75.0 22.4 %collective-permute-start.6 = (bf16[256,512]{1,0:T(8,128)(2,1)S(1)}, bf16[256,512]{1,0:T(8,128)(2,1)S(1)}, u32[]{:S(2)}, u32[]{:S(2)}) collective-permute-start(bf16[256,512]{1,0:T(8,128)(2,1)S(1)} %detector_block.9), channel_id=1, source_target_pairs={{128,256},{129,257},{130,258},{131,259},{132,260},{133,261},{134,2... | collective-permute-start | bytes 786440 | tf_op jit(solution)/shard_map/ppermute | solution.py:459
  76.9 26.6 %collective-permute-start.10 = (bf16[256,512]{1,0:T(8,128)(2,1)S(1)}, bf16[256,512]{1,0:T(8,128)(2,1)S(1)}, u32[]{:S(2)}, u32[]{:S(2)}) collective-permute-start(bf16[256,512]{1,0:T(8,128)(2,1)S(1)} %detector_block.13), channel_id=1, source_target_pairs={{128,256},{129,257},{130,258},{131,259},{132,260},{133,261},{134,2... | collective-permute-start | bytes 786440 | tf_op jit(solution)/shard_map/ppermute | solution.py:459
  102.2 7.2 %collective-permute-start.7 = (bf16[256,512]{1,0:T(8,128)(2,1)S(1)}, bf16[256,512]{1,0:T(8,128)(2,1)S(1)}, u32[]{:S(2)}, u32[]{:S(2)}) collective-permute-start(bf16[256,512]{1,0:T(8,128)(2,1)S(1)} %detector_block.10), channel_id=1, source_target_pairs={{256,384},{257,385},{258,386},{259,387},{260,388},{261,389},{262,3... | collective-permute-start | bytes 786440 | tf_op jit(solution)/shard_map/ppermute | solution.py:459
  108.1 6.3 %collective-permute-start.11 = (bf16[256,512]{1,0:T(8,128)(2,1)S(1)}, bf16[256,512]{1,0:T(8,128)(2,1)S(1)}, u32[]{:S(2)}, u32[]{:S(2)}) collective-permute-start(bf16[256,512]{1,0:T(8,128)(2,1)S(1)} %detector_block.14), channel_id=1, source_target_pairs={{256,384},{257,385},{258,386},{259,387},{260,388},{261,389},{262,3... | collective-permute-start | bytes 786440 | tf_op jit(solution)/shard_map/ppermute | solution.py:459
  110.0 6.4 %collective-permute-start.13 = (bf16[256,512]{1,0:T(8,128)(2,1)S(1)}, bf16[256,512]{1,0:T(8,128)(2,1)S(1)}, u32[]{:S(2)}, u32[]{:S(2)}) collective-permute-start(bf16[256,512]{1,0:T(8,128)(2,1)S(1)} %detector_block.11.refs_2_), channel_id=1, source_target_pairs={{385,384},{386,385},{387,386},{388,387},{389,388},{390,389},{391,3... | collective-permute-start | bytes 786440 | tf_op jit(solution)/shard_map/ppermute | solution.py:464
  110.7 5.7 %collective-permute-start.8 = (bf16[256,512]{1,0:T(8,128)(2,1)S(1)}, bf16[256,512]{1,0:T(8,128)(2,1)S(1)}, u32[]{:S(2)}, u32[]{:S(2)}) collective-permute-start(bf16[256,512]{1,0:T(8,128)(2,1)S(1)} %detector_block.11.refs_2_), channel_id=1, source_target_pairs={{384,385},{385,386},{386,387},{387,388},{388,389},{389,390},{390,3... | collective-permute-start | bytes 786440 | tf_op jit(solution)/shard_map/ppermute | solution.py:463
  115.0 1.4 collective-permute-start.14
  115.7 0.7 collective-permute-start.12
  117.0 7.7 %collective-permute-start.15 = (bf16[208,512]{1,0:T(8,128)(2,1)S(1)}, bf16[208,512]{1,0:T(8,128)(2,1)S(1)}, u32[]{:S(2)}, u32[]{:S(2)}) collective-permute-start(bf16[208,512]{1,0:T(8,128)(2,1)S(1)} %get-tuple-element.24), channel_id=1, source_target_pairs={{384,0},{385,1},{386,2},{387,3},{388,4},{389,5},{390,6},{391,7},{3... | collective-permute-start | bytes 638984 | tf_op jit(solution)/shard_map/ppermute | solution.py:466
  117.7 7.0 %collective-permute-start.16 = (bf16[208,512]{1,0:T(8,128)(2,1)S(1)}, bf16[208,512]{1,0:T(8,128)(2,1)S(1)}, u32[]{:S(2)}, u32[]{:S(2)}) collective-permute-start(bf16[208,512]{1,0:T(8,128)(2,1)S(1)} %get-tuple-element.25), channel_id=1, source_target_pairs={{384,128},{385,129},{386,130},{387,131},{388,132},{389,133},{390,1... | collective-permute-start | bytes 638984 | tf_op jit(solution)/shard_map/ppermute | solution.py:466
  118.4 38.0 %collective-permute-start.17 = (bf16[208,512]{1,0:T(8,128)(2,1)S(1)}, bf16[208,512]{1,0:T(8,128)(2,1)S(1)}, u32[]{:S(2)}, u32[]{:S(2)}) collective-permute-start(bf16[208,512]{1,0:T(8,128)(2,1)S(1)} %get-tuple-element.26), channel_id=1, source_target_pairs={{384,256},{385,257},{386,258},{387,259},{388,260},{389,261},{390,2... | collective-permute-start | bytes 638984 | tf_op jit(solution)/shard_map/ppermute | solution.py:466
  119.9 36.5 %copy-start.2 = (f32[2,1024]{1,0:T(2,128)S(1)}, f32[2,1024]{1,0:T(2,128)}, u32[]{:S(2)}) copy-start(f32[2,1024]{1,0:T(2,128)} %refs_6_.1) | copy-start | bytes 24580
Sparse Core Ops, SparseCore 0:
  9.5 53.7 all-gather.2

commit v3 on v2

--- a/solution.py
+++ b/solution.py
@@ -20,6 +20,7 @@
 EPSILON = 1e-06
 SLOT_AT = 36
 SECTION_AT = 40
+CORE_AT = 41
 
 ANY = pl.BlockSpec(memory_space=pl.ANY)
 SMEM = pl.BlockSpec(memory_space=pltpu.SMEM)
@@ -54,49 +55,93 @@
     return ints_ref[SECTION_AT] == number
 
 
-def block_body(ints_ref, tile_ref, param_ref, own_ref, other_ref, out_ref, wide, conv, *, number):
+def conv_norm(tile_ref, param_ref, normed_ref, wide, conv):
+    slabs = wide.shape[0]
+    wide[:, :, 0:8, :] = jnp.zeros((slabs, TILE, 8, LANES), jnp.float32)
+    wide[:, :, 24:32, :] = jnp.zeros((slabs, TILE, 8, LANES), jnp.float32)
+    for slab in range(slabs):
+        part = tile_ref[:, slab * LANES : (slab + 1) * LANES].astype(jnp.float32)
+        wide[slab, :, 8:24, :] = part.reshape(TILE, TILE, LANES)
+
+    def one_slab(slab, carry):
+        sums = [None] * TILE
+        for col in range(7):
+            taps = [param_ref[slab, pl.ds(row * 7 + col, 1), :] for row in range(7)]
+            for source in range(TILE):
+                cells = wide[slab, source, pl.ds(5 + col, TILE), :]
+                for row in range(7):
+                    target = source + 3 - row
+                    if 0 <= target < TILE:
+                        term = cells * taps[row]
+                        sums[target] = term if sums[target] is None else sums[target] + term
+        for target in range(TILE):
+            conv[slab, pl.ds(target * TILE, TILE), :] = sums[target]
+        return carry
+
+    lax.fori_loop(0, slabs, one_slab, 0)
+    width = slabs * LANES
+    total = conv[0]
+    for slab in range(1, slabs):
+        total = total + conv[slab]
+    mean = jnp.sum(total, axis=-1, keepdims=True) / width
+    squares = None
+    for slab in range(slabs):
+        centred = conv[slab] - mean
+        squares = centred * centred if squares is None else squares + centred * centred
+    scale = lax.rsqrt(jnp.sum(squares, axis=-1, keepdims=True) / width + EPSILON)
+    for slab in range(slabs):
+        normed_ref[:, slab * LANES : (slab + 1) * LANES] = (
+            (conv[slab] - mean) * scale * param_ref[slab, pl.ds(49, 1), :]
+        ).astype(jnp.bfloat16)
+
+
+def early_body(ints_ref, tile_ref, param_ref, normed_ref, wide, conv):
+    @pl.when(active(ints_ref, 0) & (ints_ref[CORE_AT] == 0))
+    def _():
+        conv_norm(tile_ref, param_ref, normed_ref, wide, conv)
+
+
+def conv_scratch(tile):
+    cells, width = tile.shape
+    slabs = width // LANES
+    return [
+        pltpu.VMEM((slabs, TILE, 32, LANES), jnp.float32),
+        pltpu.VMEM((slabs, cells, LANES), jnp.float32),
+    ]
+
+
+def early_norm(ints, tile, params):
+    return pl.pallas_call(
+        early_body,
+        out_shape=pltpu.VMEM(tile.shape, jnp.bfloat16),
+        in_specs=[SMEM, VMEM, VMEM],
+        out_specs=VMEM,
+        scratch_shapes=conv_scratch(tile),
+        compiler_params=LIMITED,
+        name="early_norm",
+    )(ints, resident(tile), resident(params))
+
+
+def block_body(ints_ref, tile_ref, param_ref, own_ref, other_ref, *refs, number):
+    early_refs, (out_ref, normed, wide, conv) = refs[:-4], refs[-4:]
+
     @pl.when(active(ints_ref, number))
     def _():
+        if early_refs:
+
+            @pl.when(ints_ref[CORE_AT] == 0)
+            def _():
+                normed[...] = early_refs[0][...]
+
+            @pl.when(ints_ref[CORE_AT] == 1)
+            def _():
+                conv_norm(tile_ref, param_ref, normed, wide, conv)
+
+        else:
+            conv_norm(tile_ref, param_ref, normed, wide, conv)
         slabs = wide.shape[0]
-        wide[:, :, 0:8, :] = jnp.zeros((slabs, TILE, 8, LANES), jnp.float32)
-        wide[:, :, 24:32, :] = jnp.zeros((slabs, TILE, 8, LANES), jnp.float32)
-        for slab in range(slabs):
-            part = tile_ref[:, slab * LANES : (slab + 1) * LANES].astype(jnp.float32)
-            wide[slab, :, 8:24, :] = part.reshape(TILE, TILE, LANES)
-
-        def one_slab(slab, carry):
-            sums = [None] * TILE
-            for col in range(7):
-                taps = [param_ref[slab, pl.ds(row * 7 + col, 1), :] for row in range(7)]
-                for source in range(TILE):
-                    cells = wide[slab, source, pl.ds(5 + col, TILE), :]
-                    for row in range(7):
-                        target = source + 3 - row
-                        if 0 <= target < TILE:
-                            term = cells * taps[row]
-                            sums[target] = term if sums[target] is None else sums[target] + term
-            for target in range(TILE):
-                conv[slab, pl.ds(target * TILE, TILE), :] = sums[target]
-            return carry
-
-        lax.fori_loop(0, slabs, one_slab, 0)
         width = slabs * LANES
-        total = conv[0]
-        for slab in range(1, slabs):
-            total = total + conv[slab]
-        mean = jnp.sum(total, axis=-1, keepdims=True) / width
-        squares = None
-        for slab in range(slabs):
-            centred = conv[slab] - mean
-            squares = centred * centred if squares is None else squares + centred * centred
-        scale = lax.rsqrt(jnp.sum(squares, axis=-1, keepdims=True) / width + EPSILON)
-        normed = jnp.concatenate(
-            [
-                ((conv[slab] - mean) * scale * param_ref[slab, pl.ds(49, 1), :]).astype(jnp.bfloat16)
-                for slab in range(slabs)
-            ],
-            axis=1,
-        )
+        rows = normed[...]
         update = None
         step = 32
         for ref in (own_ref, other_ref):
@@ -104,7 +149,7 @@
                 into = ref[pl.ds(chunk, step), 0].reshape(step * 16, width)
                 outof = ref[pl.ds(chunk, step), 1].reshape(step * 16, width)
                 hidden = lax.dot_general(
-                    normed, into, (((1,), (1,)), ((), ())), preferred_element_type=jnp.float32
+                    rows, into, (((1,), (1,)), ((), ())), preferred_element_type=jnp.float32
                 )
                 hidden = jax.nn.gelu(hidden, approximate=True).astype(jnp.bfloat16)
                 term = jnp.dot(hidden, outof, preferred_element_type=jnp.float32)
@@ -116,21 +161,16 @@
             ).astype(jnp.bfloat16)
 
 
-def detector_block(number, ints, tile, params, own, other):
-    cells, width = tile.shape
-    slabs = width // LANES
+def detector_block(number, ints, tile, params, own, other, *early):
     return pl.pallas_call(
         functools.partial(block_body, number=number),
         out_shape=pltpu.VMEM(tile.shape, jnp.bfloat16),
-        in_specs=[SMEM, VMEM, VMEM, VMEM, VMEM],
+        in_specs=[SMEM] + [VMEM] * (4 + len(early)),
         out_specs=VMEM,
-        scratch_shapes=[
-            pltpu.VMEM((slabs, TILE, 32, LANES), jnp.float32),
-            pltpu.VMEM((slabs, cells, LANES), jnp.float32),
-        ],
+        scratch_shapes=[pltpu.VMEM(tile.shape, jnp.bfloat16)] + conv_scratch(tile),
         compiler_params=LIMITED,
         name="detector_block",
-    )(ints, *map(resident, (tile, params, own, other)))
+    )(ints, *map(resident, (tile, params, own, other, *early)))
 
 
 def selection(top, left):
@@ -175,16 +215,24 @@
 
     @pl.when(active(ints_ref, len(out_refs) - 1))
     def _():
+        core = ints_ref[CORE_AT]
         for slot, out_ref in enumerate(out_refs):
             source = ints_ref[SLOT_AT + slot]
-            for number, (plan_ref, turn) in enumerate(((below_ref, 2), (ints_ref, 1), (above_ref, 0))):
-                base = slot * 9 + turn * 3
-                wanted = (source == number + 1) if number != 1 else ((source == 2) | (source == 0))
-                for micro in range(2):
-
-                    @pl.when(wanted & (plan_ref[base] == micro))
-                    def _(plan_ref=plan_ref, base=base, tile=tiles[2 * number + micro], out_ref=out_ref):
-                        chosen = selection(plan_ref[base + 1], plan_ref[base + 2])
+            base = slot * 9
+
+            def entry(part, source=source, base=base):
+                inner = jnp.where(source == 3, above_ref[base + part], ints_ref[base + 3 + part])
+                return jnp.where(source == 1, below_ref[base + 6 + part], inner)
+
+            same_chip = ((source == 1) & (core == 1)) | ((source == 3) & (core == 0))
+            away = (source == 1) | (source == 3)
+            micro = entry(0)
+            chosen = selection(entry(1), entry(2))
+            for number, wanted in enumerate((same_chip, ~away, away & ~same_chip)):
+                for index in range(2):
+
+                    @pl.when(wanted & (micro == index))
+                    def _(chosen=chosen, tile=tiles[2 * number + index], out_ref=out_ref):
                         rows = jnp.dot(chosen, tile[...], preferred_element_type=jnp.float32)
                         out_ref[...] = rows.astype(jnp.bfloat16)
 
@@ -424,16 +472,16 @@
     sections = lax.axis_size("section")
     count = lax.axis_size(REP)
     section = lax.axis_index("section").astype(jnp.int32)
-    parity = (lax.axis_index(REP) % 2).astype(jnp.int32).reshape(1)
+    core = lax.axis_index("core").astype(jnp.int32)
     width = tile_features.shape[3]
     slabs = width // LANES
     last = sections - 1
     upward = [(index, index + 1) for index in range(count - 1)]
     downward = [(target, origin) for origin, target in upward]
     swap = [(index, index ^ 1) for index in range(count)]
-    ints = jnp.concatenate([crop_plan.reshape(-1), slot_from.reshape(-1), section.reshape(1)])
-
-    half = packed_half(parity, cls_embed, cls_merge, cls_pos, cls_qkv.transpose(1, 0, 2), cls_out)
+    ints = jnp.concatenate([crop_plan.reshape(-1), slot_from.reshape(-1), section.reshape(1), core.reshape(1)])
+
+    half = packed_half(core.reshape(1), cls_embed, cls_merge, cls_pos, cls_qkv.transpose(1, 0, 2), cls_out)
     weights = lax.all_gather(half, ("section", "core"), axis=0)
 
     shard = jnp.stack([det_in[0].T, det_out[0]], axis=0)
@@ -447,22 +495,27 @@
         [det_kernel[0].reshape(49, width), det_gain, det_scale, jnp.zeros((5, width), jnp.float32)], axis=0
     )
     params = params.reshape(56, slabs, LANES).transpose(1, 0, 2)
-    plane = after(plane, below, above, params, *pixels)
+    start = tile_features.reshape(2, CELLS, width)
+    tiles = [start[0], start[1]]
+    early = early_norm(ints, tiles[0], params)
+    plane = after(plane, below, above, early, *pixels)
     own = plane.reshape((SIDE * SIDE,) + shard.shape)
     other = lax.ppermute(own, REP, swap)
 
-    start = tile_features.reshape(2, CELLS, width)
-    tiles = [start[0], start[1]]
     for number in range(sections):
-        done = [detector_block(number, ints, tile, params, own, other) for tile in tiles]
+        ahead = [(early,), ()] if number == 0 else [(), ()]
+        done = [
+            detector_block(number, ints, tile, params, own, other, *more) for tile, more in zip(tiles, ahead)
+        ]
         if number < last:
             tiles = [lax.ppermute(tile, "section", [(number, number + 1)]) for tile in done]
 
-    along = [(last * count + origin, last * count + target) for origin, target in upward]
-    back = [(target, origin) for origin, target in along]
-    from_below = [lax.ppermute(tile, ("section",) + REP, along) for tile in done]
-    from_above = [lax.ppermute(tile, ("section",) + REP, back) for tile in done]
-    crops = pick_crops(after(ints, weights), below, above, from_below + done + from_above, sections)
+    within = [(last * count + origin, last * count + target) for origin, target in swap]
+    across = [(last * count + index, last * count + index + 1) for index in range(1, count - 1, 2)]
+    across += [(target, origin) for origin, target in across]
+    near = [lax.ppermute(tile, ("section",) + REP, within) for tile in done]
+    far = [lax.ppermute(tile, ("section",) + REP, across) for tile in done]
+    crops = pick_crops(after(ints, weights), below, above, near + done + far, sections)
     feats = [lax.ppermute(crops[slot], "section", [(last, slot)]) for slot in range(last)] + [crops[last]]
     weights, base = staged(after(ints, *crops), pixels, weights)
     result = classify(ints, feats, base, weights, cls_gain)

time: 168 us -> 163 us (0.970)
  waiting for transfers between devices: 69.7 us -> 63.2 us
    ppermute x1, waiting for transfers between devices: 11.5 us -> 0.56 us  [per_device(): above = lax.ppermute(ints, REP, downward)]
    ppermute x1, waiting for transfers between devices: 0.01 us -> 9.87 us  [per_device(): lax.ppermute(cut[2], REP, upward)]
    ppermute x3, waiting for transfers between devices: 31.7 us -> 26.2 us  [per_device(): lax.ppermute(crops[slot], 'section', [(last, slot)])]
  transfers between devices with their start and end apart: 20 -> 20, of which waited for: 5 -> 6; matrix products, arithmetic and copies ran while one was open for 1% -> 1% of each run, Pallas kernels for 12% -> 12%
where the time goes in v3:
time: 163 us
  waiting for transfers between devices  63.2 us (39%)
  starting transfers between devices  34.4 us (21%)
  Pallas kernels  27.6 us (17%)
  blocking collectives  20.6 us (13%)
  between operations  13.9 us (9%)
  local copies, waits for them, and re-layouts  2.79 us (2%)
    ppermute x3, waiting for transfers between devices, per_device(): lax.ppermute(crops[slot], 'section', [(last, slot)])  26.2 us
    ppermute x6, waiting for transfers between devices, per_device(): lax.ppermute(tile, 'section', [(number, number + 1)])  22.4 us
    all_to_all x1, blocking collectives, spread_in_groups(): return lax.all_to_all(copies, REP, 0, 0, axis_index_groups=groups)  20.6 us
    pallas_call x8, Pallas kernels, detector_block(): pl.pallas_call(functools.partial(block_body, number=number), out_shape=pl...  12.7 us
    ppermute x1, waiting for transfers between devices, per_device(): lax.ppermute(cut[2], REP, upward)  9.87 us
    all_to_all x1, starting transfers between devices, spread_in_groups(): return lax.all_to_all(copies, REP, 0, 0, axis_index_groups=groups)  7.35 us
    ppermute x1, starting transfers between devices, per_device(): lax.ppermute(cut[0], REP, downward)  6.8 us
    ppermute x6, starting transfers between devices, per_device(): lax.ppermute(tile, 'section', [(number, number + 1)])  6.55 us
  transfers between devices with their start and end apart: 20, of which 6 were waited for; matrix products, arithmetic and copies ran while one was open for 1% of the time, Pallas kernels for 12%

profile of v3, /device:TPU:36, one launch (start us, length us, event | category | flops | bytes accessed | tf_op | source)
XLA Modules:
  0.0 162.5 jit_solution(9906659332575355356)
XLA Ops:
  6.5 2.3 %pack_weights.1 = bf16[3584,128]{1,0:T(8,128)(2,1)} custom-call(s32[1]{0:T(128)} %bitcast.2.parity_ref, bf16[768,256]{1,0:T(8,128)(2,1)} %embed.1, bf16[512,256]{1,0:T(8,128)(2,1)} %merge.1, bf16[196,256]{1,0:T(8,128)(2,1)} %pos.1, bf16[3,1024,128]{2,1,0:T(8,128)(2,1)} %bitcast.34, bf16[128,1024]{1,0:T(8,128)(2,1)} %out.1), custom_call_target="tpu_custom_call" | custom-call | tf_op jit(solution)/shard_map/pack_weights/pallas_call | solution.py:289
  8.9 0.0 all-gather.3.cloned.1.call-update
  9.0 20.6 %all_to_all.10 = bf16[8,2,16,512]{3,2,1,0:T(8,128)(2,1)S(1)} all-to-all(bf16[8,2,16,512]{3,2,1,0:T(8,128)(2,1)S(1)} %broadcast_in_dim.9), channel_id=1, replica_groups={{0,2,4,6,8,10,12,14},{16,18,20,22,24,26,28,30},{32,34,36,38,40,42,44,46..., dimensions={0} | all-to-all | bytes 524288 | tf_op jit(solution)/shard_map/all_to_all | solution.py:43
  29.6 1.7 %broadcast_in_dim.20 = bf16[8,8,2,16,512]{4,3,2,1,0:T(8,128)(2,1)} broadcast(bf16[8,2,16,512]{3,2,1,0:T(8,128)(2,1)S(1)} %all_to_all.10), dimensions={1,2,3,4} | broadcast | bytes 2359296 | tf_op jit(solution)/shard_map/broadcast_in_dim | solution.py:42
  31.2 0.0 copy-start.9
  31.2 0.0 copy-start.10
  31.3 0.0 copy-start.3
  31.3 7.3 %all-to-all-start.1 = ((bf16[8,8,2,16,512]{4,3,2,1,0:T(8,128)(2,1)}), bf16[8,8,2,16,512]{4,3,2,1,0:T(8,128)(2,1)S(1)}, u32[]{:S(2)}, u32[]{:S(2)}) async-start(bf16[8,8,2,16,512]{4,3,2,1,0:T(8,128)(2,1)} %broadcast_in_dim.20), calls=%async_computation.1 | async-start | bytes 4194304 | tf_op jit(solution)/shard_map/all_to_all | solution.py:43
  38.6 0.1 copy.17
  38.7 0.1 reshape.32
  38.8 0.1 pad_add_fusion.ints_ref
  38.9 1.9 %collective-permute-start.1 = (s32[42]{0:T(128)S(1)}, s32[42]{0:T(128)S(1)}, u32[]{:S(2)}, u32[]{:S(2)}) collective-permute-start(s32[42]{0:T(128)S(1)} %pad_add_fusion.ints_ref), channel_id=1, source_target_pairs={{1,0},{2,1},{3,2},{4,3},{5,4},{6,5},{7,6},{8,7},{9,8},{10,9},{11,1... | collective-permute-start | bytes 512 | tf_op jit(solution)/shard_map/ppermute | solution.py:493
  40.8 2.4 %collective-permute-start = (s32[42]{0:T(128)S(1)}, s32[42]{0:T(128)S(1)}, u32[]{:S(2)}, u32[]{:S(2)}) collective-permute-start(s32[42]{0:T(128)S(1)} %pad_add_fusion.ints_ref), channel_id=1, source_target_pairs={{0,1},{1,2},{2,3},{3,4},{4,5},{5,6},{6,7},{7,8},{8,9},{9,10},{10,1... | collective-permute-start | bytes 512 | tf_op jit(solution)/shard_map/ppermute | solution.py:492
  43.3 2.0 %cut_pixels.1 = (bf16[208,768]{1,0:T(8,128)(2,1)S(1)}, bf16[208,768]{1,0:T(8,128)(2,1)S(1)}, bf16[208,768]{1,0:T(8,128)(2,1)S(1)}) custom-call(s32[42]{0:T(128)S(1)} %pad_add_fusion.ints_ref, bf16[2,256,768]{2,1,0:T(8,128)(2,1)S(1)} %bitcast.32), custom_call_target="tpu_custom_call" | custom-call | tf_op jit(solution)/shard_map/cut_pixels/pallas_call | solution.py:202
  45.3 2.1 %collective-permute-start.2 = (bf16[208,768]{1,0:T(8,128)(2,1)S(1)}, bf16[208,768]{1,0:T(8,128)(2,1)S(1)}, u32[]{:S(2)}, u32[]{:S(2)}) collective-permute-start(bf16[208,768]{1,0:T(8,128)(2,1)S(1)} %get-tuple-element.20), channel_id=1, source_target_pairs={{0,1},{1,2},{2,3},{3,4},{4,5},{5,6},{6,7},{7,8},{8,9},{9,10},{10,1... | collective-permute-start | bytes 958472 | tf_op jit(solution)/shard_map/ppermute | solution.py:491
  47.4 6.8 %collective-permute-start.3 = (bf16[208,768]{1,0:T(8,128)(2,1)S(1)}, bf16[208,768]{1,0:T(8,128)(2,1)}, u32[]{:S(2)}, u32[]{:S(2)}) collective-permute-start(bf16[208,768]{1,0:T(8,128)(2,1)S(1)} %get-tuple-element.22), channel_id=1, source_target_pairs={{1,0},{2,1},{3,2},{4,3},{5,4},{6,5},{7,6},{8,7},{9,8},{10,9},{11,1... | collective-permute-start | bytes 958472 | tf_op jit(solution)/shard_map/ppermute | solution.py:491
  54.2 0.1 pad.5.clone
  54.3 0.1 maximum_bitcast_fusion.param_ref
  54.4 0.6 early_norm.1.refs_0_
  55.0 0.6 collective-permute-done.1.above_ref
  55.5 0.0 collective-permute-done.below_ref
  55.6 9.9 %collective-permute-done.2.pix_below = bf16[208,768]{1,0:T(8,128)(2,1)S(1)} collective-permute-done((bf16[208,768]{1,0:T(8,128)(2,1)S(1)}, bf16[208,768]{1,0:T(8,128)(2,1)S(1)}, u32[]{:S(2)}, u32[]{:S(2)}) %collective-permute-start.2) | collective-permute-done | bytes 319520 | tf_op jit(solution)/shard_map/ppermute | solution.py:491
  65.4 0.7 copy-done.4
  66.2 0.0 collective-permute-done.3.pix_above
  66.2 0.0 all-to-all-done.1
  66.2 1.9 %collective-permute-start.4 = (bf16[64,2,16,512]{3,2,1,0:T(8,128)(2,1)S(1)}, bf16[64,2,16,512]{3,2,1,0:T(8,128)(2,1)S(1)}, u32[]{:S(2)}, u32[]{:S(2)}) collective-permute-start(bf16[64,2,16,512]{3,2,1,0:T(8,128)(2,1)S(1)} %bitcast.20), channel_id=1, source_target_pairs={{0,1},{1,0},{2,3},{3,2},{4,5},{5,4},{6,7},{7,6},{8,9},{9,8},{10,11... | collective-permute-start | bytes 6291464 | tf_op jit(solution)/shard_map/ppermute | solution.py:503
  68.1 4.1 %collective-permute-done.4.other_ref = bf16[64,2,16,512]{3,2,1,0:T(8,128)(2,1)S(1)} collective-permute-done((bf16[64,2,16,512]{3,2,1,0:T(8,128)(2,1)S(1)}, bf16[64,2,16,512]{3,2,1,0:T(8,128)(2,1)S(1)}, u32[]{:S(2)}, u32[]{:S(2)}) %collective-permute-start.4) | collective-permute-done | bytes 2097184 | tf_op jit(solution)/shard_map/ppermute | solution.py:503
  72.2 0.5 detector_block.12
  72.8 0.7 collective-permute-start.9
  73.5 0.6 detector_block.8
  74.0 0.7 collective-permute-start.5
  74.7 0.0 collective-permute-done.9.tile_ref
  74.7 0.6 detector_block.13
  75.3 1.3 collective-permute-start.10
  76.6 0.0 collective-permute-done.5.tile_ref
  76.6 0.6 detector_block.9
  77.1 1.3 collective-permute-start.6
  78.4 19.3 %collective-permute-done.10.tile_ref = bf16[256,512]{1,0:T(8,128)(2,1)S(1)} collective-permute-done((bf16[256,512]{1,0:T(8,128)(2,1)S(1)}, bf16[256,512]{1,0:T(8,128)(2,1)S(1)}, u32[]{:S(2)}, u32[]{:S(2)}) %collective-permute-start.10) | collective-permute-done | bytes 262176 | tf_op jit(solution)/shard_map/ppermute | solution.py:511
  97.8 4.8 %detector_block.14 = bf16[256,512]{1,0:T(8,128)(2,1)S(1)} custom-call(s32[42]{0:T(128)S(1)} %pad_add_fusion.ints_ref, bf16[256,512]{1,0:T(8,128)(2,1)S(1)} %collective-permute-done.10.tile_ref, f32[4,56,128]{2,1,0:T(8,128)S(1)} %maximum_bitcast_fusion.param_ref, bf16[64,2,16,512]{3,2,1,0:T(8,128)(2,1)S(1)} %bitcast.25, ...), custom_call_target="tpu_custom_call" | custom-call | tf_op jit(solution)/shard_map/detector_block/pallas_call | solution.py:165
  102.6 1.3 collective-permute-start.11
  103.9 0.0 collective-permute-done.6.tile_ref
  103.9 4.6 %detector_block.10 = bf16[256,512]{1,0:T(8,128)(2,1)S(1)} custom-call(s32[42]{0:T(128)S(1)} %pad_add_fusion.ints_ref, bf16[256,512]{1,0:T(8,128)(2,1)S(1)} %collective-permute-done.6.tile_ref, f32[4,56,128]{2,1,0:T(8,128)S(1)} %maximum_bitcast_fusion.param_ref, bf16[64,2,16,512]{3,2,1,0:T(8,128)(2,1)S(1)} %bitcast.26, ...), custom_call_target="tpu_custom_call" | custom-call | tf_op jit(solution)/shard_map/detector_block/pallas_call | solution.py:165
  108.5 1.3 collective-permute-start.7
  109.8 0.0 collective-permute-done.11.tile_ref
  109.8 0.6 detector_block.15.refs_3_
  110.4 0.7 collective-permute-start.14
  111.1 0.7 collective-permute-start.12
  111.7 3.1 %collective-permute-done.7.tile_ref = bf16[256,512]{1,0:T(8,128)(2,1)S(1)} collective-permute-done((bf16[256,512]{1,0:T(8,128)(2,1)S(1)}, bf16[256,512]{1,0:T(8,128)(2,1)S(1)}, u32[]{:S(2)}, u32[]{:S(2)}) %collective-permute-start.7) | collective-permute-done | bytes 262176 | tf_op jit(solution)/shard_map/ppermute | solution.py:511
  114.8 0.5 detector_block.11.refs_2_
  115.4 0.7 collective-permute-start.13
  116.1 0.7 collective-permute-start.8
  116.8 0.0 all-gather.3.cloned.1.call-done
  116.8 0.0 collective-permute-done.14.refs_5_
  116.8 0.0 collective-permute-done.12.refs_1_
  116.8 0.6 pick_crops.1
  117.4 0.7 collective-permute-start.15
  118.1 0.7 collective-permute-start.16
  118.8 1.3 collective-permute-start.17
  120.1 0.0 copy-start.2
  120.1 4.8 %stage_weights.1 = (bf16[8,3584,128]{2,1,0:T(8,128)(2,1)S(1)}, f32[208,1024]{1,0:T(8,128)S(1)}) custom-call(s32[42]{0:T(128)S(1)} %pad_add_fusion.ints_ref, bf16[208,768]{1,0:T(8,128)(2,1)} %copy-done.4, bf16[208,768]{1,0:T(8,128)(2,1)} %copy-done.1, bf16[208,768]{1,0:T(8,128)(2,1)} %collective-permute-done.3.pix_above, bf16[8,3584,128]{2,1,0:T(8,128)(2,1)} %bitcast.33), custom_call_target="tpu_custom_call" | custom-call | tf_op jit(solution)/shard_map/stage_weights/pallas_call | solution.py:342
  124.8 0.0 collective-permute-done.15.refs_0_
  124.8 0.0 collective-permute-done.16.refs_1_
  124.9 26.2 %collective-permute-done.17.refs_2_ = bf16[208,512]{1,0:T(8,128)(2,1)S(1)} collective-permute-done((bf16[208,512]{1,0:T(8,128)(2,1)S(1)}, bf16[208,512]{1,0:T(8,128)(2,1)S(1)}, u32[]{:S(2)}, u32[]{:S(2)}) %collective-permute-start.17) | collective-permute-done | bytes 213024 | tf_op jit(solution)/shard_map/ppermute | solution.py:519
  151.0 4.7 %classify.1 = f32[1,1024]{1,0:T(1,128)} custom-call(s32[42]{0:T(128)S(1)} %pad_add_fusion.ints_ref, bf16[208,512]{1,0:T(8,128)(2,1)S(1)} %collective-permute-done.15.refs_0_, bf16[208,512]{1,0:T(8,128)(2,1)S(1)} %collective-permute-done.16.refs_1_, bf16[208,512]{1,0:T(8,128)(2,1)S(1)} %collective-permute-done.17.refs_2_, ...), custom_call_target="tpu_custom_call" | custom-call | tf_op jit(solution)/shard_map/classify/pallas_call | solution.py:440
  (27 shorter events, 0.1 us)
Async XLA Ops:
  6.5 2.4 %copy-start.6 = (bf16[1,16,512]{2,1,0:T(8,128)(2,1)S(1)}, bf16[1,16,512]{2,1,0:T(8,128)(2,1)}, u32[]{:S(2)}) copy-start(bf16[1,16,512]{2,1,0:T(8,128)(2,1)} %param.20) | copy-start | bytes 49156
  6.5 2.4 %copy-start.7 = (bf16[1,512,16]{1,2,0:T(8,128)(2,1)S(1)}, bf16[1,512,16]{1,2,0:T(8,128)(2,1)}, u32[]{:S(2)}) copy-start(bf16[1,512,16]{1,2,0:T(8,128)(2,1)} %param.19) | copy-start | bytes 49156
  6.5 110.2 %all-gather.3.cloned.1.call-start = ((), (), s32[]{:S(2)}) async-start(), calls=%async_computation.2 | async-start | bytes 8257536 | tf_op jit(solution)/shard_map/all_gather | solution.py:485
  31.2 7.4 %copy-start.8 = (s32[1,4,3,3]{1,0,3,2:T(1,128)S(1)}, s32[1,4,3,3]{1,0,3,2:T(1,128)}, u32[]{:S(2)}) copy-start(s32[1,4,3,3]{1,0,3,2:T(1,128)} %param.28) | copy-start | bytes 436
  31.2 7.6 %copy-start.11 = (s32[1,4]{1,0:T(1,128)S(1)}, s32[1,4]{1,0:T(1,128)}, u32[]{:S(2)}) copy-start(s32[1,4]{1,0:T(1,128)} %param.29) | copy-start | bytes 52
  31.2 12.0 %copy-start = (bf16[2,16,16,768]{3,2,1,0:T(8,128)(2,1)S(1)}, bf16[2,16,16,768]{3,2,1,0:T(8,128)(2,1)}, u32[]{:S(2)}) copy-start(bf16[2,16,16,768]{3,2,1,0:T(8,128)(2,1)} %param.16) | copy-start | bytes 2359300
  31.2 23.0 %copy-start.5 = (f32[1,7,7,512]{3,0,2,1:T(1,128)S(1)}, f32[1,7,7,512]{3,0,2,1:T(1,128)}, u32[]{:S(2)}) copy-start(f32[1,7,7,512]{3,0,2,1:T(1,128)} %param.17) | copy-start | bytes 301060
  31.2 23.1 %copy-start.9 = (f32[1,512]{1,0:T(1,128)S(1)}, f32[1,512]{1,0:T(1,128)}, u32[]{:S(2)}) copy-start(f32[1,512]{1,0:T(1,128)} %param.21) | copy-start | bytes 6148
  31.2 23.1 %copy-start.10 = (f32[1,512]{1,0:T(1,128)S(1)}, f32[1,512]{1,0:T(1,128)}, u32[]{:S(2)}) copy-start(f32[1,512]{1,0:T(1,128)} %param.18) | copy-start | bytes 6148
  31.3 23.1 %copy-start.3 = (bf16[2,16,16,512]{3,2,1,0:T(8,128)(2,1)S(1)}, bf16[2,16,16,512]{3,2,1,0:T(8,128)(2,1)}, u32[]{:S(2)}) copy-start(bf16[2,16,16,512]{3,2,1,0:T(8,128)(2,1)} %param.15) | copy-start | bytes 1572868
  31.3 34.9 %all-to-all-start.1 = ((bf16[8,8,2,16,512]{4,3,2,1,0:T(8,128)(2,1)}), bf16[8,8,2,16,512]{4,3,2,1,0:T(8,128)(2,1)S(1)}, u32[]{:S(2)}, u32[]{:S(2)}) async-start(bf16[8,8,2,16,512]{4,3,2,1,0:T(8,128)(2,1)} %broadcast_in_dim.20), calls=%async_computation.1 | async-start | bytes 4194304 | tf_op jit(solution)/shard_map/all_to_all | solution.py:43
  38.9 16.6 %collective-permute-start.1 = (s32[42]{0:T(128)S(1)}, s32[42]{0:T(128)S(1)}, u32[]{:S(2)}, u32[]{:S(2)}) collective-permute-start(s32[42]{0:T(128)S(1)} %pad_add_fusion.ints_ref), channel_id=1, source_target_pairs={{1,0},{2,1},{3,2},{4,3},{5,4},{6,5},{7,6},{8,7},{9,8},{10,9},{11,1... | collective-permute-start | bytes 512 | tf_op jit(solution)/shard_map/ppermute | solution.py:493
  40.8 14.7 %collective-permute-start = (s32[42]{0:T(128)S(1)}, s32[42]{0:T(128)S(1)}, u32[]{:S(2)}, u32[]{:S(2)}) collective-permute-start(s32[42]{0:T(128)S(1)} %pad_add_fusion.ints_ref), channel_id=1, source_target_pairs={{0,1},{1,2},{2,3},{3,4},{4,5},{5,6},{6,7},{7,8},{8,9},{9,10},{10,1... | collective-permute-start | bytes 512 | tf_op jit(solution)/shard_map/ppermute | solution.py:492
  45.3 20.2 %copy-start.1 = (bf16[208,768]{1,0:T(8,128)(2,1)}, bf16[208,768]{1,0:T(8,128)(2,1)S(1)}, u32[]{:S(2)}) copy-start(bf16[208,768]{1,0:T(8,128)(2,1)S(1)} %get-tuple-element.21.pix_own) | copy-start | bytes 958468
  45.3 20.1 %collective-permute-start.2 = (bf16[208,768]{1,0:T(8,128)(2,1)S(1)}, bf16[208,768]{1,0:T(8,128)(2,1)S(1)}, u32[]{:S(2)}, u32[]{:S(2)}) collective-permute-start(bf16[208,768]{1,0:T(8,128)(2,1)S(1)} %get-tuple-element.20), channel_id=1, source_target_pairs={{0,1},{1,2},{2,3},{3,4},{4,5},{5,6},{6,7},{7,8},{8,9},{9,10},{10,1... | collective-permute-start | bytes 958472 | tf_op jit(solution)/shard_map/ppermute | solution.py:491
  47.4 18.8 %collective-permute-start.3 = (bf16[208,768]{1,0:T(8,128)(2,1)S(1)}, bf16[208,768]{1,0:T(8,128)(2,1)}, u32[]{:S(2)}, u32[]{:S(2)}) collective-permute-start(bf16[208,768]{1,0:T(8,128)(2,1)S(1)} %get-tuple-element.22), channel_id=1, source_target_pairs={{1,0},{2,1},{3,2},{4,3},{5,4},{6,5},{7,6},{8,7},{9,8},{10,9},{11,1... | collective-permute-start | bytes 958472 | tf_op jit(solution)/shard_map/ppermute | solution.py:491
  65.4 0.7 copy-start.4
  66.2 6.0 %collective-permute-start.4 = (bf16[64,2,16,512]{3,2,1,0:T(8,128)(2,1)S(1)}, bf16[64,2,16,512]{3,2,1,0:T(8,128)(2,1)S(1)}, u32[]{:S(2)}, u32[]{:S(2)}) collective-permute-start(bf16[64,2,16,512]{3,2,1,0:T(8,128)(2,1)S(1)} %bitcast.20), channel_id=1, source_target_pairs={{0,1},{1,0},{2,3},{3,2},{4,5},{5,4},{6,7},{7,6},{8,9},{9,8},{10,11... | collective-permute-start | bytes 6291464 | tf_op jit(solution)/shard_map/ppermute | solution.py:503
  72.8 1.9 %collective-permute-start.9 = (bf16[256,512]{1,0:T(8,128)(2,1)S(1)}, bf16[256,512]{1,0:T(8,128)(2,1)S(1)}, u32[]{:S(2)}, u32[]{:S(2)}) collective-permute-start(bf16[256,512]{1,0:T(8,128)(2,1)S(1)} %detector_block.12), channel_id=1, source_target_pairs={{0,128},{1,129},{2,130},{3,131},{4,132},{5,133},{6,134},{7,135},{8... | collective-permute-start | bytes 786440 | tf_op jit(solution)/shard_map/ppermute | solution.py:511
  74.0 2.6 %collective-permute-start.5 = (bf16[256,512]{1,0:T(8,128)(2,1)S(1)}, bf16[256,512]{1,0:T(8,128)(2,1)S(1)}, u32[]{:S(2)}, u32[]{:S(2)}) collective-permute-start(bf16[256,512]{1,0:T(8,128)(2,1)S(1)} %detector_block.8), channel_id=1, source_target_pairs={{0,128},{1,129},{2,130},{3,131},{4,132},{5,133},{6,134},{7,135},{8... | collective-permute-start | bytes 786440 | tf_op jit(solution)/shard_map/ppermute | solution.py:511
  75.3 22.5 %collective-permute-start.10 = (bf16[256,512]{1,0:T(8,128)(2,1)S(1)}, bf16[256,512]{1,0:T(8,128)(2,1)S(1)}, u32[]{:S(2)}, u32[]{:S(2)}) collective-permute-start(bf16[256,512]{1,0:T(8,128)(2,1)S(1)} %detector_block.13), channel_id=1, source_target_pairs={{128,256},{129,257},{130,258},{131,259},{132,260},{133,261},{134,2... | collective-permute-start | bytes 786440 | tf_op jit(solution)/shard_map/ppermute | solution.py:511
  77.1 26.7 %collective-permute-start.6 = (bf16[256,512]{1,0:T(8,128)(2,1)S(1)}, bf16[256,512]{1,0:T(8,128)(2,1)S(1)}, u32[]{:S(2)}, u32[]{:S(2)}) collective-permute-start(bf16[256,512]{1,0:T(8,128)(2,1)S(1)} %detector_block.9), channel_id=1, source_target_pairs={{128,256},{129,257},{130,258},{131,259},{132,260},{133,261},{134,2... | collective-permute-start | bytes 786440 | tf_op jit(solution)/shard_map/ppermute | solution.py:511
  102.6 7.3 %collective-permute-start.11 = (bf16[256,512]{1,0:T(8,128)(2,1)S(1)}, bf16[256,512]{1,0:T(8,128)(2,1)S(1)}, u32[]{:S(2)}, u32[]{:S(2)}) collective-permute-start(bf16[256,512]{1,0:T(8,128)(2,1)S(1)} %detector_block.14), channel_id=1, source_target_pairs={{256,384},{257,385},{258,386},{259,387},{260,388},{261,389},{262,3... | collective-permute-start | bytes 786440 | tf_op jit(solution)/shard_map/ppermute | solution.py:511
  108.5 6.3 %collective-permute-start.7 = (bf16[256,512]{1,0:T(8,128)(2,1)S(1)}, bf16[256,512]{1,0:T(8,128)(2,1)S(1)}, u32[]{:S(2)}, u32[]{:S(2)}) collective-permute-start(bf16[256,512]{1,0:T(8,128)(2,1)S(1)} %detector_block.10), channel_id=1, source_target_pairs={{256,384},{257,385},{258,386},{259,387},{260,388},{261,389},{262,3... | collective-permute-start | bytes 786440 | tf_op jit(solution)/shard_map/ppermute | solution.py:511
  110.4 6.4 %collective-permute-start.14 = (bf16[256,512]{1,0:T(8,128)(2,1)S(1)}, bf16[256,512]{1,0:T(8,128)(2,1)S(1)}, u32[]{:S(2)}, u32[]{:S(2)}) collective-permute-start(bf16[256,512]{1,0:T(8,128)(2,1)S(1)} %detector_block.15.refs_3_), channel_id=1, source_target_pairs={{385,386},{387,388},{389,390},{391,392},{393,394},{395,396},{397,3... | collective-permute-start | bytes 786440 | tf_op jit(solution)/shard_map/ppermute | solution.py:517
  111.1 5.7 %collective-permute-start.12 = (bf16[256,512]{1,0:T(8,128)(2,1)S(1)}, bf16[256,512]{1,0:T(8,128)(2,1)S(1)}, u32[]{:S(2)}, u32[]{:S(2)}) collective-permute-start(bf16[256,512]{1,0:T(8,128)(2,1)S(1)} %detector_block.15.refs_3_), channel_id=1, source_target_pairs={{384,385},{385,384},{386,387},{387,386},{388,389},{389,388},{390,3... | collective-permute-start | bytes 786440 | tf_op jit(solution)/shard_map/ppermute | solution.py:516
  115.4 1.4 collective-permute-start.13
  116.1 0.7 collective-permute-start.8
  117.4 7.4 %collective-permute-start.15 = (bf16[208,512]{1,0:T(8,128)(2,1)S(1)}, bf16[208,512]{1,0:T(8,128)(2,1)S(1)}, u32[]{:S(2)}, u32[]{:S(2)}) collective-permute-start(bf16[208,512]{1,0:T(8,128)(2,1)S(1)} %get-tuple-element.24), channel_id=1, source_target_pairs={{384,0},{385,1},{386,2},{387,3},{388,4},{389,5},{390,6},{391,7},{3... | collective-permute-start | bytes 638984 | tf_op jit(solution)/shard_map/ppermute | solution.py:519
  118.1 6.8 %collective-permute-start.16 = (bf16[208,512]{1,0:T(8,128)(2,1)S(1)}, bf16[208,512]{1,0:T(8,128)(2,1)S(1)}, u32[]{:S(2)}, u32[]{:S(2)}) collective-permute-start(bf16[208,512]{1,0:T(8,128)(2,1)S(1)} %get-tuple-element.25), channel_id=1, source_target_pairs={{384,128},{385,129},{386,130},{387,131},{388,132},{389,133},{390,1... | collective-permute-start | bytes 638984 | tf_op jit(solution)/shard_map/ppermute | solution.py:519
  118.8 32.3 %collective-permute-start.17 = (bf16[208,512]{1,0:T(8,128)(2,1)S(1)}, bf16[208,512]{1,0:T(8,128)(2,1)S(1)}, u32[]{:S(2)}, u32[]{:S(2)}) collective-permute-start(bf16[208,512]{1,0:T(8,128)(2,1)S(1)} %get-tuple-element.26), channel_id=1, source_target_pairs={{384,256},{385,257},{386,258},{387,259},{388,260},{389,261},{390,2... | collective-permute-start | bytes 638984 | tf_op jit(solution)/shard_map/ppermute | solution.py:519
  120.1 31.0 %copy-start.2 = (f32[2,1024]{1,0:T(2,128)S(1)}, f32[2,1024]{1,0:T(2,128)}, u32[]{:S(2)}) copy-start(f32[2,1024]{1,0:T(2,128)} %refs_6_.1) | copy-start | bytes 24580
Sparse Core Ops, SparseCore 0:
  9.5 53.7 all-gather.2

commit v4 on v3

--- a/solution.py
+++ b/solution.py
@@ -271,18 +271,19 @@
 
         @pl.when(parity_ref[0] == parity)
         def _(pieces=pieces):
-            copies = [
-                pltpu.make_async_copy(piece, buffer.at[pl.ds(at, piece.shape[0])], sems.at[number])
-                for number, (piece, at) in enumerate(pieces)
-            ]
-            for copy in copies:
-                copy.start()
-            for copy in copies:
+            copies, results = [], []
+            for number, (piece, at) in enumerate(pieces):
+                place = pl.ds(at, piece.shape[0])
+                copies.append(pltpu.make_async_copy(piece, buffer.at[place], sems.at[2 * number]))
+                results.append(
+                    pltpu.make_async_copy(buffer.at[place], packed.at[place], sems.at[2 * number + 1])
+                )
+                copies[-1].start()
+            for copy, result in zip(copies, results):
                 copy.wait()
-
-    result = pltpu.make_async_copy(buffer, packed, sems.at[12])
-    result.start()
-    result.wait()
+                result.start()
+            for result in results:
+                result.wait()
 
 
 def packed_half(parity, embed, merge, pos, qkv, out):
@@ -291,7 +292,7 @@
         out_shape=jax.ShapeDtypeStruct((HALF, LANES), jnp.bfloat16),
         in_specs=[SMEM] + [ANY] * 5,
         out_specs=ANY,
-        scratch_shapes=[pltpu.VMEM((HALF, LANES), jnp.bfloat16), pltpu.SemaphoreType.DMA((13,))],
+        scratch_shapes=[pltpu.VMEM((HALF, LANES), jnp.bfloat16), pltpu.SemaphoreType.DMA((24,))],
         compiler_params=LIMITED,
         name="pack_weights",
     )(parity, *map(in_hbm, (embed, merge, pos, qkv, out)))
@@ -504,17 +505,18 @@
 
     for number in range(sections):
         ahead = [(early,), ()] if number == 0 else [(), ()]
-        done = [
-            detector_block(number, ints, tile, params, own, other, *more) for tile, more in zip(tiles, ahead)
-        ]
+        done = []
+        for tile, more in zip(tiles, ahead):
+            order = after(ints, *done)
+            done.append(detector_block(number, order, tile, params, own, other, *more))
         if number < last:
             tiles = [lax.ppermute(tile, "section", [(number, number + 1)]) for tile in done]
 
     within = [(last * count + origin, last * count + target) for origin, target in swap]
     across = [(last * count + index, last * count + index + 1) for index in range(1, count - 1, 2)]
     across += [(target, origin) for origin, target in across]
-    near = [lax.ppermute(tile, ("section",) + REP, within) for tile in done]
     far = [lax.ppermute(tile, ("section",) + REP, across) for tile in done]
+    near = [lax.ppermute(tile, ("section",) + REP, within) for tile in lax.optimization_barrier(tuple(done))]
     crops = pick_crops(after(ints, weights), below, above, near + done + far, sections)
     feats = [lax.ppermute(crops[slot], "section", [(last, slot)]) for slot in range(last)] + [crops[last]]
     weights, base = staged(after(ints, *crops), pixels, weights)

time: 163 us -> 165 us (1.012)
  waiting for transfers between devices: 63.2 us -> 65.2 us
    ppermute x3, waiting for transfers between devices: 26.2 us -> 27.8 us  [per_device(): lax.ppermute(crops[slot], 'section', [(last, slot)])]
  transfers between devices with their start and end apart: 20 -> 20, of which waited for: 6 -> 7; matrix products, arithmetic and copies ran while one was open for 1% -> 1% of each run, Pallas kernels for 12% -> 12%
where the time goes in v4:
time: 165 us; the launch traced here: 164 us
  waiting for transfers between devices  65.2 us (40%)
  starting transfers between devices  34.4 us (21%)
  Pallas kernels  27.4 us (17%)
  blocking collectives  20.6 us (12%)
  between operations  13.9 us (8%)
  local copies, waits for them, and re-layouts  2.79 us (2%)
    ppermute x3, waiting for transfers between devices, per_device(): lax.ppermute(crops[slot], 'section', [(last, slot)])  27.8 us
    ppermute x6, waiting for transfers between devices, per_device(): lax.ppermute(tile, 'section', [(number, number + 1)])  22.7 us
    all_to_all x1, blocking collectives, spread_in_groups(): return lax.all_to_all(copies, REP, 0, 0, axis_index_groups=groups)  20.6 us
    pallas_call x8, Pallas kernels, detector_block(): pl.pallas_call(functools.partial(block_body, number=number), out_shape=pl...  12.7 us
    ppermute x1, waiting for transfers between devices, per_device(): lax.ppermute(cut[2], REP, upward)  9.87 us
    all_to_all x1, starting transfers between devices, spread_in_groups(): return lax.all_to_all(copies, REP, 0, 0, axis_index_groups=groups)  7.35 us
    ppermute x1, starting transfers between devices, per_device(): lax.ppermute(cut[0], REP, downward)  6.67 us
    ppermute x6, starting transfers between devices, per_device(): lax.ppermute(tile, 'section', [(number, number + 1)])  6.55 us
  transfers between devices with their start and end apart: 20, of which 7 were waited for; matrix products, arithmetic and copies ran while one was open for 1% of the time, Pallas kernels for 12%

profile of v4, /device:TPU:36, one launch (start us, length us, event | category | flops | bytes accessed | tf_op | source)
XLA Modules:
  0.0 164.4 jit_solution(8118028516820047728)
XLA Ops:
  6.5 2.2 %pack_weights.1 = bf16[3584,128]{1,0:T(8,128)(2,1)} custom-call(s32[1]{0:T(128)} %bitcast.2.parity_ref, bf16[768,256]{1,0:T(8,128)(2,1)} %embed.1, bf16[512,256]{1,0:T(8,128)(2,1)} %merge.1, bf16[196,256]{1,0:T(8,128)(2,1)} %pos.1, bf16[3,1024,128]{2,1,0:T(8,128)(2,1)} %bitcast.34, bf16[128,1024]{1,0:T(8,128)(2,1)} %out.1), custom_call_target="tpu_custom_call" | custom-call | tf_op jit(solution)/shard_map/pack_weights/pallas_call | solution.py:290
  8.7 0.0 all-gather.3.cloned.1.call-update
  8.8 20.6 %all_to_all.10 = bf16[8,2,16,512]{3,2,1,0:T(8,128)(2,1)S(1)} all-to-all(bf16[8,2,16,512]{3,2,1,0:T(8,128)(2,1)S(1)} %broadcast_in_dim.9), channel_id=1, replica_groups={{0,2,4,6,8,10,12,14},{16,18,20,22,24,26,28,30},{32,34,36,38,40,42,44,46..., dimensions={0} | all-to-all | bytes 524288 | tf_op jit(solution)/shard_map/all_to_all | solution.py:43
  29.4 1.7 %broadcast_in_dim.20 = bf16[8,8,2,16,512]{4,3,2,1,0:T(8,128)(2,1)} broadcast(bf16[8,2,16,512]{3,2,1,0:T(8,128)(2,1)S(1)} %all_to_all.10), dimensions={1,2,3,4} | broadcast | bytes 2359296 | tf_op jit(solution)/shard_map/broadcast_in_dim | solution.py:42
  31.1 0.0 copy-start.9
  31.1 0.0 copy-start.10
  31.1 0.0 copy-start.3
  31.1 7.3 %all-to-all-start.1 = ((bf16[8,8,2,16,512]{4,3,2,1,0:T(8,128)(2,1)}), bf16[8,8,2,16,512]{4,3,2,1,0:T(8,128)(2,1)S(1)}, u32[]{:S(2)}, u32[]{:S(2)}) async-start(bf16[8,8,2,16,512]{4,3,2,1,0:T(8,128)(2,1)} %broadcast_in_dim.20), calls=%async_computation.1 | async-start | bytes 4194304 | tf_op jit(solution)/shard_map/all_to_all | solution.py:43
  38.5 0.1 copy.17
  38.6 0.1 reshape.32
  38.7 0.1 pad_add_fusion.ints_ref
  38.8 1.9 %collective-permute-start.1 = (s32[42]{0:T(128)S(1)}, s32[42]{0:T(128)S(1)}, u32[]{:S(2)}, u32[]{:S(2)}) collective-permute-start(s32[42]{0:T(128)S(1)} %pad_add_fusion.ints_ref), channel_id=1, source_target_pairs={{1,0},{2,1},{3,2},{4,3},{5,4},{6,5},{7,6},{8,7},{9,8},{10,9},{11,1... | collective-permute-start | bytes 512 | tf_op jit(solution)/shard_map/ppermute | solution.py:494
  40.7 2.4 %collective-permute-start = (s32[42]{0:T(128)S(1)}, s32[42]{0:T(128)S(1)}, u32[]{:S(2)}, u32[]{:S(2)}) collective-permute-start(s32[42]{0:T(128)S(1)} %pad_add_fusion.ints_ref), channel_id=1, source_target_pairs={{0,1},{1,2},{2,3},{3,4},{4,5},{5,6},{6,7},{7,8},{8,9},{9,10},{10,1... | collective-permute-start | bytes 512 | tf_op jit(solution)/shard_map/ppermute | solution.py:493
  43.1 2.0 %cut_pixels.1 = (bf16[208,768]{1,0:T(8,128)(2,1)S(1)}, bf16[208,768]{1,0:T(8,128)(2,1)S(1)}, bf16[208,768]{1,0:T(8,128)(2,1)S(1)}) custom-call(s32[42]{0:T(128)S(1)} %pad_add_fusion.ints_ref, bf16[2,256,768]{2,1,0:T(8,128)(2,1)S(1)} %bitcast.32), custom_call_target="tpu_custom_call" | custom-call | tf_op jit(solution)/shard_map/cut_pixels/pallas_call | solution.py:202
  45.2 2.2 %collective-permute-start.2 = (bf16[208,768]{1,0:T(8,128)(2,1)S(1)}, bf16[208,768]{1,0:T(8,128)(2,1)S(1)}, u32[]{:S(2)}, u32[]{:S(2)}) collective-permute-start(bf16[208,768]{1,0:T(8,128)(2,1)S(1)} %get-tuple-element.26), channel_id=1, source_target_pairs={{0,1},{1,2},{2,3},{3,4},{4,5},{5,6},{6,7},{7,8},{8,9},{9,10},{10,1... | collective-permute-start | bytes 958472 | tf_op jit(solution)/shard_map/ppermute | solution.py:492
  47.4 6.7 %collective-permute-start.3 = (bf16[208,768]{1,0:T(8,128)(2,1)S(1)}, bf16[208,768]{1,0:T(8,128)(2,1)}, u32[]{:S(2)}, u32[]{:S(2)}) collective-permute-start(bf16[208,768]{1,0:T(8,128)(2,1)S(1)} %get-tuple-element.28), channel_id=1, source_target_pairs={{1,0},{2,1},{3,2},{4,3},{5,4},{6,5},{7,6},{8,7},{9,8},{10,9},{11,1... | collective-permute-start | bytes 958472 | tf_op jit(solution)/shard_map/ppermute | solution.py:492
  54.1 0.1 pad.5.clone
  54.2 0.1 maximum_bitcast_fusion.param_ref
  54.3 0.6 early_norm.1.refs_0_
  54.9 0.6 collective-permute-done.1.above_ref
  55.4 0.0 collective-permute-done.below_ref
  55.4 9.9 %collective-permute-done.2.pix_below = bf16[208,768]{1,0:T(8,128)(2,1)S(1)} collective-permute-done((bf16[208,768]{1,0:T(8,128)(2,1)S(1)}, bf16[208,768]{1,0:T(8,128)(2,1)S(1)}, u32[]{:S(2)}, u32[]{:S(2)}) %collective-permute-start.2) | collective-permute-done | bytes 319520 | tf_op jit(solution)/shard_map/ppermute | solution.py:492
  65.3 0.7 copy-done.4
  66.0 0.0 collective-permute-done.3.pix_above
  66.0 0.0 all-to-all-done.1
  66.0 1.9 %collective-permute-start.4 = (bf16[64,2,16,512]{3,2,1,0:T(8,128)(2,1)S(1)}, bf16[64,2,16,512]{3,2,1,0:T(8,128)(2,1)S(1)}, u32[]{:S(2)}, u32[]{:S(2)}) collective-permute-start(bf16[64,2,16,512]{3,2,1,0:T(8,128)(2,1)S(1)} %bitcast.20), channel_id=1, source_target_pairs={{0,1},{1,0},{2,3},{3,2},{4,5},{5,4},{6,7},{7,6},{8,9},{9,8},{10,11... | collective-permute-start | bytes 6291464 | tf_op jit(solution)/shard_map/ppermute | solution.py:504
  68.0 4.1 %collective-permute-done.4.other_ref = bf16[64,2,16,512]{3,2,1,0:T(8,128)(2,1)S(1)} collective-permute-done((bf16[64,2,16,512]{3,2,1,0:T(8,128)(2,1)S(1)}, bf16[64,2,16,512]{3,2,1,0:T(8,128)(2,1)S(1)}, u32[]{:S(2)}, u32[]{:S(2)}) %collective-permute-start.4) | collective-permute-done | bytes 2097184 | tf_op jit(solution)/shard_map/ppermute | solution.py:504
  72.1 0.5 detector_block.8
  72.6 0.7 collective-permute-start.5
  73.3 0.6 detector_block.12
  73.9 0.7 collective-permute-start.8
  74.6 0.0 collective-permute-done.5.tile_ref
  74.6 0.6 detector_block.9
  75.1 1.3 collective-permute-start.6
  76.4 0.0 collective-permute-done.8.tile_ref
  76.5 0.6 detector_block.13
  77.0 1.3 collective-permute-start.9
  78.3 16.9 %collective-permute-done.6.tile_ref = bf16[256,512]{1,0:T(8,128)(2,1)S(1)} collective-permute-done((bf16[256,512]{1,0:T(8,128)(2,1)S(1)}, bf16[256,512]{1,0:T(8,128)(2,1)S(1)}, u32[]{:S(2)}, u32[]{:S(2)}) %collective-permute-start.6) | collective-permute-done | bytes 262176 | tf_op jit(solution)/shard_map/ppermute | solution.py:513
  95.2 4.8 %detector_block.10 = bf16[256,512]{1,0:T(8,128)(2,1)S(1)} custom-call(s32[42]{0:T(128)S(1)} %pad_add_fusion.ints_ref, bf16[256,512]{1,0:T(8,128)(2,1)S(1)} %collective-permute-done.6.tile_ref, f32[4,56,128]{2,1,0:T(8,128)S(1)} %maximum_bitcast_fusion.param_ref, bf16[64,2,16,512]{3,2,1,0:T(8,128)(2,1)S(1)} %bitcast.25, ...), custom_call_target="tpu_custom_call" | custom-call | tf_op jit(solution)/shard_map/detector_block/pallas_call | solution.py:165
  100.0 1.3 collective-permute-start.7
  101.3 0.0 collective-permute-done.9.tile_ref
  101.3 4.6 %detector_block.14 = bf16[256,512]{1,0:T(8,128)(2,1)S(1)} custom-call(s32[42]{0:T(128)S(1)} %pad_add_fusion.ints_ref, bf16[256,512]{1,0:T(8,128)(2,1)S(1)} %collective-permute-done.9.tile_ref, f32[4,56,128]{2,1,0:T(8,128)S(1)} %maximum_bitcast_fusion.param_ref, bf16[64,2,16,512]{3,2,1,0:T(8,128)(2,1)S(1)} %bitcast.26, ...), custom_call_target="tpu_custom_call" | custom-call | tf_op jit(solution)/shard_map/detector_block/pallas_call | solution.py:165
  106.0 1.3 collective-permute-start.10
  107.3 0.4 collective-permute-done.7.tile_ref
  107.7 0.5 detector_block.11.refs_2_
  108.3 5.4 %collective-permute-done.10.tile_ref = bf16[256,512]{1,0:T(8,128)(2,1)S(1)} collective-permute-done((bf16[256,512]{1,0:T(8,128)(2,1)S(1)}, bf16[256,512]{1,0:T(8,128)(2,1)S(1)}, u32[]{:S(2)}, u32[]{:S(2)}) %collective-permute-start.10) | collective-permute-done | bytes 262176 | tf_op jit(solution)/shard_map/ppermute | solution.py:513
  113.7 0.5 detector_block.15.refs_3_
  114.2 0.7 collective-permute-start.11
  114.9 0.7 collective-permute-start.12
  115.6 0.7 collective-permute-start.14
  116.3 0.7 collective-permute-start.13
  117.0 0.0 all-gather.3.cloned.1.call-done
  117.0 0.0 collective-permute-done.11.refs_0_
  117.0 0.0 collective-permute-done.12.refs_1_
  117.0 0.0 collective-permute-done.14.refs_5_
  117.0 0.6 pick_crops.1
  117.6 0.7 collective-permute-start.15
  118.3 0.7 collective-permute-start.16
  119.0 1.3 collective-permute-start.17
  120.3 0.0 copy-start.2
  120.3 4.8 %stage_weights.1 = (bf16[8,3584,128]{2,1,0:T(8,128)(2,1)S(1)}, f32[208,1024]{1,0:T(8,128)S(1)}) custom-call(s32[42]{0:T(128)S(1)} %pad_add_fusion.ints_ref, bf16[208,768]{1,0:T(8,128)(2,1)} %copy-done.4, bf16[208,768]{1,0:T(8,128)(2,1)} %copy-done.1, bf16[208,768]{1,0:T(8,128)(2,1)} %collective-permute-done.3.pix_above, bf16[8,3584,128]{2,1,0:T(8,128)(2,1)} %bitcast.33), custom_call_target="tpu_custom_call" | custom-call | tf_op jit(solution)/shard_map/stage_weights/pallas_call | solution.py:343
  125.0 0.0 collective-permute-done.15.refs_0_
  125.1 27.8 %collective-permute-done.17.refs_2_ = bf16[208,512]{1,0:T(8,128)(2,1)S(1)} collective-permute-done((bf16[208,512]{1,0:T(8,128)(2,1)S(1)}, bf16[208,512]{1,0:T(8,128)(2,1)S(1)}, u32[]{:S(2)}, u32[]{:S(2)}) %collective-permute-start.17) | collective-permute-done | bytes 213024 | tf_op jit(solution)/shard_map/ppermute | solution.py:521
  152.9 4.7 %classify.1 = f32[1,1024]{1,0:T(1,128)} custom-call(s32[42]{0:T(128)S(1)} %pad_add_fusion.ints_ref, bf16[208,512]{1,0:T(8,128)(2,1)S(1)} %collective-permute-done.15.refs_0_, bf16[208,512]{1,0:T(8,128)(2,1)S(1)} %collective-permute-done.16.refs_1_, bf16[208,512]{1,0:T(8,128)(2,1)S(1)} %collective-permute-done.17.refs_2_, ...), custom_call_target="tpu_custom_call" | custom-call | tf_op jit(solution)/shard_map/classify/pallas_call | solution.py:441
  (27 shorter events, 0.1 us)
Async XLA Ops:
  6.5 2.2 %copy-start.6 = (bf16[1,16,512]{2,1,0:T(8,128)(2,1)S(1)}, bf16[1,16,512]{2,1,0:T(8,128)(2,1)}, u32[]{:S(2)}) copy-start(bf16[1,16,512]{2,1,0:T(8,128)(2,1)} %param.20) | copy-start | bytes 49156
  6.5 2.2 %copy-start.7 = (bf16[1,512,16]{1,2,0:T(8,128)(2,1)S(1)}, bf16[1,512,16]{1,2,0:T(8,128)(2,1)}, u32[]{:S(2)}) copy-start(bf16[1,512,16]{1,2,0:T(8,128)(2,1)} %param.19) | copy-start | bytes 49156
  6.5 110.4 %all-gather.3.cloned.1.call-start = ((), (), s32[]{:S(2)}) async-start(), calls=%async_computation.2 | async-start | bytes 8257536 | tf_op jit(solution)/shard_map/all_gather | solution.py:486
  31.1 7.4 %copy-start.8 = (s32[1,4,3,3]{1,0,3,2:T(1,128)S(1)}, s32[1,4,3,3]{1,0,3,2:T(1,128)}, u32[]{:S(2)}) copy-start(s32[1,4,3,3]{1,0,3,2:T(1,128)} %param.28) | copy-start | bytes 436
  31.1 7.6 %copy-start.11 = (s32[1,4]{1,0:T(1,128)S(1)}, s32[1,4]{1,0:T(1,128)}, u32[]{:S(2)}) copy-start(s32[1,4]{1,0:T(1,128)} %param.29) | copy-start | bytes 52
  31.1 12.0 %copy-start = (bf16[2,16,16,768]{3,2,1,0:T(8,128)(2,1)S(1)}, bf16[2,16,16,768]{3,2,1,0:T(8,128)(2,1)}, u32[]{:S(2)}) copy-start(bf16[2,16,16,768]{3,2,1,0:T(8,128)(2,1)} %param.16) | copy-start | bytes 2359300
  31.1 23.0 %copy-start.5 = (f32[1,7,7,512]{3,0,2,1:T(1,128)S(1)}, f32[1,7,7,512]{3,0,2,1:T(1,128)}, u32[]{:S(2)}) copy-start(f32[1,7,7,512]{3,0,2,1:T(1,128)} %param.17) | copy-start | bytes 301060
  31.1 23.1 %copy-start.9 = (f32[1,512]{1,0:T(1,128)S(1)}, f32[1,512]{1,0:T(1,128)}, u32[]{:S(2)}) copy-start(f32[1,512]{1,0:T(1,128)} %param.21) | copy-start | bytes 6148
  31.1 23.1 %copy-start.10 = (f32[1,512]{1,0:T(1,128)S(1)}, f32[1,512]{1,0:T(1,128)}, u32[]{:S(2)}) copy-start(f32[1,512]{1,0:T(1,128)} %param.18) | copy-start | bytes 6148
  31.1 23.1 %copy-start.3 = (bf16[2,16,16,512]{3,2,1,0:T(8,128)(2,1)S(1)}, bf16[2,16,16,512]{3,2,1,0:T(8,128)(2,1)}, u32[]{:S(2)}) copy-start(bf16[2,16,16,512]{3,2,1,0:T(8,128)(2,1)} %param.15) | copy-start | bytes 1572868
  31.1 34.9 %all-to-all-start.1 = ((bf16[8,8,2,16,512]{4,3,2,1,0:T(8,128)(2,1)}), bf16[8,8,2,16,512]{4,3,2,1,0:T(8,128)(2,1)S(1)}, u32[]{:S(2)}, u32[]{:S(2)}) async-start(bf16[8,8,2,16,512]{4,3,2,1,0:T(8,128)(2,1)} %broadcast_in_dim.20), calls=%async_computation.1 | async-start | bytes 4194304 | tf_op jit(solution)/shard_map/all_to_all | solution.py:43
  38.8 16.6 %collective-permute-start.1 = (s32[42]{0:T(128)S(1)}, s32[42]{0:T(128)S(1)}, u32[]{:S(2)}, u32[]{:S(2)}) collective-permute-start(s32[42]{0:T(128)S(1)} %pad_add_fusion.ints_ref), channel_id=1, source_target_pairs={{1,0},{2,1},{3,2},{4,3},{5,4},{6,5},{7,6},{8,7},{9,8},{10,9},{11,1... | collective-permute-start | bytes 512 | tf_op jit(solution)/shard_map/ppermute | solution.py:494
  40.7 14.7 %collective-permute-start = (s32[42]{0:T(128)S(1)}, s32[42]{0:T(128)S(1)}, u32[]{:S(2)}, u32[]{:S(2)}) collective-permute-start(s32[42]{0:T(128)S(1)} %pad_add_fusion.ints_ref), channel_id=1, source_target_pairs={{0,1},{1,2},{2,3},{3,4},{4,5},{5,6},{6,7},{7,8},{8,9},{9,10},{10,1... | collective-permute-start | bytes 512 | tf_op jit(solution)/shard_map/ppermute | solution.py:493
  45.1 20.2 %copy-start.1 = (bf16[208,768]{1,0:T(8,128)(2,1)}, bf16[208,768]{1,0:T(8,128)(2,1)S(1)}, u32[]{:S(2)}) copy-start(bf16[208,768]{1,0:T(8,128)(2,1)S(1)} %get-tuple-element.27.pix_own) | copy-start | bytes 958468
  45.2 20.1 %collective-permute-start.2 = (bf16[208,768]{1,0:T(8,128)(2,1)S(1)}, bf16[208,768]{1,0:T(8,128)(2,1)S(1)}, u32[]{:S(2)}, u32[]{:S(2)}) collective-permute-start(bf16[208,768]{1,0:T(8,128)(2,1)S(1)} %get-tuple-element.26), channel_id=1, source_target_pairs={{0,1},{1,2},{2,3},{3,4},{4,5},{5,6},{6,7},{7,8},{8,9},{9,10},{10,1... | collective-permute-start | bytes 958472 | tf_op jit(solution)/shard_map/ppermute | solution.py:492
  47.4 18.7 %collective-permute-start.3 = (bf16[208,768]{1,0:T(8,128)(2,1)S(1)}, bf16[208,768]{1,0:T(8,128)(2,1)}, u32[]{:S(2)}, u32[]{:S(2)}) collective-permute-start(bf16[208,768]{1,0:T(8,128)(2,1)S(1)} %get-tuple-element.28), channel_id=1, source_target_pairs={{1,0},{2,1},{3,2},{4,3},{5,4},{6,5},{7,6},{8,7},{9,8},{10,9},{11,1... | collective-permute-start | bytes 958472 | tf_op jit(solution)/shard_map/ppermute | solution.py:492
  65.3 0.7 copy-start.4
  66.0 6.0 %collective-permute-start.4 = (bf16[64,2,16,512]{3,2,1,0:T(8,128)(2,1)S(1)}, bf16[64,2,16,512]{3,2,1,0:T(8,128)(2,1)S(1)}, u32[]{:S(2)}, u32[]{:S(2)}) collective-permute-start(bf16[64,2,16,512]{3,2,1,0:T(8,128)(2,1)S(1)} %bitcast.20), channel_id=1, source_target_pairs={{0,1},{1,0},{2,3},{3,2},{4,5},{5,4},{6,7},{7,6},{8,9},{9,8},{10,11... | collective-permute-start | bytes 6291464 | tf_op jit(solution)/shard_map/ppermute | solution.py:504
  72.6 1.9 %collective-permute-start.5 = (bf16[256,512]{1,0:T(8,128)(2,1)S(1)}, bf16[256,512]{1,0:T(8,128)(2,1)S(1)}, u32[]{:S(2)}, u32[]{:S(2)}) collective-permute-start(bf16[256,512]{1,0:T(8,128)(2,1)S(1)} %detector_block.8), channel_id=1, source_target_pairs={{0,128},{1,129},{2,130},{3,131},{4,132},{5,133},{6,134},{7,135},{8... | collective-permute-start | bytes 786440 | tf_op jit(solution)/shard_map/ppermute | solution.py:513
  73.9 2.6 %collective-permute-start.8 = (bf16[256,512]{1,0:T(8,128)(2,1)S(1)}, bf16[256,512]{1,0:T(8,128)(2,1)S(1)}, u32[]{:S(2)}, u32[]{:S(2)}) collective-permute-start(bf16[256,512]{1,0:T(8,128)(2,1)S(1)} %detector_block.12), channel_id=1, source_target_pairs={{0,128},{1,129},{2,130},{3,131},{4,132},{5,133},{6,134},{7,135},{8... | collective-permute-start | bytes 786440 | tf_op jit(solution)/shard_map/ppermute | solution.py:513
  75.1 20.1 %collective-permute-start.6 = (bf16[256,512]{1,0:T(8,128)(2,1)S(1)}, bf16[256,512]{1,0:T(8,128)(2,1)S(1)}, u32[]{:S(2)}, u32[]{:S(2)}) collective-permute-start(bf16[256,512]{1,0:T(8,128)(2,1)S(1)} %detector_block.9), channel_id=1, source_target_pairs={{128,256},{129,257},{130,258},{131,259},{132,260},{133,261},{134,2... | collective-permute-start | bytes 786440 | tf_op jit(solution)/shard_map/ppermute | solution.py:513
  77.0 24.3 %collective-permute-start.9 = (bf16[256,512]{1,0:T(8,128)(2,1)S(1)}, bf16[256,512]{1,0:T(8,128)(2,1)S(1)}, u32[]{:S(2)}, u32[]{:S(2)}) collective-permute-start(bf16[256,512]{1,0:T(8,128)(2,1)S(1)} %detector_block.13), channel_id=1, source_target_pairs={{128,256},{129,257},{130,258},{131,259},{132,260},{133,261},{134,2... | collective-permute-start | bytes 786440 | tf_op jit(solution)/shard_map/ppermute | solution.py:513
  100.0 7.7 %collective-permute-start.7 = (bf16[256,512]{1,0:T(8,128)(2,1)S(1)}, bf16[256,512]{1,0:T(8,128)(2,1)S(1)}, u32[]{:S(2)}, u32[]{:S(2)}) collective-permute-start(bf16[256,512]{1,0:T(8,128)(2,1)S(1)} %detector_block.10), channel_id=1, source_target_pairs={{256,384},{257,385},{258,386},{259,387},{260,388},{261,389},{262,3... | collective-permute-start | bytes 786440 | tf_op jit(solution)/shard_map/ppermute | solution.py:513
  106.0 7.7 %collective-permute-start.10 = (bf16[256,512]{1,0:T(8,128)(2,1)S(1)}, bf16[256,512]{1,0:T(8,128)(2,1)S(1)}, u32[]{:S(2)}, u32[]{:S(2)}) collective-permute-start(bf16[256,512]{1,0:T(8,128)(2,1)S(1)} %detector_block.14), channel_id=1, source_target_pairs={{256,384},{257,385},{258,386},{259,387},{260,388},{261,389},{262,3... | collective-permute-start | bytes 786440 | tf_op jit(solution)/shard_map/ppermute | solution.py:513
  114.2 2.8 %collective-permute-start.11 = (bf16[256,512]{1,0:T(8,128)(2,1)S(1)}, bf16[256,512]{1,0:T(8,128)(2,1)S(1)}, u32[]{:S(2)}, u32[]{:S(2)}) collective-permute-start(bf16[256,512]{1,0:T(8,128)(2,1)S(1)} %detector_block.11.refs_2_), channel_id=1, source_target_pairs={{384,385},{385,384},{386,387},{387,386},{388,389},{389,388},{390,3... | collective-permute-start | bytes 786440 | tf_op jit(solution)/shard_map/ppermute | solution.py:519
  114.9 2.1 %collective-permute-start.12 = (bf16[256,512]{1,0:T(8,128)(2,1)S(1)}, bf16[256,512]{1,0:T(8,128)(2,1)S(1)}, u32[]{:S(2)}, u32[]{:S(2)}) collective-permute-start(bf16[256,512]{1,0:T(8,128)(2,1)S(1)} %detector_block.15.refs_3_), channel_id=1, source_target_pairs={{384,385},{385,384},{386,387},{387,386},{388,389},{389,388},{390,3... | collective-permute-start | bytes 786440 | tf_op jit(solution)/shard_map/ppermute | solution.py:519
  115.6 1.4 collective-permute-start.14
  116.3 0.7 collective-permute-start.13
  117.6 7.4 %collective-permute-start.15 = (bf16[208,512]{1,0:T(8,128)(2,1)S(1)}, bf16[208,512]{1,0:T(8,128)(2,1)S(1)}, u32[]{:S(2)}, u32[]{:S(2)}) collective-permute-start(bf16[208,512]{1,0:T(8,128)(2,1)S(1)} %get-tuple-element.36), channel_id=1, source_target_pairs={{384,0},{385,1},{386,2},{387,3},{388,4},{389,5},{390,6},{391,7},{3... | collective-permute-start | bytes 638984 | tf_op jit(solution)/shard_map/ppermute | solution.py:521
  118.3 6.8 %collective-permute-start.16 = (bf16[208,512]{1,0:T(8,128)(2,1)S(1)}, bf16[208,512]{1,0:T(8,128)(2,1)S(1)}, u32[]{:S(2)}, u32[]{:S(2)}) collective-permute-start(bf16[208,512]{1,0:T(8,128)(2,1)S(1)} %get-tuple-element.37), channel_id=1, source_target_pairs={{384,128},{385,129},{386,130},{387,131},{388,132},{389,133},{390,1... | collective-permute-start | bytes 638984 | tf_op jit(solution)/shard_map/ppermute | solution.py:521
  119.0 33.9 %collective-permute-start.17 = (bf16[208,512]{1,0:T(8,128)(2,1)S(1)}, bf16[208,512]{1,0:T(8,128)(2,1)S(1)}, u32[]{:S(2)}, u32[]{:S(2)}) collective-permute-start(bf16[208,512]{1,0:T(8,128)(2,1)S(1)} %get-tuple-element.38), channel_id=1, source_target_pairs={{384,256},{385,257},{386,258},{387,259},{388,260},{389,261},{390,2... | collective-permute-start | bytes 638984 | tf_op jit(solution)/shard_map/ppermute | solution.py:521
  120.3 32.6 %copy-start.2 = (f32[2,1024]{1,0:T(2,128)S(1)}, f32[2,1024]{1,0:T(2,128)}, u32[]{:S(2)}) copy-start(f32[2,1024]{1,0:T(2,128)} %refs_6_.1) | copy-start | bytes 24580
Sparse Core Ops, SparseCore 0:
  9.5 53.7 all-gather.2

commit v5 on v4

--- a/solution.py
+++ b/solution.py
@@ -38,13 +38,13 @@
     return along_z + along_y
 
 
+def resident(array):
+    return pltpu.with_memory_space_constraint(array, pltpu.VMEM)
+
+
 def spread_in_groups(block, groups):
     copies = jnp.broadcast_to(block[None], (SIDE,) + block.shape)
     return lax.all_to_all(copies, REP, 0, 0, axis_index_groups=groups)
-
-
-def resident(array):
-    return pltpu.with_memory_space_constraint(array, pltpu.VMEM)
 
 
 def in_hbm(array):
@@ -96,7 +96,7 @@
 
 
 def early_body(ints_ref, tile_ref, param_ref, normed_ref, wide, conv):
-    @pl.when(active(ints_ref, 0) & (ints_ref[CORE_AT] == 0))
+    @pl.when(active(ints_ref, 0))
     def _():
         conv_norm(tile_ref, param_ref, normed_ref, wide, conv)
 
@@ -122,55 +122,70 @@
     )(ints, resident(tile), resident(params))
 
 
+def mlp(normed_ref, own_ref, other_ref, tile_ref, param_ref, out_ref):
+    width = tile_ref.shape[1]
+    slabs = width // LANES
+    rows = normed_ref[...]
+    update = None
+    step = 64
+    for ref in (own_ref, other_ref):
+        for chunk in range(0, ref.shape[0], step):
+            into = ref[pl.ds(chunk, step), 0].reshape(step * 16, width)
+            outof = ref[pl.ds(chunk, step), 1].reshape(step * 16, width)
+            hidden = lax.dot_general(
+                rows, into, (((1,), (1,)), ((), ())), preferred_element_type=jnp.float32
+            )
+            hidden = jax.nn.gelu(hidden, approximate=True).astype(jnp.bfloat16)
+            term = jnp.dot(hidden, outof, preferred_element_type=jnp.float32)
+            update = term if update is None else update + term
+    for slab in range(slabs):
+        part = slice(slab * LANES, (slab + 1) * LANES)
+        out_ref[:, part] = (
+            tile_ref[:, part].astype(jnp.float32) + param_ref[slab, pl.ds(50, 1), :] * update[:, part]
+        ).astype(jnp.bfloat16)
+
+
+def early_block_body(ints_ref, tile_ref, param_ref, own_ref, other_ref, normed_ref, out_ref):
+    @pl.when(active(ints_ref, 0))
+    def _():
+        mlp(normed_ref, own_ref, other_ref, tile_ref, param_ref, out_ref)
+
+
 def block_body(ints_ref, tile_ref, param_ref, own_ref, other_ref, *refs, number):
-    early_refs, (out_ref, normed, wide, conv) = refs[:-4], refs[-4:]
+    before, (out_ref, normed, wide, conv) = refs[:-4], refs[-4:]
 
     @pl.when(active(ints_ref, number))
     def _():
-        if early_refs:
-
-            @pl.when(ints_ref[CORE_AT] == 0)
-            def _():
-                normed[...] = early_refs[0][...]
-
-            @pl.when(ints_ref[CORE_AT] == 1)
-            def _():
-                conv_norm(tile_ref, param_ref, normed, wide, conv)
-
-        else:
-            conv_norm(tile_ref, param_ref, normed, wide, conv)
-        slabs = wide.shape[0]
-        width = slabs * LANES
-        rows = normed[...]
-        update = None
-        step = 32
-        for ref in (own_ref, other_ref):
-            for chunk in range(0, ref.shape[0], step):
-                into = ref[pl.ds(chunk, step), 0].reshape(step * 16, width)
-                outof = ref[pl.ds(chunk, step), 1].reshape(step * 16, width)
-                hidden = lax.dot_general(
-                    rows, into, (((1,), (1,)), ((), ())), preferred_element_type=jnp.float32
-                )
-                hidden = jax.nn.gelu(hidden, approximate=True).astype(jnp.bfloat16)
-                term = jnp.dot(hidden, outof, preferred_element_type=jnp.float32)
-                update = term if update is None else update + term
-        for slab in range(slabs):
-            part = slice(slab * LANES, (slab + 1) * LANES)
-            out_ref[:, part] = (
-                tile_ref[:, part].astype(jnp.float32) + param_ref[slab, pl.ds(50, 1), :] * update[:, part]
-            ).astype(jnp.bfloat16)
-
-
-def detector_block(number, ints, tile, params, own, other, *early):
+        conv_norm(tile_ref, param_ref, normed, wide, conv)
+        result_ref = out_ref
+        if before:
+            out_ref[0] = before[0][...]
+            result_ref = out_ref.at[1]
+        mlp(normed, own_ref, other_ref, tile_ref, param_ref, result_ref)
+
+
+def early_block(ints, tile, params, own, other, normed):
+    return pl.pallas_call(
+        early_block_body,
+        out_shape=pltpu.VMEM(tile.shape, jnp.bfloat16),
+        in_specs=[SMEM] + [VMEM] * 5,
+        out_specs=VMEM,
+        compiler_params=LIMITED,
+        name="early_block",
+    )(ints, *map(resident, (tile, params, own, other, normed)))
+
+
+def detector_block(number, ints, tile, params, own, other, *before):
+    shape = (2,) + tile.shape if before else tile.shape
     return pl.pallas_call(
         functools.partial(block_body, number=number),
-        out_shape=pltpu.VMEM(tile.shape, jnp.bfloat16),
-        in_specs=[SMEM] + [VMEM] * (4 + len(early)),
+        out_shape=pltpu.VMEM(shape, jnp.bfloat16),
+        in_specs=[SMEM] + [VMEM] * (4 + len(before)),
         out_specs=VMEM,
         scratch_shapes=[pltpu.VMEM(tile.shape, jnp.bfloat16)] + conv_scratch(tile),
         compiler_params=LIMITED,
         name="detector_block",
-    )(ints, *map(resident, (tile, params, own, other, *early)))
+    )(ints, *map(resident, (tile, params, own, other, *before)))
 
 
 def selection(top, left):
@@ -211,7 +226,7 @@
 
 
 def pick_body(ints_ref, below_ref, above_ref, *refs):
-    tiles, out_refs = refs[:6], refs[6:]
+    pairs, out_refs = refs[:3], refs[3:]
 
     @pl.when(active(ints_ref, len(out_refs) - 1))
     def _():
@@ -228,25 +243,24 @@
             away = (source == 1) | (source == 3)
             micro = entry(0)
             chosen = selection(entry(1), entry(2))
-            for number, wanted in enumerate((same_chip, ~away, away & ~same_chip)):
-                for index in range(2):
-
-                    @pl.when(wanted & (micro == index))
-                    def _(chosen=chosen, tile=tiles[2 * number + index], out_ref=out_ref):
-                        rows = jnp.dot(chosen, tile[...], preferred_element_type=jnp.float32)
-                        out_ref[...] = rows.astype(jnp.bfloat16)
-
-
-def pick_crops(ints, below, above, tiles, slots):
-    width = tiles[0].shape[1]
+            for pair, wanted in zip(pairs, (same_chip, ~away, away & ~same_chip)):
+
+                @pl.when(wanted)
+                def _(chosen=chosen, pair=pair, micro=micro, out_ref=out_ref):
+                    rows = jnp.dot(chosen, pair[micro], preferred_element_type=jnp.float32)
+                    out_ref[...] = rows.astype(jnp.bfloat16)
+
+
+def pick_crops(ints, below, above, pairs, slots):
+    width = pairs[0].shape[2]
     return pl.pallas_call(
         pick_body,
         out_shape=[pltpu.VMEM((PADDED, width), jnp.bfloat16)] * slots,
-        in_specs=[SMEM] * 3 + [VMEM] * len(tiles),
+        in_specs=[SMEM] * 3 + [VMEM] * len(pairs),
         out_specs=[VMEM] * slots,
         compiler_params=LIMITED,
         name="pick_crops",
-    )(ints, below, above, *map(resident, tiles))
+    )(ints, below, above, *map(resident, pairs))
 
 
 EMBED, MERGE, QUERY = 0, 1536, 2560
@@ -408,8 +422,9 @@
             scores = jnp.where(key_ok, scores, -jnp.inf)
             top = jnp.max(scores, axis=-1, keepdims=True)
             numer = jnp.exp(scores - top)
-            probs = (numer * (1.0 / jnp.sum(numer, axis=-1, keepdims=True))).astype(jnp.bfloat16)
-            contexts.append(jnp.dot(probs, value, preferred_element_type=jnp.float32))
+            share = 1.0 / jnp.sum(numer, axis=-1, keepdims=True)
+            summed = jnp.dot(numer.astype(jnp.bfloat16), value, preferred_element_type=jnp.float32)
+            contexts.append(summed * share)
         context = jnp.where(lane < HEAD_DIM, contexts[0], contexts[1]).astype(jnp.bfloat16)
         context = jnp.where(row_ok, context.astype(jnp.float32), 0.0)
         context_sums.append(jnp.sum(context, axis=0, keepdims=True))
@@ -504,20 +519,21 @@
     other = lax.ppermute(own, REP, swap)
 
     for number in range(sections):
-        ahead = [(early,), ()] if number == 0 else [(), ()]
-        done = []
-        for tile, more in zip(tiles, ahead):
-            order = after(ints, *done)
-            done.append(detector_block(number, order, tile, params, own, other, *more))
+        if number == 0:
+            first = early_block(ints, tiles[0], params, own, other, early)
+        else:
+            first = detector_block(number, ints, tiles[0], params, own, other)
+        before = (first,) if number == last else ()
+        second = detector_block(number, after(ints, first), tiles[1], params, own, other, *before)
         if number < last:
-            tiles = [lax.ppermute(tile, "section", [(number, number + 1)]) for tile in done]
+            tiles = [lax.ppermute(tile, "section", [(number, number + 1)]) for tile in (first, second)]
 
     within = [(last * count + origin, last * count + target) for origin, target in swap]
     across = [(last * count + index, last * count + index + 1) for index in range(1, count - 1, 2)]
     across += [(target, origin) for origin, target in across]
-    far = [lax.ppermute(tile, ("section",) + REP, across) for tile in done]
-    near = [lax.ppermute(tile, ("section",) + REP, within) for tile in lax.optimization_barrier(tuple(done))]
-    crops = pick_crops(after(ints, weights), below, above, near + done + far, sections)
+    far = lax.ppermute(second, ("section",) + REP, across)
+    near = lax.ppermute(second, ("section",) + REP, within)
+    crops = pick_crops(after(ints, weights), below, above, (near, second, far), sections)
     feats = [lax.ppermute(crops[slot], "section", [(last, slot)]) for slot in range(last)] + [crops[last]]
     weights, base = staged(after(ints, *crops), pixels, weights)
     result = classify(ints, feats, base, weights, cls_gain)

time: 165 us -> 157 us (0.952)
  the two profiles are of different devices: /device:TPU:36 before, /device:TPU:12 now
where the time goes in v5:
time: 157 us; the launch traced here: 156 us
  waiting for transfers between devices  59 us (38%)
  starting transfers between devices  32.2 us (21%)
  Pallas kernels  27.4 us (17%)
  blocking collectives  20.6 us (13%)
  between operations  13.8 us (9%)
  local copies, waits for them, and re-layouts  2.79 us (2%)
    ppermute x3, waiting for transfers between devices, per_device(): lax.ppermute(crops[slot], 'section', [(last, slot)])  20.9 us
    ppermute x6, waiting for transfers between devices, per_device(): lax.ppermute(tile, 'section', [(number, number + 1)])  20.9 us
    all_to_all x1, blocking collectives, spread_in_groups(): return lax.all_to_all(copies, REP, 0, 0, axis_index_groups=groups)  20.6 us
    pallas_call x7, Pallas kernels, detector_block(): pl.pallas_call(functools.partial(block_body, number=number), out_shape=pl...  12.2 us
    ppermute x1, waiting for transfers between devices, per_device(): above = lax.ppermute(ints, REP, downward)  8.75 us
    all_to_all x1, starting transfers between devices, spread_in_groups(): return lax.all_to_all(copies, REP, 0, 0, axis_index_groups=groups)  7.69 us
    ppermute x6, starting transfers between devices, per_device(): lax.ppermute(tile, 'section', [(number, number + 1)])  6.55 us
    ppermute x1, starting transfers between devices, per_device(): lax.ppermute(cut[0], REP, downward)  5.44 us
  transfers between devices with their start and end apart: 18, of which 7 were waited for; matrix products, arithmetic and copies ran while one was open for 1% of the time, Pallas kernels for 13%

profile of v5, /device:TPU:12, one launch (start us, length us, event | category | flops | bytes accessed | tf_op | source)
XLA Modules:
  0.0 156.0 jit_solution(6453490553752498688)
XLA Ops:
  6.5 2.2 %pack_weights.1 = bf16[3584,128]{1,0:T(8,128)(2,1)} custom-call(s32[1]{0:T(128)} %bitcast.2.parity_ref, bf16[768,256]{1,0:T(8,128)(2,1)} %embed.1, bf16[512,256]{1,0:T(8,128)(2,1)} %merge.1, bf16[196,256]{1,0:T(8,128)(2,1)} %pos.1, bf16[3,1024,128]{2,1,0:T(8,128)(2,1)} %bitcast.34, bf16[128,1024]{1,0:T(8,128)(2,1)} %out.1), custom_call_target="tpu_custom_call" | custom-call | tf_op jit(solution)/shard_map/pack_weights/pallas_call | solution.py:304
  8.7 0.0 all-gather.3.cloned.1.call-update
  8.8 20.6 %all_to_all.10 = bf16[8,2,16,512]{3,2,1,0:T(8,128)(2,1)S(1)} all-to-all(bf16[8,2,16,512]{3,2,1,0:T(8,128)(2,1)S(1)} %broadcast_in_dim.9), channel_id=1, replica_groups={{0,2,4,6,8,10,12,14},{16,18,20,22,24,26,28,30},{32,34,36,38,40,42,44,46..., dimensions={0} | all-to-all | bytes 524288 | tf_op jit(solution)/shard_map/all_to_all | solution.py:47
  29.4 1.7 %broadcast_in_dim.20 = bf16[8,8,2,16,512]{4,3,2,1,0:T(8,128)(2,1)} broadcast(bf16[8,2,16,512]{3,2,1,0:T(8,128)(2,1)S(1)} %all_to_all.10), dimensions={1,2,3,4} | broadcast | bytes 2359296 | tf_op jit(solution)/shard_map/broadcast_in_dim | solution.py:46
  31.1 0.0 copy-start.9
  31.1 0.0 copy-start.10
  31.1 0.0 copy-start.3
  31.1 7.7 %all-to-all-start.1 = ((bf16[8,8,2,16,512]{4,3,2,1,0:T(8,128)(2,1)}), bf16[8,8,2,16,512]{4,3,2,1,0:T(8,128)(2,1)S(1)}, u32[]{:S(2)}, u32[]{:S(2)}) async-start(bf16[8,8,2,16,512]{4,3,2,1,0:T(8,128)(2,1)} %broadcast_in_dim.20), calls=%async_computation.1 | async-start | bytes 4194304 | tf_op jit(solution)/shard_map/all_to_all | solution.py:47
  38.8 0.0 copy-done.8
  38.8 0.1 copy.17
  38.9 0.1 reshape.32
  39.1 0.1 pad_add_fusion.ints_ref
  39.1 2.1 %collective-permute-start.1 = (s32[42]{0:T(128)S(1)}, s32[42]{0:T(128)S(1)}, u32[]{:S(2)}, u32[]{:S(2)}) collective-permute-start(s32[42]{0:T(128)S(1)} %pad_add_fusion.ints_ref), channel_id=1, source_target_pairs={{1,0},{2,1},{3,2},{4,3},{5,4},{6,5},{7,6},{8,7},{9,8},{10,9},{11,1... | collective-permute-start | bytes 512 | tf_op jit(solution)/shard_map/ppermute | solution.py:509
  41.2 2.2 %collective-permute-start = (s32[42]{0:T(128)S(1)}, s32[42]{0:T(128)S(1)}, u32[]{:S(2)}, u32[]{:S(2)}) collective-permute-start(s32[42]{0:T(128)S(1)} %pad_add_fusion.ints_ref), channel_id=1, source_target_pairs={{0,1},{1,2},{2,3},{3,4},{4,5},{5,6},{6,7},{7,8},{8,9},{9,10},{10,1... | collective-permute-start | bytes 512 | tf_op jit(solution)/shard_map/ppermute | solution.py:508
  43.5 2.0 %cut_pixels.1 = (bf16[208,768]{1,0:T(8,128)(2,1)S(1)}, bf16[208,768]{1,0:T(8,128)(2,1)S(1)}, bf16[208,768]{1,0:T(8,128)(2,1)S(1)}) custom-call(s32[42]{0:T(128)S(1)} %pad_add_fusion.ints_ref, bf16[2,256,768]{2,1,0:T(8,128)(2,1)S(1)} %bitcast.32), custom_call_target="tpu_custom_call" | custom-call | tf_op jit(solution)/shard_map/cut_pixels/pallas_call | solution.py:217
  45.5 2.2 %collective-permute-start.2 = (bf16[208,768]{1,0:T(8,128)(2,1)S(1)}, bf16[208,768]{1,0:T(8,128)(2,1)S(1)}, u32[]{:S(2)}, u32[]{:S(2)}) collective-permute-start(bf16[208,768]{1,0:T(8,128)(2,1)S(1)} %get-tuple-element.24), channel_id=1, source_target_pairs={{0,1},{1,2},{2,3},{3,4},{4,5},{5,6},{6,7},{7,8},{8,9},{9,10},{10,1... | collective-permute-start | bytes 958472 | tf_op jit(solution)/shard_map/ppermute | solution.py:507
  47.7 5.4 %collective-permute-start.3 = (bf16[208,768]{1,0:T(8,128)(2,1)S(1)}, bf16[208,768]{1,0:T(8,128)(2,1)}, u32[]{:S(2)}, u32[]{:S(2)}) collective-permute-start(bf16[208,768]{1,0:T(8,128)(2,1)S(1)} %get-tuple-element.26), channel_id=1, source_target_pairs={{1,0},{2,1},{3,2},{4,3},{5,4},{6,5},{7,6},{8,7},{9,8},{10,9},{11,1... | collective-permute-start | bytes 958472 | tf_op jit(solution)/shard_map/ppermute | solution.py:507
  53.2 0.1 pad.5.clone
  53.3 0.1 maximum_bitcast_fusion.param_ref
  53.4 0.5 early_norm.1.normed_ref
  54.0 8.8 %collective-permute-done.1.above_ref = s32[42]{0:T(128)S(1)} collective-permute-done((s32[42]{0:T(128)S(1)}, s32[42]{0:T(128)S(1)}, u32[]{:S(2)}, u32[]{:S(2)}) %collective-permute-start.1) | collective-permute-done | bytes 200 | tf_op jit(solution)/shard_map/ppermute | solution.py:509
  62.7 0.0 collective-permute-done.below_ref
  62.7 0.0 collective-permute-done.2.pix_below
  62.7 0.0 copy-done.1
  62.8 0.7 copy-done.4
  63.5 3.1 %collective-permute-done.3.pix_above = bf16[208,768]{1,0:T(8,128)(2,1)} collective-permute-done((bf16[208,768]{1,0:T(8,128)(2,1)S(1)}, bf16[208,768]{1,0:T(8,128)(2,1)}, u32[]{:S(2)}, u32[]{:S(2)}) %collective-permute-start.3) | collective-permute-done | bytes 319520 | tf_op jit(solution)/shard_map/ppermute | solution.py:507
  66.6 1.2 all-to-all-done.1
  67.8 1.9 %collective-permute-start.4 = (bf16[64,2,16,512]{3,2,1,0:T(8,128)(2,1)S(1)}, bf16[64,2,16,512]{3,2,1,0:T(8,128)(2,1)S(1)}, u32[]{:S(2)}, u32[]{:S(2)}) collective-permute-start(bf16[64,2,16,512]{3,2,1,0:T(8,128)(2,1)S(1)} %bitcast.20), channel_id=1, source_target_pairs={{0,1},{1,0},{2,3},{3,2},{4,5},{5,4},{6,7},{7,6},{8,9},{9,8},{10,11... | collective-permute-start | bytes 6291464 | tf_op jit(solution)/shard_map/ppermute | solution.py:519
  69.7 4.1 %collective-permute-done.4.other_ref = bf16[64,2,16,512]{3,2,1,0:T(8,128)(2,1)S(1)} collective-permute-done((bf16[64,2,16,512]{3,2,1,0:T(8,128)(2,1)S(1)}, bf16[64,2,16,512]{3,2,1,0:T(8,128)(2,1)S(1)}, u32[]{:S(2)}, u32[]{:S(2)}) %collective-permute-start.4) | collective-permute-done | bytes 2097184 | tf_op jit(solution)/shard_map/ppermute | solution.py:519
  73.8 0.5 early_block.1
  74.4 0.7 collective-permute-start.5
  75.0 0.6 detector_block.10
  75.6 0.7 collective-permute-start.8
  76.3 0.0 collective-permute-done.5.tile_ref
  76.3 0.6 detector_block.7
  76.9 1.3 collective-permute-start.6
  78.2 0.0 collective-permute-done.8.tile_ref
  78.2 0.6 detector_block.11
  78.7 1.3 collective-permute-start.9
  80.0 16.8 %collective-permute-done.6.tile_ref = bf16[256,512]{1,0:T(8,128)(2,1)S(1)} collective-permute-done((bf16[256,512]{1,0:T(8,128)(2,1)S(1)}, bf16[256,512]{1,0:T(8,128)(2,1)S(1)}, u32[]{:S(2)}, u32[]{:S(2)}) %collective-permute-start.6) | collective-permute-done | bytes 262176 | tf_op jit(solution)/shard_map/ppermute | solution.py:529
  96.8 4.8 %detector_block.8 = bf16[256,512]{1,0:T(8,128)(2,1)S(1)} custom-call(s32[42]{0:T(128)S(1)} %pad_add_fusion.ints_ref, bf16[256,512]{1,0:T(8,128)(2,1)S(1)} %collective-permute-done.6.tile_ref, f32[4,56,128]{2,1,0:T(8,128)S(1)} %maximum_bitcast_fusion.param_ref, bf16[64,2,16,512]{3,2,1,0:T(8,128)(2,1)S(1)} %bitcast.25, ...), custom_call_target="tpu_custom_call" | custom-call | tf_op jit(solution)/shard_map/detector_block/pallas_call | solution.py:180
  101.7 1.3 collective-permute-start.7
  103.0 0.0 collective-permute-done.9.tile_ref
  103.0 4.6 %detector_block.12 = bf16[256,512]{1,0:T(8,128)(2,1)S(1)} custom-call(s32[42]{0:T(128)S(1)} %pad_add_fusion.ints_ref, bf16[256,512]{1,0:T(8,128)(2,1)S(1)} %collective-permute-done.9.tile_ref, f32[4,56,128]{2,1,0:T(8,128)S(1)} %maximum_bitcast_fusion.param_ref, bf16[64,2,16,512]{3,2,1,0:T(8,128)(2,1)S(1)} %bitcast.26, ...), custom_call_target="tpu_custom_call" | custom-call | tf_op jit(solution)/shard_map/detector_block/pallas_call | solution.py:180
  107.7 1.3 collective-permute-start.10
  109.0 0.0 collective-permute-done.7.tile_ref
  109.0 0.6 detector_block.9.refs_0_
  109.5 4.1 %collective-permute-done.10.tile_ref = bf16[256,512]{1,0:T(8,128)(2,1)S(1)} collective-permute-done((bf16[256,512]{1,0:T(8,128)(2,1)S(1)}, bf16[256,512]{1,0:T(8,128)(2,1)S(1)}, u32[]{:S(2)}, u32[]{:S(2)}) %collective-permute-start.10) | collective-permute-done | bytes 262176 | tf_op jit(solution)/shard_map/ppermute | solution.py:529
  113.6 0.5 detector_block.13.refs_1_
  114.2 0.7 collective-permute-start.12
  114.9 0.7 collective-permute-start.11
  115.6 0.0 all-gather.3.cloned.1.call-done
  115.6 0.0 collective-permute-done.12.refs_2_
  115.6 0.0 collective-permute-done.11.refs_0_
  115.6 0.6 pick_crops.1
  116.2 0.7 collective-permute-start.13
  116.9 0.7 collective-permute-start.14
  117.6 1.3 collective-permute-start.15
  118.9 0.0 copy-start.2
  118.9 4.8 %stage_weights.1 = (bf16[8,3584,128]{2,1,0:T(8,128)(2,1)S(1)}, f32[208,1024]{1,0:T(8,128)S(1)}) custom-call(s32[42]{0:T(128)S(1)} %pad_add_fusion.ints_ref, bf16[208,768]{1,0:T(8,128)(2,1)} %copy-done.4, bf16[208,768]{1,0:T(8,128)(2,1)} %copy-done.1, bf16[208,768]{1,0:T(8,128)(2,1)} %collective-permute-done.3.pix_above, bf16[8,3584,128]{2,1,0:T(8,128)(2,1)} %bitcast.33), custom_call_target="tpu_custom_call" | custom-call | tf_op jit(solution)/shard_map/stage_weights/pallas_call | solution.py:357
  123.6 0.0 collective-permute-done.13.refs_0_
  123.7 0.0 collective-permute-done.14.refs_1_
  123.7 20.9 %collective-permute-done.15.refs_2_ = bf16[208,512]{1,0:T(8,128)(2,1)S(1)} collective-permute-done((bf16[208,512]{1,0:T(8,128)(2,1)S(1)}, bf16[208,512]{1,0:T(8,128)(2,1)S(1)}, u32[]{:S(2)}, u32[]{:S(2)}) %collective-permute-start.15) | collective-permute-done | bytes 213024 | tf_op jit(solution)/shard_map/ppermute | solution.py:537
  144.6 4.6 %classify.1 = f32[1,1024]{1,0:T(1,128)} custom-call(s32[42]{0:T(128)S(1)} %pad_add_fusion.ints_ref, bf16[208,512]{1,0:T(8,128)(2,1)S(1)} %collective-permute-done.13.refs_0_, bf16[208,512]{1,0:T(8,128)(2,1)S(1)} %collective-permute-done.14.refs_1_, bf16[208,512]{1,0:T(8,128)(2,1)S(1)} %collective-permute-done.15.refs_2_, ...), custom_call_target="tpu_custom_call" | custom-call | tf_op jit(solution)/shard_map/classify/pallas_call | solution.py:456
  (23 shorter events, 0.1 us)
Async XLA Ops:
  6.5 2.2 %copy-start.6 = (bf16[1,16,512]{2,1,0:T(8,128)(2,1)S(1)}, bf16[1,16,512]{2,1,0:T(8,128)(2,1)}, u32[]{:S(2)}) copy-start(bf16[1,16,512]{2,1,0:T(8,128)(2,1)} %param.20) | copy-start | bytes 49156
  6.5 2.2 %copy-start.7 = (bf16[1,512,16]{1,2,0:T(8,128)(2,1)S(1)}, bf16[1,512,16]{1,2,0:T(8,128)(2,1)}, u32[]{:S(2)}) copy-start(bf16[1,512,16]{1,2,0:T(8,128)(2,1)} %param.19) | copy-start | bytes 49156
  6.5 109.1 %all-gather.3.cloned.1.call-start = ((), (), s32[]{:S(2)}) async-start(), calls=%async_computation.2 | async-start | bytes 8257536 | tf_op jit(solution)/shard_map/all_gather | solution.py:501
  31.1 7.7 %copy-start.8 = (s32[1,4,3,3]{1,0,3,2:T(1,128)S(1)}, s32[1,4,3,3]{1,0,3,2:T(1,128)}, u32[]{:S(2)}) copy-start(s32[1,4,3,3]{1,0,3,2:T(1,128)} %param.28) | copy-start | bytes 436
  31.1 7.9 %copy-start.11 = (s32[1,4]{1,0:T(1,128)S(1)}, s32[1,4]{1,0:T(1,128)}, u32[]{:S(2)}) copy-start(s32[1,4]{1,0:T(1,128)} %param.29) | copy-start | bytes 52
  31.1 12.4 %copy-start = (bf16[2,16,16,768]{3,2,1,0:T(8,128)(2,1)S(1)}, bf16[2,16,16,768]{3,2,1,0:T(8,128)(2,1)}, u32[]{:S(2)}) copy-start(bf16[2,16,16,768]{3,2,1,0:T(8,128)(2,1)} %param.16) | copy-start | bytes 2359300
  31.1 22.1 %copy-start.5 = (f32[1,7,7,512]{3,0,2,1:T(1,128)S(1)}, f32[1,7,7,512]{3,0,2,1:T(1,128)}, u32[]{:S(2)}) copy-start(f32[1,7,7,512]{3,0,2,1:T(1,128)} %param.17) | copy-start | bytes 301060
  31.1 22.2 %copy-start.9 = (f32[1,512]{1,0:T(1,128)S(1)}, f32[1,512]{1,0:T(1,128)}, u32[]{:S(2)}) copy-start(f32[1,512]{1,0:T(1,128)} %param.21) | copy-start | bytes 6148
  31.1 22.2 %copy-start.10 = (f32[1,512]{1,0:T(1,128)S(1)}, f32[1,512]{1,0:T(1,128)}, u32[]{:S(2)}) copy-start(f32[1,512]{1,0:T(1,128)} %param.18) | copy-start | bytes 6148
  31.1 22.2 %copy-start.3 = (bf16[2,16,16,512]{3,2,1,0:T(8,128)(2,1)S(1)}, bf16[2,16,16,512]{3,2,1,0:T(8,128)(2,1)}, u32[]{:S(2)}) copy-start(bf16[2,16,16,512]{3,2,1,0:T(8,128)(2,1)} %param.15) | copy-start | bytes 1572868
  31.1 36.6 %all-to-all-start.1 = ((bf16[8,8,2,16,512]{4,3,2,1,0:T(8,128)(2,1)}), bf16[8,8,2,16,512]{4,3,2,1,0:T(8,128)(2,1)S(1)}, u32[]{:S(2)}, u32[]{:S(2)}) async-start(bf16[8,8,2,16,512]{4,3,2,1,0:T(8,128)(2,1)} %broadcast_in_dim.20), calls=%async_computation.1 | async-start | bytes 4194304 | tf_op jit(solution)/shard_map/all_to_all | solution.py:47
  39.1 23.6 %collective-permute-start.1 = (s32[42]{0:T(128)S(1)}, s32[42]{0:T(128)S(1)}, u32[]{:S(2)}, u32[]{:S(2)}) collective-permute-start(s32[42]{0:T(128)S(1)} %pad_add_fusion.ints_ref), channel_id=1, source_target_pairs={{1,0},{2,1},{3,2},{4,3},{5,4},{6,5},{7,6},{8,7},{9,8},{10,9},{11,1... | collective-permute-start | bytes 512 | tf_op jit(solution)/shard_map/ppermute | solution.py:509
  41.2 21.5 %collective-permute-start = (s32[42]{0:T(128)S(1)}, s32[42]{0:T(128)S(1)}, u32[]{:S(2)}, u32[]{:S(2)}) collective-permute-start(s32[42]{0:T(128)S(1)} %pad_add_fusion.ints_ref), channel_id=1, source_target_pairs={{0,1},{1,2},{2,3},{3,4},{4,5},{5,6},{6,7},{7,8},{8,9},{9,10},{10,1... | collective-permute-start | bytes 512 | tf_op jit(solution)/shard_map/ppermute | solution.py:508
  45.5 17.3 %copy-start.1 = (bf16[208,768]{1,0:T(8,128)(2,1)}, bf16[208,768]{1,0:T(8,128)(2,1)S(1)}, u32[]{:S(2)}) copy-start(bf16[208,768]{1,0:T(8,128)(2,1)S(1)} %get-tuple-element.25.pix_own) | copy-start | bytes 958468
  45.5 17.3 %collective-permute-start.2 = (bf16[208,768]{1,0:T(8,128)(2,1)S(1)}, bf16[208,768]{1,0:T(8,128)(2,1)S(1)}, u32[]{:S(2)}, u32[]{:S(2)}) collective-permute-start(bf16[208,768]{1,0:T(8,128)(2,1)S(1)} %get-tuple-element.24), channel_id=1, source_target_pairs={{0,1},{1,2},{2,3},{3,4},{4,5},{5,6},{6,7},{7,8},{8,9},{9,10},{10,1... | collective-permute-start | bytes 958472 | tf_op jit(solution)/shard_map/ppermute | solution.py:507
  47.7 18.9 %collective-permute-start.3 = (bf16[208,768]{1,0:T(8,128)(2,1)S(1)}, bf16[208,768]{1,0:T(8,128)(2,1)}, u32[]{:S(2)}, u32[]{:S(2)}) collective-permute-start(bf16[208,768]{1,0:T(8,128)(2,1)S(1)} %get-tuple-element.26), channel_id=1, source_target_pairs={{1,0},{2,1},{3,2},{4,3},{5,4},{6,5},{7,6},{8,7},{9,8},{10,9},{11,1... | collective-permute-start | bytes 958472 | tf_op jit(solution)/shard_map/ppermute | solution.py:507
  62.7 0.7 copy-start.4
  67.8 6.0 %collective-permute-start.4 = (bf16[64,2,16,512]{3,2,1,0:T(8,128)(2,1)S(1)}, bf16[64,2,16,512]{3,2,1,0:T(8,128)(2,1)S(1)}, u32[]{:S(2)}, u32[]{:S(2)}) collective-permute-start(bf16[64,2,16,512]{3,2,1,0:T(8,128)(2,1)S(1)} %bitcast.20), channel_id=1, source_target_pairs={{0,1},{1,0},{2,3},{3,2},{4,5},{5,4},{6,7},{7,6},{8,9},{9,8},{10,11... | collective-permute-start | bytes 6291464 | tf_op jit(solution)/shard_map/ppermute | solution.py:519
  74.4 1.9 %collective-permute-start.5 = (bf16[256,512]{1,0:T(8,128)(2,1)S(1)}, bf16[256,512]{1,0:T(8,128)(2,1)S(1)}, u32[]{:S(2)}, u32[]{:S(2)}) collective-permute-start(bf16[256,512]{1,0:T(8,128)(2,1)S(1)} %early_block.1), channel_id=1, source_target_pairs={{0,128},{1,129},{2,130},{3,131},{4,132},{5,133},{6,134},{7,135},{8... | collective-permute-start | bytes 786440 | tf_op jit(solution)/shard_map/ppermute | solution.py:529
  75.6 2.6 %collective-permute-start.8 = (bf16[256,512]{1,0:T(8,128)(2,1)S(1)}, bf16[256,512]{1,0:T(8,128)(2,1)S(1)}, u32[]{:S(2)}, u32[]{:S(2)}) collective-permute-start(bf16[256,512]{1,0:T(8,128)(2,1)S(1)} %detector_block.10), channel_id=1, source_target_pairs={{0,128},{1,129},{2,130},{3,131},{4,132},{5,133},{6,134},{7,135},{8... | collective-permute-start | bytes 786440 | tf_op jit(solution)/shard_map/ppermute | solution.py:529
  76.9 20.0 %collective-permute-start.6 = (bf16[256,512]{1,0:T(8,128)(2,1)S(1)}, bf16[256,512]{1,0:T(8,128)(2,1)S(1)}, u32[]{:S(2)}, u32[]{:S(2)}) collective-permute-start(bf16[256,512]{1,0:T(8,128)(2,1)S(1)} %detector_block.7), channel_id=1, source_target_pairs={{128,256},{129,257},{130,258},{131,259},{132,260},{133,261},{134,2... | collective-permute-start | bytes 786440 | tf_op jit(solution)/shard_map/ppermute | solution.py:529
  78.7 24.3 %collective-permute-start.9 = (bf16[256,512]{1,0:T(8,128)(2,1)S(1)}, bf16[256,512]{1,0:T(8,128)(2,1)S(1)}, u32[]{:S(2)}, u32[]{:S(2)}) collective-permute-start(bf16[256,512]{1,0:T(8,128)(2,1)S(1)} %detector_block.11), channel_id=1, source_target_pairs={{128,256},{129,257},{130,258},{131,259},{132,260},{133,261},{134,2... | collective-permute-start | bytes 786440 | tf_op jit(solution)/shard_map/ppermute | solution.py:529
  101.7 7.3 %collective-permute-start.7 = (bf16[256,512]{1,0:T(8,128)(2,1)S(1)}, bf16[256,512]{1,0:T(8,128)(2,1)S(1)}, u32[]{:S(2)}, u32[]{:S(2)}) collective-permute-start(bf16[256,512]{1,0:T(8,128)(2,1)S(1)} %detector_block.8), channel_id=1, source_target_pairs={{256,384},{257,385},{258,386},{259,387},{260,388},{261,389},{262,3... | collective-permute-start | bytes 786440 | tf_op jit(solution)/shard_map/ppermute | solution.py:529
  107.7 6.0 %collective-permute-start.10 = (bf16[256,512]{1,0:T(8,128)(2,1)S(1)}, bf16[256,512]{1,0:T(8,128)(2,1)S(1)}, u32[]{:S(2)}, u32[]{:S(2)}) collective-permute-start(bf16[256,512]{1,0:T(8,128)(2,1)S(1)} %detector_block.12), channel_id=1, source_target_pairs={{256,384},{257,385},{258,386},{259,387},{260,388},{261,389},{262,3... | collective-permute-start | bytes 786440 | tf_op jit(solution)/shard_map/ppermute | solution.py:529
  114.2 1.4 collective-permute-start.12
  114.9 0.7 collective-permute-start.11
  116.2 7.4 %collective-permute-start.13 = (bf16[208,512]{1,0:T(8,128)(2,1)S(1)}, bf16[208,512]{1,0:T(8,128)(2,1)S(1)}, u32[]{:S(2)}, u32[]{:S(2)}) collective-permute-start(bf16[208,512]{1,0:T(8,128)(2,1)S(1)} %get-tuple-element.32), channel_id=1, source_target_pairs={{384,0},{385,1},{386,2},{387,3},{388,4},{389,5},{390,6},{391,7},{3... | collective-permute-start | bytes 638984 | tf_op jit(solution)/shard_map/ppermute | solution.py:537
  116.9 6.8 %collective-permute-start.14 = (bf16[208,512]{1,0:T(8,128)(2,1)S(1)}, bf16[208,512]{1,0:T(8,128)(2,1)S(1)}, u32[]{:S(2)}, u32[]{:S(2)}) collective-permute-start(bf16[208,512]{1,0:T(8,128)(2,1)S(1)} %get-tuple-element.33), channel_id=1, source_target_pairs={{384,128},{385,129},{386,130},{387,131},{388,132},{389,133},{390,1... | collective-permute-start | bytes 638984 | tf_op jit(solution)/shard_map/ppermute | solution.py:537
  117.6 27.0 %collective-permute-start.15 = (bf16[208,512]{1,0:T(8,128)(2,1)S(1)}, bf16[208,512]{1,0:T(8,128)(2,1)S(1)}, u32[]{:S(2)}, u32[]{:S(2)}) collective-permute-start(bf16[208,512]{1,0:T(8,128)(2,1)S(1)} %get-tuple-element.34), channel_id=1, source_target_pairs={{384,256},{385,257},{386,258},{387,259},{388,260},{389,261},{390,2... | collective-permute-start | bytes 638984 | tf_op jit(solution)/shard_map/ppermute | solution.py:537
  118.9 25.7 %copy-start.2 = (f32[2,1024]{1,0:T(2,128)S(1)}, f32[2,1024]{1,0:T(2,128)}, u32[]{:S(2)}) copy-start(f32[2,1024]{1,0:T(2,128)} %refs_6_.1) | copy-start | bytes 24580
Sparse Core Ops, SparseCore 0:
  9.5 54.0 all-gather.2

commit v6 on v5

--- a/solution.py
+++ b/solution.py
@@ -198,15 +198,14 @@
 
 def cut_body(ints_ref, tile_ref, *refs):
     out_refs, buffer, sems = refs[:3], refs[3], refs[4]
-    base = ints_ref[SECTION_AT] * 9
+    core = ints_ref[CORE_AT]
+    bases = [ints_ref[SECTION_AT] * 9 + 3 * turn for turn in (2 - 2 * core, 1, 2 * core)]
     copies = []
-    for turn in range(3):
-        copies.append(
-            pltpu.make_async_copy(tile_ref.at[ints_ref[base + 3 * turn]], buffer.at[turn], sems.at[turn])
-        )
+    for turn, base in enumerate(bases):
+        copies.append(pltpu.make_async_copy(tile_ref.at[ints_ref[base]], buffer.at[turn], sems.at[turn]))
         copies[-1].start()
-    for turn in range(3):
-        chosen = selection(ints_ref[base + 3 * turn + 1], ints_ref[base + 3 * turn + 2])
+    for turn, base in enumerate(bases):
+        chosen = selection(ints_ref[base + 1], ints_ref[base + 2])
         copies[turn].wait()
         rows = jnp.dot(chosen, buffer[turn], preferred_element_type=jnp.float32)
         out_refs[turn][...] = rows.astype(jnp.bfloat16)
@@ -318,7 +317,7 @@
     )
 
 
-def stage_body(ints_ref, pix_below, pix_own, pix_above, packed, weights, base_ref, pix, sems):
+def stage_body(ints_ref, pix_near, pix_own, pix_far, packed, weights, base_ref, pix, sems):
     source = ints_ref[SLOT_AT + ints_ref[SECTION_AT]]
     sections = packed.shape[0] // 2
     spans = [(0, EMBED, MERGE), (1, POS, HALF), (0, MERGE, HALF), (1, KEY, POS)]
@@ -329,9 +328,12 @@
             copies.append(
                 pltpu.make_async_copy(packed.at[place], weights.at[place], sems.at[1 + len(copies)])
             )
-    for number, pix_ref in enumerate((pix_below, pix_own, pix_above)):
-
-        @pl.when((source == number + 1) if number != 1 else ((source == 2) | (source == 0)))
+    core = ints_ref[CORE_AT]
+    same_chip = ((source == 1) & (core == 1)) | ((source == 3) & (core == 0))
+    away = (source == 1) | (source == 3)
+    for pix_ref, wanted in ((pix_near, same_chip), (pix_own, ~away), (pix_far, away & ~same_chip)):
+
+        @pl.when(wanted)
         def _(pix_ref=pix_ref):
             copy = pltpu.make_async_copy(pix_ref, pix, sems.at[0])
             copy.start()
@@ -504,7 +506,6 @@
     line = spread_in_groups(shard, line_groups(True))
     plane = spread_in_groups(after(line, half), line_groups(False))
     cut = cut_pixels(ints, patches.reshape(2, CELLS, patches.shape[3]))
-    pixels = (lax.ppermute(cut[2], REP, upward), cut[1], lax.ppermute(cut[0], REP, downward))
     below = lax.ppermute(ints, REP, upward)
     above = lax.ppermute(ints, REP, downward)
     params = jnp.concatenate(
@@ -514,7 +515,11 @@
     start = tile_features.reshape(2, CELLS, width)
     tiles = [start[0], start[1]]
     early = early_norm(ints, tiles[0], params)
-    plane = after(plane, below, above, early, *pixels)
+    plane = after(plane, below, above, early, *cut)
+    cut = lax.optimization_barrier((*cut, plane))[:3]
+    beyond = [(index, index + 1) for index in range(1, count - 1, 2)]
+    beyond += [(target, origin) for origin, target in beyond]
+    pixels = (lax.ppermute(cut[0], REP, swap), cut[1], lax.ppermute(cut[2], REP, beyond))
     own = plane.reshape((SIDE * SIDE,) + shard.shape)
     other = lax.ppermute(own, REP, swap)
 
@@ -522,15 +527,15 @@
         if number == 0:
             first = early_block(ints, tiles[0], params, own, other, early)
         else:
-            first = detector_block(number, ints, tiles[0], params, own, other)
+            order = after(ints, *pixels) if number == 1 else ints
+            first = detector_block(number, order, tiles[0], params, own, other)
         before = (first,) if number == last else ()
         second = detector_block(number, after(ints, first), tiles[1], params, own, other, *before)
         if number < last:
             tiles = [lax.ppermute(tile, "section", [(number, number + 1)]) for tile in (first, second)]
 
     within = [(last * count + origin, last * count + target) for origin, target in swap]
-    across = [(last * count + index, last * count + index + 1) for index in range(1, count - 1, 2)]
-    across += [(target, origin) for origin, target in across]
+    across = [(last * count + origin, last * count + target) for origin, target in beyond]
     far = lax.ppermute(second, ("section",) + REP, across)
     near = lax.ppermute(second, ("section",) + REP, within)
     crops = pick_crops(after(ints, weights), below, above, (near, second, far), sections)

time: 157 us -> 158 us (level)
  waiting for transfers between devices: 59 us -> 63.2 us
  starting transfers between devices: 32.2 us -> 28.8 us
    ppermute x1, waiting for transfers between devices: 8.75 us -> 15.3 us  [per_device(): above = lax.ppermute(ints, REP, downward)]
    ppermute x6, waiting for transfers between devices: 20.9 us -> 16.3 us  [per_device(): lax.ppermute(tile, 'section', [(number, number + 1)])]
    ppermute x1, waiting for transfers between devices: 4.13 us -> 0.01 us  [per_device(): other = lax.ppermute(own, REP, swap)]
    all_to_all x1, waiting for transfers between devices: 1.16 us -> 4.86 us  [spread_in_groups(): return lax.all_to_all(copies, REP, 0, 0, axis_index_groups=groups)]
    ppermute x2, starting transfers between devices: 7.67 us -> 4.33 us  [the longest x1 2.41 us: per_device(): lax.ppermute(cut[0], REP, swap)]
    ppermute x2, waiting for transfers between devices: 3.13 us -> 5.97 us  [the longest x1 5.97 us: per_device(): lax.ppermute(cut[2], REP, beyond)]
  transfers between devices with their start and end apart: 18 -> 18, of which waited for: 7 -> 6; matrix products, arithmetic and copies ran while one was open for 1% -> 2% of each run, Pallas kernels for 13% -> 13%
where the time goes in v6:
time: 158 us; the launch traced here: 157 us
  waiting for transfers between devices  63.2 us (40%)
  starting transfers between devices  28.8 us (18%)
  Pallas kernels  27.4 us (17%)
  blocking collectives  20.6 us (13%)
  between operations  13.8 us (9%)
  local copies, waits for them, and re-layouts  3.34 us (2%)
    ppermute x3, waiting for transfers between devices, per_device(): lax.ppermute(crops[slot], 'section', [(last, slot)])  20.6 us
    all_to_all x1, blocking collectives, spread_in_groups(): return lax.all_to_all(copies, REP, 0, 0, axis_index_groups=groups)  20.6 us
    ppermute x6, waiting for transfers between devices, per_device(): lax.ppermute(tile, 'section', [(number, number + 1)])  16.3 us
    ppermute x1, waiting for transfers between devices, per_device(): above = lax.ppermute(ints, REP, downward)  15.3 us
    pallas_call x7, Pallas kernels, detector_block(): pl.pallas_call(functools.partial(block_body, number=number), out_shape=pl...  12.2 us
    all_to_all x1, starting transfers between devices, spread_in_groups(): return lax.all_to_all(copies, REP, 0, 0, axis_index_groups=groups)  7.69 us
    ppermute x6, starting transfers between devices, per_device(): lax.ppermute(tile, 'section', [(number, number + 1)])  6.54 us
    ppermute x1, waiting for transfers between devices, per_device(): lax.ppermute(cut[2], REP, beyond)  5.97 us
  transfers between devices with their start and end apart: 18, of which 6 were waited for; matrix products, arithmetic and copies ran while one was open for 2% of the time, Pallas kernels for 13%

profile of v6, /device:TPU:12, one launch (start us, length us, event | category | flops | bytes accessed | tf_op | source)
XLA Modules:
  0.0 157.3 jit_solution(2997943157273789727)
XLA Ops:
  6.5 2.2 %pack_weights.1 = bf16[3584,128]{1,0:T(8,128)(2,1)} custom-call(s32[1]{0:T(128)} %bitcast.2.parity_ref, bf16[768,256]{1,0:T(8,128)(2,1)} %embed.1, bf16[512,256]{1,0:T(8,128)(2,1)} %merge.1, bf16[196,256]{1,0:T(8,128)(2,1)} %pos.1, bf16[3,1024,128]{2,1,0:T(8,128)(2,1)} %bitcast.34, bf16[128,1024]{1,0:T(8,128)(2,1)} %out.1), custom_call_target="tpu_custom_call" | custom-call | tf_op jit(solution)/shard_map/pack_weights/pallas_call | solution.py:303
  8.7 0.0 all-gather.3.cloned.1.call-update
  8.8 20.6 %all_to_all.10 = bf16[8,2,16,512]{3,2,1,0:T(8,128)(2,1)S(1)} all-to-all(bf16[8,2,16,512]{3,2,1,0:T(8,128)(2,1)S(1)} %broadcast_in_dim.8), channel_id=1, replica_groups={{0,2,4,6,8,10,12,14},{16,18,20,22,24,26,28,30},{32,34,36,38,40,42,44,46..., dimensions={0} | all-to-all | bytes 524288 | tf_op jit(solution)/shard_map/all_to_all | solution.py:47
  29.4 1.7 %broadcast_in_dim.9 = bf16[8,8,2,16,512]{4,3,2,1,0:T(8,128)(2,1)} broadcast(bf16[8,2,16,512]{3,2,1,0:T(8,128)(2,1)S(1)} %all_to_all.10), dimensions={1,2,3,4} | broadcast | bytes 2359296 | tf_op jit(solution)/shard_map/broadcast_in_dim | solution.py:46
  31.1 0.0 copy-start.10
  31.1 0.0 copy-start.11
  31.1 7.7 %all-to-all-start.1 = ((bf16[8,8,2,16,512]{4,3,2,1,0:T(8,128)(2,1)}), bf16[8,8,2,16,512]{4,3,2,1,0:T(8,128)(2,1)S(1)}, u32[]{:S(2)}, u32[]{:S(2)}) async-start(bf16[8,8,2,16,512]{4,3,2,1,0:T(8,128)(2,1)} %broadcast_in_dim.9), calls=%async_computation.1 | async-start | bytes 4194304 | tf_op jit(solution)/shard_map/all_to_all | solution.py:47
  38.8 0.1 copy.17
  38.9 0.1 reshape.32
  39.0 0.1 pad_add_fusion.ints_ref
  39.1 2.0 %collective-permute-start.1 = (s32[42]{0:T(128)S(1)}, s32[42]{0:T(128)S(1)}, u32[]{:S(2)}, u32[]{:S(2)}) collective-permute-start(s32[42]{0:T(128)S(1)} %pad_add_fusion.ints_ref), channel_id=1, source_target_pairs={{1,0},{2,1},{3,2},{4,3},{5,4},{6,5},{7,6},{8,7},{9,8},{10,9},{11,1... | collective-permute-start | bytes 512 | tf_op jit(solution)/shard_map/ppermute | solution.py:510
  41.1 2.4 %collective-permute-start = (s32[42]{0:T(128)S(1)}, s32[42]{0:T(128)S(1)}, u32[]{:S(2)}, u32[]{:S(2)}) collective-permute-start(s32[42]{0:T(128)S(1)} %pad_add_fusion.ints_ref), channel_id=1, source_target_pairs={{0,1},{1,2},{2,3},{3,4},{4,5},{5,6},{6,7},{7,8},{8,9},{9,10},{10,1... | collective-permute-start | bytes 512 | tf_op jit(solution)/shard_map/ppermute | solution.py:509
  43.4 0.0 copy-done.6
  43.5 0.0 copy-done
  43.5 2.0 %cut_pixels.1 = (bf16[208,768]{1,0:T(8,128)(2,1)S(1)}, bf16[208,768]{1,0:T(8,128)(2,1)S(1)}, bf16[208,768]{1,0:T(8,128)(2,1)S(1)}) custom-call(s32[42]{0:T(128)S(1)} %pad_add_fusion.ints_ref, bf16[2,256,768]{2,1,0:T(8,128)(2,1)S(1)} %bitcast.32), custom_call_target="tpu_custom_call" | custom-call | tf_op jit(solution)/shard_map/cut_pixels/pallas_call | solution.py:216
  45.5 0.1 pad.3.clone
  45.6 0.1 maximum_bitcast_fusion.param_ref
  45.7 1.1 fusion
  46.8 0.5 early_norm.1.normed_ref
  47.4 15.3 %collective-permute-done.1.above_ref = s32[42]{0:T(128)S(1)} collective-permute-done((s32[42]{0:T(128)S(1)}, s32[42]{0:T(128)S(1)}, u32[]{:S(2)}, u32[]{:S(2)}) %collective-permute-start.1) | collective-permute-done | bytes 200 | tf_op jit(solution)/shard_map/ppermute | solution.py:510
  62.7 0.0 collective-permute-done.below_ref
  62.7 4.9 %all-to-all-done.1 = bf16[8,8,2,16,512]{4,3,2,1,0:T(8,128)(2,1)S(1)} async-done(((bf16[8,8,2,16,512]{4,3,2,1,0:T(8,128)(2,1)}), bf16[8,8,2,16,512]{4,3,2,1,0:T(8,128)(2,1)S(1)}, u32[]{:S(2)}, u32[]{:S(2)}) %all-to-all-start.1) | async-done | bytes 2097184 | tf_op jit(solution)/shard_map/all_to_all | solution.py:47
  67.6 1.9 %collective-permute-start.4 = (bf16[64,2,16,512]{3,2,1,0:T(8,128)(2,1)S(1)}, bf16[64,2,16,512]{3,2,1,0:T(8,128)(2,1)S(1)}, u32[]{:S(2)}, u32[]{:S(2)}) collective-permute-start(bf16[64,2,16,512]{3,2,1,0:T(8,128)(2,1)S(1)} %bitcast.20), channel_id=1, source_target_pairs={{0,1},{1,0},{2,3},{3,2},{4,5},{5,4},{6,7},{7,6},{8,9},{9,8},{10,11... | collective-permute-start | bytes 6291464 | tf_op jit(solution)/shard_map/ppermute | solution.py:524
  69.5 2.4 %collective-permute-start.2 = (bf16[208,768]{1,0:T(8,128)(2,1)}, bf16[208,768]{1,0:T(8,128)(2,1)S(1)}, u32[]{:S(2)}, u32[]{:S(2)}) collective-permute-start(bf16[208,768]{1,0:T(8,128)(2,1)} %copy-done.3), channel_id=1, source_target_pairs={{0,1},{1,0},{2,3},{3,2},{4,5},{5,4},{6,7},{7,6},{8,9},{9,8},{10,11... | collective-permute-start | bytes 958472 | tf_op jit(solution)/shard_map/ppermute | solution.py:522
  71.9 1.9 %collective-permute-start.3 = (bf16[208,768]{1,0:T(8,128)(2,1)S(1)}, bf16[208,768]{1,0:T(8,128)(2,1)S(1)}, u32[]{:S(2)}, u32[]{:S(2)}) collective-permute-start(bf16[208,768]{1,0:T(8,128)(2,1)S(1)} %get-tuple-element.34), channel_id=1, source_target_pairs={{1,2},{3,4},{5,6},{7,8},{9,10},{11,12},{13,14},{15,16},{17,18},{19... | collective-permute-start | bytes 958472 | tf_op jit(solution)/shard_map/ppermute | solution.py:522
  73.8 0.0 collective-permute-done.4.other_ref
  73.8 0.6 early_block.1
  74.4 0.7 collective-permute-start.5
  75.1 0.6 detector_block.10
  75.6 0.7 collective-permute-start.8
  76.3 0.0 collective-permute-done.2.pix_near
  76.3 6.0 %collective-permute-done.3.pix_far = bf16[208,768]{1,0:T(8,128)(2,1)S(1)} collective-permute-done((bf16[208,768]{1,0:T(8,128)(2,1)S(1)}, bf16[208,768]{1,0:T(8,128)(2,1)S(1)}, u32[]{:S(2)}, u32[]{:S(2)}) %collective-permute-start.3) | collective-permute-done | bytes 319520 | tf_op jit(solution)/shard_map/ppermute | solution.py:522
  82.3 0.0 collective-permute-done.5.tile_ref
  82.3 0.5 detector_block.7
  82.9 0.2 copy-done.5
  83.1 1.3 collective-permute-start.6
  84.3 0.0 collective-permute-done.8.tile_ref
  84.4 0.6 detector_block.11
  84.9 1.3 collective-permute-start.9
  86.2 11.7 %collective-permute-done.6.tile_ref = bf16[256,512]{1,0:T(8,128)(2,1)S(1)} collective-permute-done((bf16[256,512]{1,0:T(8,128)(2,1)S(1)}, bf16[256,512]{1,0:T(8,128)(2,1)S(1)}, u32[]{:S(2)}, u32[]{:S(2)}) %collective-permute-start.6) | collective-permute-done | bytes 262176 | tf_op jit(solution)/shard_map/ppermute | solution.py:535
  97.9 4.8 %detector_block.8 = bf16[256,512]{1,0:T(8,128)(2,1)S(1)} custom-call(s32[42]{0:T(128)S(1)} %pad_add_fusion.ints_ref, bf16[256,512]{1,0:T(8,128)(2,1)S(1)} %collective-permute-done.6.tile_ref, f32[4,56,128]{2,1,0:T(8,128)S(1)} %maximum_bitcast_fusion.param_ref, bf16[64,2,16,512]{3,2,1,0:T(8,128)(2,1)S(1)} %bitcast.25, ...), custom_call_target="tpu_custom_call" | custom-call | tf_op jit(solution)/shard_map/detector_block/pallas_call | solution.py:180
  102.7 1.3 collective-permute-start.7
  104.1 0.0 collective-permute-done.9.tile_ref
  104.1 4.6 %detector_block.12 = bf16[256,512]{1,0:T(8,128)(2,1)S(1)} custom-call(s32[42]{0:T(128)S(1)} %pad_add_fusion.ints_ref, bf16[256,512]{1,0:T(8,128)(2,1)S(1)} %collective-permute-done.9.tile_ref, f32[4,56,128]{2,1,0:T(8,128)S(1)} %maximum_bitcast_fusion.param_ref, bf16[64,2,16,512]{3,2,1,0:T(8,128)(2,1)S(1)} %bitcast.26, ...), custom_call_target="tpu_custom_call" | custom-call | tf_op jit(solution)/shard_map/detector_block/pallas_call | solution.py:180
  108.7 1.3 collective-permute-start.10
  110.0 0.0 collective-permute-done.7.tile_ref
  110.0 0.6 detector_block.9.refs_0_
  110.6 4.6 %collective-permute-done.10.tile_ref = bf16[256,512]{1,0:T(8,128)(2,1)S(1)} collective-permute-done((bf16[256,512]{1,0:T(8,128)(2,1)S(1)}, bf16[256,512]{1,0:T(8,128)(2,1)S(1)}, u32[]{:S(2)}, u32[]{:S(2)}) %collective-permute-start.10) | collective-permute-done | bytes 262176 | tf_op jit(solution)/shard_map/ppermute | solution.py:535
  115.2 0.5 detector_block.13.refs_1_
  115.8 0.7 collective-permute-start.12
  116.5 0.7 collective-permute-start.11
  117.2 0.0 all-gather.3.cloned.1.call-done
  117.2 0.0 collective-permute-done.12.refs_2_
  117.2 0.0 collective-permute-done.11.refs_0_
  117.3 0.6 pick_crops.1
  117.8 0.7 collective-permute-start.13
  118.5 0.7 collective-permute-start.14
  119.2 1.3 collective-permute-start.15
  120.5 0.0 copy-start.2
  120.5 4.8 %stage_weights.1 = (bf16[8,3584,128]{2,1,0:T(8,128)(2,1)S(1)}, f32[208,1024]{1,0:T(8,128)S(1)}) custom-call(s32[42]{0:T(128)S(1)} %pad_add_fusion.ints_ref, bf16[208,768]{1,0:T(8,128)(2,1)} %copy-done.4, bf16[208,768]{1,0:T(8,128)(2,1)} %copy-done.1, bf16[208,768]{1,0:T(8,128)(2,1)} %copy-done.5, bf16[8,3584,128]{2,1,0:T(8,128)(2,1)} %bitcast.33), custom_call_target="tpu_custom_call" | custom-call | tf_op jit(solution)/shard_map/stage_weights/pallas_call | solution.py:359
  125.3 0.0 collective-permute-done.13.refs_0_
  125.3 0.0 collective-permute-done.14.refs_1_
  125.3 20.6 %collective-permute-done.15.refs_2_ = bf16[208,512]{1,0:T(8,128)(2,1)S(1)} collective-permute-done((bf16[208,512]{1,0:T(8,128)(2,1)S(1)}, bf16[208,512]{1,0:T(8,128)(2,1)S(1)}, u32[]{:S(2)}, u32[]{:S(2)}) %collective-permute-start.15) | collective-permute-done | bytes 213024 | tf_op jit(solution)/shard_map/ppermute | solution.py:542
  145.9 4.6 %classify.1 = f32[1,1024]{1,0:T(1,128)} custom-call(s32[42]{0:T(128)S(1)} %pad_add_fusion.ints_ref, bf16[208,512]{1,0:T(8,128)(2,1)S(1)} %collective-permute-done.13.refs_0_, bf16[208,512]{1,0:T(8,128)(2,1)S(1)} %collective-permute-done.14.refs_1_, bf16[208,512]{1,0:T(8,128)(2,1)S(1)} %collective-permute-done.15.refs_2_, ...), custom_call_target="tpu_custom_call" | custom-call | tf_op jit(solution)/shard_map/classify/pallas_call | solution.py:458
  (25 shorter events, 0.1 us)
Async XLA Ops:
  6.5 2.2 %copy-start.7 = (bf16[1,16,512]{2,1,0:T(8,128)(2,1)S(1)}, bf16[1,16,512]{2,1,0:T(8,128)(2,1)}, u32[]{:S(2)}) copy-start(bf16[1,16,512]{2,1,0:T(8,128)(2,1)} %param.20) | copy-start | bytes 49156
  6.5 2.2 %copy-start.8 = (bf16[1,512,16]{1,2,0:T(8,128)(2,1)S(1)}, bf16[1,512,16]{1,2,0:T(8,128)(2,1)}, u32[]{:S(2)}) copy-start(bf16[1,512,16]{1,2,0:T(8,128)(2,1)} %param.19) | copy-start | bytes 49156
  6.5 110.7 %all-gather.3.cloned.1.call-start = ((), (), s32[]{:S(2)}) async-start(), calls=%async_computation.2 | async-start | bytes 8257536 | tf_op jit(solution)/shard_map/all_gather | solution.py:503
  31.1 7.7 %copy-start.9 = (s32[1,4,3,3]{1,0,3,2:T(1,128)S(1)}, s32[1,4,3,3]{1,0,3,2:T(1,128)}, u32[]{:S(2)}) copy-start(s32[1,4,3,3]{1,0,3,2:T(1,128)} %param.28) | copy-start | bytes 436
  31.1 7.9 %copy-start.12 = (s32[1,4]{1,0:T(1,128)S(1)}, s32[1,4]{1,0:T(1,128)}, u32[]{:S(2)}) copy-start(s32[1,4]{1,0:T(1,128)} %param.29) | copy-start | bytes 52
  31.1 12.4 %copy-start.6 = (f32[1,7,7,512]{3,0,2,1:T(1,128)S(1)}, f32[1,7,7,512]{3,0,2,1:T(1,128)}, u32[]{:S(2)}) copy-start(f32[1,7,7,512]{3,0,2,1:T(1,128)} %param.17) | copy-start | bytes 301060
  31.1 12.4 %copy-start = (bf16[2,16,16,768]{3,2,1,0:T(8,128)(2,1)S(1)}, bf16[2,16,16,768]{3,2,1,0:T(8,128)(2,1)}, u32[]{:S(2)}) copy-start(bf16[2,16,16,768]{3,2,1,0:T(8,128)(2,1)} %param.16) | copy-start | bytes 2359300
  31.1 14.5 %copy-start.10 = (f32[1,512]{1,0:T(1,128)S(1)}, f32[1,512]{1,0:T(1,128)}, u32[]{:S(2)}) copy-start(f32[1,512]{1,0:T(1,128)} %param.21) | copy-start | bytes 6148
  31.1 14.5 %copy-start.11 = (f32[1,512]{1,0:T(1,128)S(1)}, f32[1,512]{1,0:T(1,128)}, u32[]{:S(2)}) copy-start(f32[1,512]{1,0:T(1,128)} %param.18) | copy-start | bytes 6148
  31.1 36.4 %all-to-all-start.1 = ((bf16[8,8,2,16,512]{4,3,2,1,0:T(8,128)(2,1)}), bf16[8,8,2,16,512]{4,3,2,1,0:T(8,128)(2,1)S(1)}, u32[]{:S(2)}, u32[]{:S(2)}) async-start(bf16[8,8,2,16,512]{4,3,2,1,0:T(8,128)(2,1)} %broadcast_in_dim.9), calls=%async_computation.1 | async-start | bytes 4194304 | tf_op jit(solution)/shard_map/all_to_all | solution.py:47
  39.1 23.6 %collective-permute-start.1 = (s32[42]{0:T(128)S(1)}, s32[42]{0:T(128)S(1)}, u32[]{:S(2)}, u32[]{:S(2)}) collective-permute-start(s32[42]{0:T(128)S(1)} %pad_add_fusion.ints_ref), channel_id=1, source_target_pairs={{1,0},{2,1},{3,2},{4,3},{5,4},{6,5},{7,6},{8,7},{9,8},{10,9},{11,1... | collective-permute-start | bytes 512 | tf_op jit(solution)/shard_map/ppermute | solution.py:510
  41.1 21.6 %collective-permute-start = (s32[42]{0:T(128)S(1)}, s32[42]{0:T(128)S(1)}, u32[]{:S(2)}, u32[]{:S(2)}) collective-permute-start(s32[42]{0:T(128)S(1)} %pad_add_fusion.ints_ref), channel_id=1, source_target_pairs={{0,1},{1,2},{2,3},{3,4},{4,5},{5,6},{6,7},{7,8},{8,9},{9,10},{10,1... | collective-permute-start | bytes 512 | tf_op jit(solution)/shard_map/ppermute | solution.py:509
  45.5 17.2 %copy-start.1 = (bf16[208,768]{1,0:T(8,128)(2,1)}, bf16[208,768]{1,0:T(8,128)(2,1)S(1)}, u32[]{:S(2)}) copy-start(bf16[208,768]{1,0:T(8,128)(2,1)S(1)} %get-tuple-element.33.pix_own) | copy-start | bytes 958468
  45.5 17.2 %copy-start.3 = (bf16[208,768]{1,0:T(8,128)(2,1)}, bf16[208,768]{1,0:T(8,128)(2,1)S(1)}, u32[]{:S(2)}) copy-start(bf16[208,768]{1,0:T(8,128)(2,1)S(1)} %get-tuple-element.32) | copy-start | bytes 958468
  67.6 6.3 %collective-permute-start.4 = (bf16[64,2,16,512]{3,2,1,0:T(8,128)(2,1)S(1)}, bf16[64,2,16,512]{3,2,1,0:T(8,128)(2,1)S(1)}, u32[]{:S(2)}, u32[]{:S(2)}) collective-permute-start(bf16[64,2,16,512]{3,2,1,0:T(8,128)(2,1)S(1)} %bitcast.20), channel_id=1, source_target_pairs={{0,1},{1,0},{2,3},{3,2},{4,5},{5,4},{6,7},{7,6},{8,9},{9,8},{10,11... | collective-permute-start | bytes 6291464 | tf_op jit(solution)/shard_map/ppermute | solution.py:524
  69.5 6.8 %collective-permute-start.2 = (bf16[208,768]{1,0:T(8,128)(2,1)}, bf16[208,768]{1,0:T(8,128)(2,1)S(1)}, u32[]{:S(2)}, u32[]{:S(2)}) collective-permute-start(bf16[208,768]{1,0:T(8,128)(2,1)} %copy-done.3), channel_id=1, source_target_pairs={{0,1},{1,0},{2,3},{3,2},{4,5},{5,4},{6,7},{7,6},{8,9},{9,8},{10,11... | collective-permute-start | bytes 958472 | tf_op jit(solution)/shard_map/ppermute | solution.py:522
  71.9 10.4 %collective-permute-start.3 = (bf16[208,768]{1,0:T(8,128)(2,1)S(1)}, bf16[208,768]{1,0:T(8,128)(2,1)S(1)}, u32[]{:S(2)}, u32[]{:S(2)}) collective-permute-start(bf16[208,768]{1,0:T(8,128)(2,1)S(1)} %get-tuple-element.34), channel_id=1, source_target_pairs={{1,2},{3,4},{5,6},{7,8},{9,10},{11,12},{13,14},{15,16},{17,18},{19... | collective-permute-start | bytes 958472 | tf_op jit(solution)/shard_map/ppermute | solution.py:522
  74.4 7.9 %collective-permute-start.5 = (bf16[256,512]{1,0:T(8,128)(2,1)S(1)}, bf16[256,512]{1,0:T(8,128)(2,1)S(1)}, u32[]{:S(2)}, u32[]{:S(2)}) collective-permute-start(bf16[256,512]{1,0:T(8,128)(2,1)S(1)} %early_block.1), channel_id=1, source_target_pairs={{0,128},{1,129},{2,130},{3,131},{4,132},{5,133},{6,134},{7,135},{8... | collective-permute-start | bytes 786440 | tf_op jit(solution)/shard_map/ppermute | solution.py:535
  75.6 8.7 %collective-permute-start.8 = (bf16[256,512]{1,0:T(8,128)(2,1)S(1)}, bf16[256,512]{1,0:T(8,128)(2,1)S(1)}, u32[]{:S(2)}, u32[]{:S(2)}) collective-permute-start(bf16[256,512]{1,0:T(8,128)(2,1)S(1)} %detector_block.10), channel_id=1, source_target_pairs={{0,128},{1,129},{2,130},{3,131},{4,132},{5,133},{6,134},{7,135},{8... | collective-permute-start | bytes 786440 | tf_op jit(solution)/shard_map/ppermute | solution.py:535
  76.3 6.5 %copy-start.4 = (bf16[208,768]{1,0:T(8,128)(2,1)}, bf16[208,768]{1,0:T(8,128)(2,1)S(1)}, u32[]{:S(2)}) copy-start(bf16[208,768]{1,0:T(8,128)(2,1)S(1)} %collective-permute-done.2.pix_near) | copy-start | bytes 958468
  82.3 0.8 copy-start.5
  83.1 14.8 %collective-permute-start.6 = (bf16[256,512]{1,0:T(8,128)(2,1)S(1)}, bf16[256,512]{1,0:T(8,128)(2,1)S(1)}, u32[]{:S(2)}, u32[]{:S(2)}) collective-permute-start(bf16[256,512]{1,0:T(8,128)(2,1)S(1)} %detector_block.7), channel_id=1, source_target_pairs={{128,256},{129,257},{130,258},{131,259},{132,260},{133,261},{134,2... | collective-permute-start | bytes 786440 | tf_op jit(solution)/shard_map/ppermute | solution.py:535
  84.9 19.1 %collective-permute-start.9 = (bf16[256,512]{1,0:T(8,128)(2,1)S(1)}, bf16[256,512]{1,0:T(8,128)(2,1)S(1)}, u32[]{:S(2)}, u32[]{:S(2)}) collective-permute-start(bf16[256,512]{1,0:T(8,128)(2,1)S(1)} %detector_block.11), channel_id=1, source_target_pairs={{128,256},{129,257},{130,258},{131,259},{132,260},{133,261},{134,2... | collective-permute-start | bytes 786440 | tf_op jit(solution)/shard_map/ppermute | solution.py:535
  102.7 7.3 %collective-permute-start.7 = (bf16[256,512]{1,0:T(8,128)(2,1)S(1)}, bf16[256,512]{1,0:T(8,128)(2,1)S(1)}, u32[]{:S(2)}, u32[]{:S(2)}) collective-permute-start(bf16[256,512]{1,0:T(8,128)(2,1)S(1)} %detector_block.8), channel_id=1, source_target_pairs={{256,384},{257,385},{258,386},{259,387},{260,388},{261,389},{262,3... | collective-permute-start | bytes 786440 | tf_op jit(solution)/shard_map/ppermute | solution.py:535
  108.7 6.5 %collective-permute-start.10 = (bf16[256,512]{1,0:T(8,128)(2,1)S(1)}, bf16[256,512]{1,0:T(8,128)(2,1)S(1)}, u32[]{:S(2)}, u32[]{:S(2)}) collective-permute-start(bf16[256,512]{1,0:T(8,128)(2,1)S(1)} %detector_block.12), channel_id=1, source_target_pairs={{256,384},{257,385},{258,386},{259,387},{260,388},{261,389},{262,3... | collective-permute-start | bytes 786440 | tf_op jit(solution)/shard_map/ppermute | solution.py:535
  115.8 1.4 collective-permute-start.12
  116.5 0.7 collective-permute-start.11
  117.8 7.5 %collective-permute-start.13 = (bf16[208,512]{1,0:T(8,128)(2,1)S(1)}, bf16[208,512]{1,0:T(8,128)(2,1)S(1)}, u32[]{:S(2)}, u32[]{:S(2)}) collective-permute-start(bf16[208,512]{1,0:T(8,128)(2,1)S(1)} %get-tuple-element.40), channel_id=1, source_target_pairs={{384,0},{385,1},{386,2},{387,3},{388,4},{389,5},{390,6},{391,7},{3... | collective-permute-start | bytes 638984 | tf_op jit(solution)/shard_map/ppermute | solution.py:542
  118.5 6.8 %collective-permute-start.14 = (bf16[208,512]{1,0:T(8,128)(2,1)S(1)}, bf16[208,512]{1,0:T(8,128)(2,1)S(1)}, u32[]{:S(2)}, u32[]{:S(2)}) collective-permute-start(bf16[208,512]{1,0:T(8,128)(2,1)S(1)} %get-tuple-element.41), channel_id=1, source_target_pairs={{384,128},{385,129},{386,130},{387,131},{388,132},{389,133},{390,1... | collective-permute-start | bytes 638984 | tf_op jit(solution)/shard_map/ppermute | solution.py:542
  119.2 26.7 %collective-permute-start.15 = (bf16[208,512]{1,0:T(8,128)(2,1)S(1)}, bf16[208,512]{1,0:T(8,128)(2,1)S(1)}, u32[]{:S(2)}, u32[]{:S(2)}) collective-permute-start(bf16[208,512]{1,0:T(8,128)(2,1)S(1)} %get-tuple-element.42), channel_id=1, source_target_pairs={{384,256},{385,257},{386,258},{387,259},{388,260},{389,261},{390,2... | collective-permute-start | bytes 638984 | tf_op jit(solution)/shard_map/ppermute | solution.py:542
  120.5 25.4 %copy-start.2 = (f32[2,1024]{1,0:T(2,128)S(1)}, f32[2,1024]{1,0:T(2,128)}, u32[]{:S(2)}) copy-start(f32[2,1024]{1,0:T(2,128)} %refs_6_.1) | copy-start | bytes 24580
Sparse Core Ops, SparseCore 0:
  9.5 54.0 all-gather.2

commit v7 on v6

--- a/solution.py
+++ b/solution.py
@@ -21,6 +21,7 @@
 SLOT_AT = 36
 SECTION_AT = 40
 CORE_AT = 41
+INTS = 42
 
 ANY = pl.BlockSpec(memory_space=pl.ANY)
 SMEM = pl.BlockSpec(memory_space=pltpu.SMEM)
@@ -51,8 +52,8 @@
     return pltpu.with_memory_space_constraint(array, pltpu.HBM)
 
 
-def active(ints_ref, number):
-    return ints_ref[SECTION_AT] == number
+def active(number):
+    return lax.axis_index("section") == number
 
 
 def conv_norm(tile_ref, param_ref, normed_ref, wide, conv):
@@ -95,8 +96,8 @@
         ).astype(jnp.bfloat16)
 
 
-def early_body(ints_ref, tile_ref, param_ref, normed_ref, wide, conv):
-    @pl.when(active(ints_ref, 0))
+def early_body(tile_ref, param_ref, normed_ref, wide, conv):
+    @pl.when(active(0))
     def _():
         conv_norm(tile_ref, param_ref, normed_ref, wide, conv)
 
@@ -110,16 +111,16 @@
     ]
 
 
-def early_norm(ints, tile, params):
+def early_norm(tile, params):
     return pl.pallas_call(
         early_body,
         out_shape=pltpu.VMEM(tile.shape, jnp.bfloat16),
-        in_specs=[SMEM, VMEM, VMEM],
+        in_specs=[VMEM, VMEM],
         out_specs=VMEM,
         scratch_shapes=conv_scratch(tile),
         compiler_params=LIMITED,
         name="early_norm",
-    )(ints, resident(tile), resident(params))
+    )(resident(tile), resident(params))
 
 
 def mlp(normed_ref, own_ref, other_ref, tile_ref, param_ref, out_ref):
@@ -145,16 +146,16 @@
         ).astype(jnp.bfloat16)
 
 
-def early_block_body(ints_ref, tile_ref, param_ref, own_ref, other_ref, normed_ref, out_ref):
-    @pl.when(active(ints_ref, 0))
+def early_block_body(tile_ref, param_ref, own_ref, other_ref, normed_ref, out_ref):
+    @pl.when(active(0))
     def _():
         mlp(normed_ref, own_ref, other_ref, tile_ref, param_ref, out_ref)
 
 
-def block_body(ints_ref, tile_ref, param_ref, own_ref, other_ref, *refs, number):
+def block_body(tile_ref, param_ref, own_ref, other_ref, *refs, number):
     before, (out_ref, normed, wide, conv) = refs[:-4], refs[-4:]
 
-    @pl.when(active(ints_ref, number))
+    @pl.when(active(number))
     def _():
         conv_norm(tile_ref, param_ref, normed, wide, conv)
         result_ref = out_ref
@@ -164,28 +165,28 @@
         mlp(normed, own_ref, other_ref, tile_ref, param_ref, result_ref)
 
 
-def early_block(ints, tile, params, own, other, normed):
+def early_block(tile, params, own, other, normed):
     return pl.pallas_call(
         early_block_body,
         out_shape=pltpu.VMEM(tile.shape, jnp.bfloat16),
-        in_specs=[SMEM] + [VMEM] * 5,
+        in_specs=[VMEM] * 5,
         out_specs=VMEM,
         compiler_params=LIMITED,
         name="early_block",
-    )(ints, *map(resident, (tile, params, own, other, normed)))
-
-
-def detector_block(number, ints, tile, params, own, other, *before):
+    )(*map(resident, (tile, params, own, other, normed)))
+
+
+def detector_block(number, tile, params, own, other, *before):
     shape = (2,) + tile.shape if before else tile.shape
     return pl.pallas_call(
         functools.partial(block_body, number=number),
         out_shape=pltpu.VMEM(shape, jnp.bfloat16),
-        in_specs=[SMEM] + [VMEM] * (4 + len(before)),
+        in_specs=[VMEM] * (4 + len(before)),
         out_specs=VMEM,
         scratch_shapes=[pltpu.VMEM(tile.shape, jnp.bfloat16)] + conv_scratch(tile),
         compiler_params=LIMITED,
         name="detector_block",
-    )(ints, *map(resident, (tile, params, own, other, *before)))
+    )(*map(resident, (tile, params, own, other, *before)))
 
 
 def selection(top, left):
@@ -224,10 +225,10 @@
     )(ints, tiles)
 
 
-def pick_body(ints_ref, below_ref, above_ref, *refs):
+def pick_body(ints_ref, *refs):
     pairs, out_refs = refs[:3], refs[3:]
 
-    @pl.when(active(ints_ref, len(out_refs) - 1))
+    @pl.when(active(len(out_refs) - 1))
     def _():
         core = ints_ref[CORE_AT]
         for slot, out_ref in enumerate(out_refs):
@@ -235,8 +236,8 @@
             base = slot * 9
 
             def entry(part, source=source, base=base):
-                inner = jnp.where(source == 3, above_ref[base + part], ints_ref[base + 3 + part])
-                return jnp.where(source == 1, below_ref[base + 6 + part], inner)
+                inner = jnp.where(source == 3, ints_ref[2 * INTS + base + part], ints_ref[base + 3 + part])
+                return jnp.where(source == 1, ints_ref[INTS + base + 6 + part], inner)
 
             same_chip = ((source == 1) & (core == 1)) | ((source == 3) & (core == 0))
             away = (source == 1) | (source == 3)
@@ -250,16 +251,16 @@
                     out_ref[...] = rows.astype(jnp.bfloat16)
 
 
-def pick_crops(ints, below, above, pairs, slots):
+def pick_crops(ints, pairs, slots):
     width = pairs[0].shape[2]
     return pl.pallas_call(
         pick_body,
         out_shape=[pltpu.VMEM((PADDED, width), jnp.bfloat16)] * slots,
-        in_specs=[SMEM] * 3 + [VMEM] * len(pairs),
+        in_specs=[SMEM] + [VMEM] * len(pairs),
         out_specs=[VMEM] * slots,
         compiler_params=LIMITED,
         name="pick_crops",
-    )(ints, below, above, *map(resident, pairs))
+    )(ints, *map(resident, pairs))
 
 
 EMBED, MERGE, QUERY = 0, 1536, 2560
@@ -370,11 +371,10 @@
     )(ints, *map(in_hbm, (*pixels, packed)))
 
 
-def classify_body(ints_ref, *refs):
+def classify_body(*refs):
     feat_refs = refs[:4]
-    base_ref, weights, gain_ref, out_ref, feat = refs[4:]
-    place = ints_ref[SECTION_AT]
-    source = ints_ref[SLOT_AT + place]
+    base_ref, weights, gain_ref, source_ref, out_ref, feat = refs[4:]
+    place = lax.axis_index("section")
     sections = weights.shape[0] // 2
     for number, feat_ref in enumerate(feat_refs):
 
@@ -451,19 +451,19 @@
     centred = pooled - pooled_mean
     var = jnp.sum(centred * centred, axis=-1, keepdims=True) / width
     result = centred * lax.rsqrt(var + EPSILON) * gain_ref[pl.ds(1, 1), :]
-    out_ref[...] = jnp.where(source == 0, 0.0, result)
-
-
-def classify(ints, feats, base, weights, gain):
+    out_ref[...] = jnp.where(source_ref[...] == 0, 0.0, result)
+
+
+def classify(source, feats, base, weights, gain):
     return pl.pallas_call(
         classify_body,
         out_shape=jax.ShapeDtypeStruct((1, gain.shape[1]), jnp.float32),
-        in_specs=[SMEM] + [VMEM] * 7,
+        in_specs=[VMEM] * 8,
         out_specs=VMEM,
         scratch_shapes=[pltpu.VMEM(feats[0].shape, jnp.bfloat16)],
         compiler_params=LIMITED,
         name="classify",
-    )(ints, *map(resident, (*feats, base, weights, gain)))
+    )(*map(resident, (*feats, base, weights, gain, source)))
 
 
 def after(value, *others):
@@ -514,8 +514,9 @@
     params = params.reshape(56, slabs, LANES).transpose(1, 0, 2)
     start = tile_features.reshape(2, CELLS, width)
     tiles = [start[0], start[1]]
-    early = early_norm(ints, tiles[0], params)
-    plane = after(plane, below, above, early, *cut)
+    early = early_norm(tiles[0], params)
+    every = jnp.concatenate([ints, below, above])
+    plane = after(plane, every, early, *cut)
     cut = lax.optimization_barrier((*cut, plane))[:3]
     beyond = [(index, index + 1) for index in range(1, count - 1, 2)]
     beyond += [(target, origin) for origin, target in beyond]
@@ -525,12 +526,12 @@
 
     for number in range(sections):
         if number == 0:
-            first = early_block(ints, tiles[0], params, own, other, early)
+            first = early_block(tiles[0], params, own, other, early)
         else:
-            order = after(ints, *pixels) if number == 1 else ints
-            first = detector_block(number, order, tiles[0], params, own, other)
+            tile = after(tiles[0], *pixels) if number == 1 else tiles[0]
+            first = detector_block(number, tile, params, own, other)
         before = (first,) if number == last else ()
-        second = detector_block(number, after(ints, first), tiles[1], params, own, other, *before)
+        second = detector_block(number, after(tiles[1], first), params, own, other, *before)
         if number < last:
             tiles = [lax.ppermute(tile, "section", [(number, number + 1)]) for tile in (first, second)]
 
@@ -538,10 +539,12 @@
     across = [(last * count + origin, last * count + target) for origin, target in beyond]
     far = lax.ppermute(second, ("section",) + REP, across)
     near = lax.ppermute(second, ("section",) + REP, within)
-    crops = pick_crops(after(ints, weights), below, above, (near, second, far), sections)
+    crops = pick_crops(after(every, weights), (near, second, far), sections)
     feats = [lax.ppermute(crops[slot], "section", [(last, slot)]) for slot in range(last)] + [crops[last]]
     weights, base = staged(after(ints, *crops), pixels, weights)
-    result = classify(ints, feats, base, weights, cls_gain)
+    source = lax.dynamic_index_in_dim(slot_from[0], section, 0)
+    source = jnp.broadcast_to(source[None], (1, cls_gain.shape[1]))
+    result = classify(source, feats, base, weights, cls_gain)
     return result[None]
 
 

time: 158 us -> 158 us (level)
  Pallas kernels: 27.4 us -> 21.2 us
  starting transfers between devices: 28.8 us -> 32.1 us
  local copies, waits for them, and re-layouts: 3.34 us -> 5.21 us
    pallas_call x7, Pallas kernels: 12.2 us -> 7.67 us  [detector_block(): pl.pallas_call(functools.partial(block_body, number=number), out_shape=pl...]
    ppermute x1, starting transfers between devices: 1.96 us -> 5.75 us  [per_device(): above = lax.ppermute(ints, REP, downward)]
    ppermute x3, waiting for transfers between devices: 20.6 us -> 23.6 us  [per_device(): lax.ppermute(crops[slot], 'section', [(last, slot)])]
    ppermute x1, waiting for transfers between devices: 15.3 us -> 12.5 us  [per_device(): above = lax.ppermute(ints, REP, downward)]
  transfers between devices with their start and end apart: 18 -> 18, of which waited for: 6 -> 7; matrix products, arithmetic and copies ran while one was open for 2% -> 2% of each run, Pallas kernels for 13% -> 9%
where the time goes in v7:
time: 158 us
  waiting for transfers between devices  64.5 us (41%)
  starting transfers between devices  32.1 us (20%)
  Pallas kernels  21.2 us (13%)
  blocking collectives  20.6 us (13%)
  between operations  13.9 us (9%)
  local copies, waits for them, and re-layouts  5.21 us (3%)
    ppermute x3, waiting for transfers between devices, per_device(): lax.ppermute(crops[slot], 'section', [(last, slot)])  23.6 us
    all_to_all x1, blocking collectives, spread_in_groups(): return lax.all_to_all(copies, REP, 0, 0, axis_index_groups=groups)  20.6 us
    ppermute x6, waiting for transfers between devices, per_device(): lax.ppermute(tile, 'section', [(number, number + 1)])  16.5 us
    ppermute x1, waiting for transfers between devices, per_device(): above = lax.ppermute(ints, REP, downward)  12.5 us
    all_to_all x1, starting transfers between devices, spread_in_groups(): return lax.all_to_all(copies, REP, 0, 0, axis_index_groups=groups)  7.69 us
    pallas_call x7, Pallas kernels, detector_block(): pl.pallas_call(functools.partial(block_body, number=number), out_shape=pl...  7.67 us
    ppermute x1, waiting for transfers between devices, per_device(): lax.ppermute(cut[2], REP, beyond)  7.04 us
    ppermute x6, starting transfers between devices, per_device(): lax.ppermute(tile, 'section', [(number, number + 1)])  6.54 us
  transfers between devices with their start and end apart: 18, of which 7 were waited for; matrix products, arithmetic and copies ran while one was open for 2% of the time, Pallas kernels for 9%

profile of v7, /device:TPU:12, one launch (start us, length us, event | category | flops | bytes accessed | tf_op | source)
XLA Modules:
  0.0 157.7 jit_solution(5920472767266211499)
XLA Ops:
  6.5 0.0 all-gather.3.cloned.1.call-start
  6.5 2.2 %pack_weights.1 = bf16[3584,128]{1,0:T(8,128)(2,1)} custom-call(s32[1]{0:T(128)} %bitcast.2.parity_ref, bf16[768,256]{1,0:T(8,128)(2,1)} %embed.1, bf16[512,256]{1,0:T(8,128)(2,1)} %merge.1, bf16[196,256]{1,0:T(8,128)(2,1)} %pos.1, bf16[3,1024,128]{2,1,0:T(8,128)(2,1)} %bitcast.35, bf16[128,1024]{1,0:T(8,128)(2,1)} %out.1), custom_call_target="tpu_custom_call" | custom-call | tf_op jit(solution)/shard_map/pack_weights/pallas_call | solution.py:304
  8.7 0.0 all-gather.3.cloned.1.call-update
  8.8 0.0 copy-done.8
  8.8 20.6 %all_to_all.10 = bf16[8,2,16,512]{3,2,1,0:T(8,128)(2,1)S(1)} all-to-all(bf16[8,2,16,512]{3,2,1,0:T(8,128)(2,1)S(1)} %broadcast_in_dim.13), channel_id=1, replica_groups={{0,2,4,6,8,10,12,14},{16,18,20,22,24,26,28,30},{32,34,36,38,40,42,44,46..., dimensions={0} | all-to-all | bytes 524288 | tf_op jit(solution)/shard_map/all_to_all | solution.py:48
  29.4 1.7 %broadcast_in_dim.28 = bf16[8,8,2,16,512]{4,3,2,1,0:T(8,128)(2,1)} broadcast(bf16[8,2,16,512]{3,2,1,0:T(8,128)(2,1)S(1)} %all_to_all.10), dimensions={1,2,3,4} | broadcast | bytes 2359296 | tf_op jit(solution)/shard_map/broadcast_in_dim | solution.py:47
  31.1 0.0 copy-start.10
  31.1 0.0 copy-start.11
  31.1 7.7 %all-to-all-start.1 = ((bf16[8,8,2,16,512]{4,3,2,1,0:T(8,128)(2,1)}), bf16[8,8,2,16,512]{4,3,2,1,0:T(8,128)(2,1)S(1)}, u32[]{:S(2)}, u32[]{:S(2)}) async-start(bf16[8,8,2,16,512]{4,3,2,1,0:T(8,128)(2,1)} %broadcast_in_dim.28), calls=%async_computation.1 | async-start | bytes 4194304 | tf_op jit(solution)/shard_map/all_to_all | solution.py:48
  38.8 0.1 copy.17
  38.9 0.1 reshape.36
  39.0 0.1 pad_add_fusion.ints_ref
  39.1 1.9 %collective-permute-start = (s32[42]{0:T(128)S(1)}, s32[42]{0:T(128)S(1)}, u32[]{:S(2)}, u32[]{:S(2)}) collective-permute-start(s32[42]{0:T(128)S(1)} %pad_add_fusion.ints_ref), channel_id=1, source_target_pairs={{0,1},{1,2},{2,3},{3,4},{4,5},{5,6},{6,7},{7,8},{8,9},{9,10},{10,1... | collective-permute-start | bytes 512 | tf_op jit(solution)/shard_map/ppermute | solution.py:509
  41.0 5.8 %collective-permute-start.1 = (s32[42]{0:T(128)S(1)}, s32[42]{0:T(128)S(1)}, u32[]{:S(2)}, u32[]{:S(2)}) collective-permute-start(s32[42]{0:T(128)S(1)} %pad_add_fusion.ints_ref), channel_id=1, source_target_pairs={{1,0},{2,1},{3,2},{4,3},{5,4},{6,5},{7,6},{8,7},{9,8},{10,9},{11,1... | collective-permute-start | bytes 512 | tf_op jit(solution)/shard_map/ppermute | solution.py:510
  46.8 2.0 %cut_pixels.1 = (bf16[208,768]{1,0:T(8,128)(2,1)S(1)}, bf16[208,768]{1,0:T(8,128)(2,1)S(1)}, bf16[208,768]{1,0:T(8,128)(2,1)S(1)}) custom-call(s32[42]{0:T(128)S(1)} %pad_add_fusion.ints_ref, bf16[2,256,768]{2,1,0:T(8,128)(2,1)S(1)} %bitcast.33), custom_call_target="tpu_custom_call" | custom-call | tf_op jit(solution)/shard_map/cut_pixels/pallas_call | solution.py:217
  48.8 0.0 copy-start.1
  48.8 0.0 copy-start.3
  48.8 0.0 copy-done.6
  48.9 0.1 pad.5.clone
  48.9 0.0 copy-done.11
  48.9 0.1 maximum_bitcast_fusion.param_ref
  49.0 1.1 fusion
  50.2 0.0 collective-permute-done
  50.2 12.5 %collective-permute-done.1 = s32[42]{0:T(128)S(1)} collective-permute-done((s32[42]{0:T(128)S(1)}, s32[42]{0:T(128)S(1)}, u32[]{:S(2)}, u32[]{:S(2)}) %collective-permute-start.1) | collective-permute-done | bytes 200 | tf_op jit(solution)/shard_map/ppermute | solution.py:510
  62.7 0.1 concatenate.18.ints_ref
  62.8 4.8 %all-to-all-done.1 = bf16[8,8,2,16,512]{4,3,2,1,0:T(8,128)(2,1)S(1)} async-done(((bf16[8,8,2,16,512]{4,3,2,1,0:T(8,128)(2,1)}), bf16[8,8,2,16,512]{4,3,2,1,0:T(8,128)(2,1)S(1)}, u32[]{:S(2)}, u32[]{:S(2)}) %all-to-all-start.1) | async-done | bytes 2097184 | tf_op jit(solution)/shard_map/all_to_all | solution.py:48
  67.6 1.9 %collective-permute-start.2 = (bf16[64,2,16,512]{3,2,1,0:T(8,128)(2,1)S(1)}, bf16[64,2,16,512]{3,2,1,0:T(8,128)(2,1)S(1)}, u32[]{:S(2)}, u32[]{:S(2)}) collective-permute-start(bf16[64,2,16,512]{3,2,1,0:T(8,128)(2,1)S(1)} %bitcast.21), channel_id=1, source_target_pairs={{0,1},{1,0},{2,3},{3,2},{4,5},{5,4},{6,7},{7,6},{8,9},{9,8},{10,11... | collective-permute-start | bytes 6291464 | tf_op jit(solution)/shard_map/ppermute | solution.py:525
  69.5 2.4 %collective-permute-start.5 = (bf16[208,768]{1,0:T(8,128)(2,1)}, bf16[208,768]{1,0:T(8,128)(2,1)S(1)}, u32[]{:S(2)}, u32[]{:S(2)}) collective-permute-start(bf16[208,768]{1,0:T(8,128)(2,1)} %copy-done.3), channel_id=1, source_target_pairs={{0,1},{1,0},{2,3},{3,2},{4,5},{5,4},{6,7},{7,6},{8,9},{9,8},{10,11... | collective-permute-start | bytes 958472 | tf_op jit(solution)/shard_map/ppermute | solution.py:523
  71.9 1.9 %collective-permute-start.6 = (bf16[208,768]{1,0:T(8,128)(2,1)S(1)}, bf16[208,768]{1,0:T(8,128)(2,1)S(1)}, u32[]{:S(2)}, u32[]{:S(2)}) collective-permute-start(bf16[208,768]{1,0:T(8,128)(2,1)S(1)} %get-tuple-element.35), channel_id=1, source_target_pairs={{1,2},{3,4},{5,6},{7,8},{9,10},{11,12},{13,14},{15,16},{17,18},{19... | collective-permute-start | bytes 958472 | tf_op jit(solution)/shard_map/ppermute | solution.py:523
  73.8 0.0 collective-permute-done.2.other_ref
  73.8 0.7 collective-permute-start.4
  74.6 0.7 collective-permute-start.3
  75.2 0.0 collective-permute-done.5.pix_near
  75.3 0.0 copy-start.4
  75.3 7.0 %collective-permute-done.6.pix_far = bf16[208,768]{1,0:T(8,128)(2,1)S(1)} collective-permute-done((bf16[208,768]{1,0:T(8,128)(2,1)S(1)}, bf16[208,768]{1,0:T(8,128)(2,1)S(1)}, u32[]{:S(2)}, u32[]{:S(2)}) %collective-permute-start.6) | collective-permute-done | bytes 319520 | tf_op jit(solution)/shard_map/ppermute | solution.py:523
  82.3 0.0 collective-permute-done.4.tile_ref
  82.3 0.8 copy-done.5
  83.1 1.3 collective-permute-start.8
  84.3 0.0 collective-permute-done.3.tile_ref
  84.4 1.3 collective-permute-start.7
  85.7 10.9 %collective-permute-done.8.tile_ref = bf16[256,512]{1,0:T(8,128)(2,1)S(1)} collective-permute-done((bf16[256,512]{1,0:T(8,128)(2,1)S(1)}, bf16[256,512]{1,0:T(8,128)(2,1)S(1)}, u32[]{:S(2)}, u32[]{:S(2)}) %collective-permute-start.8) | collective-permute-done | bytes 262176 | tf_op jit(solution)/shard_map/ppermute | solution.py:536
  96.5 3.8 %detector_block.10 = bf16[256,512]{1,0:T(8,128)(2,1)S(1)} custom-call(bf16[256,512]{1,0:T(8,128)(2,1)S(1)} %collective-permute-done.8.tile_ref, f32[4,56,128]{2,1,0:T(8,128)S(1)} %maximum_bitcast_fusion.param_ref, bf16[64,2,16,512]{3,2,1,0:T(8,128)(2,1)S(1)} %bitcast.26, bf16[64,2,16,512]{3,2,1,0:T(8,128)(2,1)S(1)} %collective-permute-done.2.other_ref), custom_call_target="tpu_custom_call" | custom-call | tf_op jit(solution)/shard_map/detector_block/pallas_call | solution.py:181
  100.4 1.3 collective-permute-start.10
  101.7 0.5 collective-permute-done.7.tile_ref
  102.2 3.8 %detector_block.11 = bf16[256,512]{1,0:T(8,128)(2,1)S(1)} custom-call(bf16[256,512]{1,0:T(8,128)(2,1)S(1)} %collective-permute-done.7.tile_ref, f32[4,56,128]{2,1,0:T(8,128)S(1)} %maximum_bitcast_fusion.param_ref, bf16[64,2,16,512]{3,2,1,0:T(8,128)(2,1)S(1)} %bitcast.27, bf16[64,2,16,512]{3,2,1,0:T(8,128)(2,1)S(1)} %collective-permute-done.2.other_ref), custom_call_target="tpu_custom_call" | custom-call | tf_op jit(solution)/shard_map/detector_block/pallas_call | solution.py:181
  106.0 1.3 collective-permute-start.9
  107.3 0.0 collective-permute-done.10.tile_ref
  107.3 5.2 %collective-permute-done.9.tile_ref = bf16[256,512]{1,0:T(8,128)(2,1)S(1)} collective-permute-done((bf16[256,512]{1,0:T(8,128)(2,1)S(1)}, bf16[256,512]{1,0:T(8,128)(2,1)S(1)}, u32[]{:S(2)}, u32[]{:S(2)}) %collective-permute-start.9) | collective-permute-done | bytes 262176 | tf_op jit(solution)/shard_map/ppermute | solution.py:536
  112.5 0.7 collective-permute-start.11
  113.2 0.7 collective-permute-start.12
  113.9 0.0 all-gather.3.cloned.1.call-done
  113.9 0.0 collective-permute-done.11.refs_0_
  114.0 0.0 collective-permute-done.12.refs_2_
  114.0 0.6 pick_crops.1
  114.5 0.7 collective-permute-start.13
  115.2 0.7 collective-permute-start.14
  115.9 1.3 collective-permute-start.15
  117.2 0.6 constant_dynamic-slice_fusion
  117.8 4.8 %stage_weights.1 = (bf16[8,3584,128]{2,1,0:T(8,128)(2,1)S(1)}, f32[208,1024]{1,0:T(8,128)S(1)}) custom-call(s32[42]{0:T(128)S(1)} %pad_add_fusion.ints_ref, bf16[208,768]{1,0:T(8,128)(2,1)} %copy-done.4, bf16[208,768]{1,0:T(8,128)(2,1)} %copy-done.1, bf16[208,768]{1,0:T(8,128)(2,1)} %copy-done.5, bf16[8,3584,128]{2,1,0:T(8,128)(2,1)} %bitcast.34), custom_call_target="tpu_custom_call" | custom-call | tf_op jit(solution)/shard_map/stage_weights/pallas_call | solution.py:360
  122.6 0.0 collective-permute-done.13.refs_0_
  122.6 0.0 collective-permute-done.14.refs_1_
  122.6 23.6 %collective-permute-done.15.refs_2_ = bf16[208,512]{1,0:T(8,128)(2,1)S(1)} collective-permute-done((bf16[208,512]{1,0:T(8,128)(2,1)S(1)}, bf16[208,512]{1,0:T(8,128)(2,1)S(1)}, u32[]{:S(2)}, u32[]{:S(2)}) %collective-permute-start.15) | collective-permute-done | bytes 213024 | tf_op jit(solution)/shard_map/ppermute | solution.py:543
  146.2 0.6 broadcast_in_dim.30.refs_7_
  146.9 4.0 %classify.1 = f32[1,1024]{1,0:T(1,128)} custom-call(bf16[208,512]{1,0:T(8,128)(2,1)S(1)} %collective-permute-done.13.refs_0_, bf16[208,512]{1,0:T(8,128)(2,1)S(1)} %collective-permute-done.14.refs_1_, bf16[208,512]{1,0:T(8,128)(2,1)S(1)} %collective-permute-done.15.refs_2_, bf16[208,512]{1,0:T(8,128)(2,1)S(1)} %get-tuple-element.43.refs_3_, ...), custom_call_target="tpu_custom_call" | custom-call | tf_op jit(solution)/shard_map/classify/pallas_call | solution.py:458
  (28 shorter events, 0.2 us)
Async XLA Ops:
  6.5 2.2 %copy-start.8 = (bf16[1,512,16]{1,2,0:T(8,128)(2,1)S(1)}, bf16[1,512,16]{1,2,0:T(8,128)(2,1)}, u32[]{:S(2)}) copy-start(bf16[1,512,16]{1,2,0:T(8,128)(2,1)} %param.19) | copy-start | bytes 49156
  6.5 2.2 %copy-start.7 = (bf16[1,16,512]{2,1,0:T(8,128)(2,1)S(1)}, bf16[1,16,512]{2,1,0:T(8,128)(2,1)}, u32[]{:S(2)}) copy-start(bf16[1,16,512]{2,1,0:T(8,128)(2,1)} %param.20) | copy-start | bytes 49156
  6.5 107.4 %all-gather.3.cloned.1.call-start = ((), (), s32[]{:S(2)}) async-start(), calls=%async_computation.2 | async-start | bytes 8257536 | tf_op jit(solution)/shard_map/all_gather | solution.py:503
  31.1 7.7 %copy-start.9 = (s32[1,4,3,3]{1,0,3,2:T(1,128)S(1)}, s32[1,4,3,3]{1,0,3,2:T(1,128)}, u32[]{:S(2)}) copy-start(s32[1,4,3,3]{1,0,3,2:T(1,128)} %param.28) | copy-start | bytes 436
  31.1 7.9 %copy-start.12 = (s32[1,4]{1,0:T(1,128)S(1)}, s32[1,4]{1,0:T(1,128)}, u32[]{:S(2)}) copy-start(s32[1,4]{1,0:T(1,128)} %param.29) | copy-start | bytes 52
  31.1 15.7 %copy-start = (bf16[2,16,16,768]{3,2,1,0:T(8,128)(2,1)S(1)}, bf16[2,16,16,768]{3,2,1,0:T(8,128)(2,1)}, u32[]{:S(2)}) copy-start(bf16[2,16,16,768]{3,2,1,0:T(8,128)(2,1)} %param.16) | copy-start | bytes 2359300
  31.1 17.7 %copy-start.6 = (f32[1,7,7,512]{3,0,2,1:T(1,128)S(1)}, f32[1,7,7,512]{3,0,2,1:T(1,128)}, u32[]{:S(2)}) copy-start(f32[1,7,7,512]{3,0,2,1:T(1,128)} %param.17) | copy-start | bytes 301060
  31.1 17.8 %copy-start.10 = (f32[1,512]{1,0:T(1,128)S(1)}, f32[1,512]{1,0:T(1,128)}, u32[]{:S(2)}) copy-start(f32[1,512]{1,0:T(1,128)} %param.21) | copy-start | bytes 6148
  31.1 17.8 %copy-start.11 = (f32[1,512]{1,0:T(1,128)S(1)}, f32[1,512]{1,0:T(1,128)}, u32[]{:S(2)}) copy-start(f32[1,512]{1,0:T(1,128)} %param.18) | copy-start | bytes 6148
  31.1 36.4 %all-to-all-start.1 = ((bf16[8,8,2,16,512]{4,3,2,1,0:T(8,128)(2,1)}), bf16[8,8,2,16,512]{4,3,2,1,0:T(8,128)(2,1)S(1)}, u32[]{:S(2)}, u32[]{:S(2)}) async-start(bf16[8,8,2,16,512]{4,3,2,1,0:T(8,128)(2,1)} %broadcast_in_dim.28), calls=%async_computation.1 | async-start | bytes 4194304 | tf_op jit(solution)/shard_map/all_to_all | solution.py:48
  39.1 11.1 %collective-permute-start = (s32[42]{0:T(128)S(1)}, s32[42]{0:T(128)S(1)}, u32[]{:S(2)}, u32[]{:S(2)}) collective-permute-start(s32[42]{0:T(128)S(1)} %pad_add_fusion.ints_ref), channel_id=1, source_target_pairs={{0,1},{1,2},{2,3},{3,4},{4,5},{5,6},{6,7},{7,8},{8,9},{9,10},{10,1... | collective-permute-start | bytes 512 | tf_op jit(solution)/shard_map/ppermute | solution.py:509
  41.0 21.7 %collective-permute-start.1 = (s32[42]{0:T(128)S(1)}, s32[42]{0:T(128)S(1)}, u32[]{:S(2)}, u32[]{:S(2)}) collective-permute-start(s32[42]{0:T(128)S(1)} %pad_add_fusion.ints_ref), channel_id=1, source_target_pairs={{1,0},{2,1},{3,2},{4,3},{5,4},{6,5},{7,6},{8,7},{9,8},{10,9},{11,1... | collective-permute-start | bytes 512 | tf_op jit(solution)/shard_map/ppermute | solution.py:510
  48.8 1.3 copy-start.1
  48.8 1.4 copy-start.3
  67.6 6.3 %collective-permute-start.2 = (bf16[64,2,16,512]{3,2,1,0:T(8,128)(2,1)S(1)}, bf16[64,2,16,512]{3,2,1,0:T(8,128)(2,1)S(1)}, u32[]{:S(2)}, u32[]{:S(2)}) collective-permute-start(bf16[64,2,16,512]{3,2,1,0:T(8,128)(2,1)S(1)} %bitcast.21), channel_id=1, source_target_pairs={{0,1},{1,0},{2,3},{3,2},{4,5},{5,4},{6,7},{7,6},{8,9},{9,8},{10,11... | collective-permute-start | bytes 6291464 | tf_op jit(solution)/shard_map/ppermute | solution.py:525
  69.5 5.8 %collective-permute-start.5 = (bf16[208,768]{1,0:T(8,128)(2,1)}, bf16[208,768]{1,0:T(8,128)(2,1)S(1)}, u32[]{:S(2)}, u32[]{:S(2)}) collective-permute-start(bf16[208,768]{1,0:T(8,128)(2,1)} %copy-done.3), channel_id=1, source_target_pairs={{0,1},{1,0},{2,3},{3,2},{4,5},{5,4},{6,7},{7,6},{8,9},{9,8},{10,11... | collective-permute-start | bytes 958472 | tf_op jit(solution)/shard_map/ppermute | solution.py:523
  71.9 10.4 %collective-permute-start.6 = (bf16[208,768]{1,0:T(8,128)(2,1)S(1)}, bf16[208,768]{1,0:T(8,128)(2,1)S(1)}, u32[]{:S(2)}, u32[]{:S(2)}) collective-permute-start(bf16[208,768]{1,0:T(8,128)(2,1)S(1)} %get-tuple-element.35), channel_id=1, source_target_pairs={{1,2},{3,4},{5,6},{7,8},{9,10},{11,12},{13,14},{15,16},{17,18},{19... | collective-permute-start | bytes 958472 | tf_op jit(solution)/shard_map/ppermute | solution.py:523
  73.8 8.5 %collective-permute-start.4 = (bf16[256,512]{1,0:T(8,128)(2,1)S(1)}, bf16[256,512]{1,0:T(8,128)(2,1)S(1)}, u32[]{:S(2)}, u32[]{:S(2)}) collective-permute-start(bf16[256,512]{1,0:T(8,128)(2,1)S(1)} %early_block.1), channel_id=1, source_target_pairs={{0,128},{1,129},{2,130},{3,131},{4,132},{5,133},{6,134},{7,135},{8... | collective-permute-start | bytes 786440 | tf_op jit(solution)/shard_map/ppermute | solution.py:536
  74.6 9.8 %collective-permute-start.3 = (bf16[256,512]{1,0:T(8,128)(2,1)S(1)}, bf16[256,512]{1,0:T(8,128)(2,1)S(1)}, u32[]{:S(2)}, u32[]{:S(2)}) collective-permute-start(bf16[256,512]{1,0:T(8,128)(2,1)S(1)} %detector_block.7), channel_id=1, source_target_pairs={{0,128},{1,129},{2,130},{3,131},{4,132},{5,133},{6,134},{7,135},{8... | collective-permute-start | bytes 786440 | tf_op jit(solution)/shard_map/ppermute | solution.py:536
  75.3 7.1 %copy-start.4 = (bf16[208,768]{1,0:T(8,128)(2,1)}, bf16[208,768]{1,0:T(8,128)(2,1)S(1)}, u32[]{:S(2)}) copy-start(bf16[208,768]{1,0:T(8,128)(2,1)S(1)} %collective-permute-done.5.pix_near) | copy-start | bytes 958468
  82.3 0.8 copy-start.5
  83.1 13.5 %collective-permute-start.8 = (bf16[256,512]{1,0:T(8,128)(2,1)S(1)}, bf16[256,512]{1,0:T(8,128)(2,1)S(1)}, u32[]{:S(2)}, u32[]{:S(2)}) collective-permute-start(bf16[256,512]{1,0:T(8,128)(2,1)S(1)} %detector_block.8), channel_id=1, source_target_pairs={{128,256},{129,257},{130,258},{131,259},{132,260},{133,261},{134,2... | collective-permute-start | bytes 786440 | tf_op jit(solution)/shard_map/ppermute | solution.py:536
  84.4 17.8 %collective-permute-start.7 = (bf16[256,512]{1,0:T(8,128)(2,1)S(1)}, bf16[256,512]{1,0:T(8,128)(2,1)S(1)}, u32[]{:S(2)}, u32[]{:S(2)}) collective-permute-start(bf16[256,512]{1,0:T(8,128)(2,1)S(1)} %detector_block.9), channel_id=1, source_target_pairs={{128,256},{129,257},{130,258},{131,259},{132,260},{133,261},{134,2... | collective-permute-start | bytes 786440 | tf_op jit(solution)/shard_map/ppermute | solution.py:536
  100.4 6.9 %collective-permute-start.10 = (bf16[256,512]{1,0:T(8,128)(2,1)S(1)}, bf16[256,512]{1,0:T(8,128)(2,1)S(1)}, u32[]{:S(2)}, u32[]{:S(2)}) collective-permute-start(bf16[256,512]{1,0:T(8,128)(2,1)S(1)} %detector_block.10), channel_id=1, source_target_pairs={{256,384},{257,385},{258,386},{259,387},{260,388},{261,389},{262,3... | collective-permute-start | bytes 786440 | tf_op jit(solution)/shard_map/ppermute | solution.py:536
  106.0 6.6 %collective-permute-start.9 = (bf16[256,512]{1,0:T(8,128)(2,1)S(1)}, bf16[256,512]{1,0:T(8,128)(2,1)S(1)}, u32[]{:S(2)}, u32[]{:S(2)}) collective-permute-start(bf16[256,512]{1,0:T(8,128)(2,1)S(1)} %detector_block.11), channel_id=1, source_target_pairs={{256,384},{257,385},{258,386},{259,387},{260,388},{261,389},{262,3... | collective-permute-start | bytes 786440 | tf_op jit(solution)/shard_map/ppermute | solution.py:536
  112.5 1.4 collective-permute-start.11
  113.2 0.7 collective-permute-start.12
  114.5 8.0 %collective-permute-start.13 = (bf16[208,512]{1,0:T(8,128)(2,1)S(1)}, bf16[208,512]{1,0:T(8,128)(2,1)S(1)}, u32[]{:S(2)}, u32[]{:S(2)}) collective-permute-start(bf16[208,512]{1,0:T(8,128)(2,1)S(1)} %get-tuple-element.40), channel_id=1, source_target_pairs={{384,0},{385,1},{386,2},{387,3},{388,4},{389,5},{390,6},{391,7},{3... | collective-permute-start | bytes 638984 | tf_op jit(solution)/shard_map/ppermute | solution.py:543
  115.2 7.4 %collective-permute-start.14 = (bf16[208,512]{1,0:T(8,128)(2,1)S(1)}, bf16[208,512]{1,0:T(8,128)(2,1)S(1)}, u32[]{:S(2)}, u32[]{:S(2)}) collective-permute-start(bf16[208,512]{1,0:T(8,128)(2,1)S(1)} %get-tuple-element.41), channel_id=1, source_target_pairs={{384,128},{385,129},{386,130},{387,131},{388,132},{389,133},{390,1... | collective-permute-start | bytes 638984 | tf_op jit(solution)/shard_map/ppermute | solution.py:543
  115.9 30.3 %collective-permute-start.15 = (bf16[208,512]{1,0:T(8,128)(2,1)S(1)}, bf16[208,512]{1,0:T(8,128)(2,1)S(1)}, u32[]{:S(2)}, u32[]{:S(2)}) collective-permute-start(bf16[208,512]{1,0:T(8,128)(2,1)S(1)} %get-tuple-element.42), channel_id=1, source_target_pairs={{384,256},{385,257},{386,258},{387,259},{388,260},{389,261},{390,2... | collective-permute-start | bytes 638984 | tf_op jit(solution)/shard_map/ppermute | solution.py:543
  117.8 29.1 %copy-start.2 = (f32[2,1024]{1,0:T(2,128)S(1)}, f32[2,1024]{1,0:T(2,128)}, u32[]{:S(2)}) copy-start(f32[2,1024]{1,0:T(2,128)} %refs_6_.1) | copy-start | bytes 24580
Sparse Core Ops, SparseCore 0:
  9.5 54.0 all-gather.2

commit v8 on v7

--- a/solution.py
+++ b/solution.py
@@ -153,16 +153,16 @@
 
 
 def block_body(tile_ref, param_ref, own_ref, other_ref, *refs, number):
-    before, (out_ref, normed, wide, conv) = refs[:-4], refs[-4:]
+    rest, (out_ref, normed, wide, conv) = refs[:-4], refs[-4:]
 
     @pl.when(active(number))
     def _():
         conv_norm(tile_ref, param_ref, normed, wide, conv)
-        result_ref = out_ref
-        if before:
-            out_ref[0] = before[0][...]
-            result_ref = out_ref.at[1]
-        mlp(normed, own_ref, other_ref, tile_ref, param_ref, result_ref)
+        mlp(normed, own_ref, other_ref, tile_ref, param_ref, out_ref)
+        if rest:
+            before_ref, pair_ref = rest
+            pair_ref[0] = before_ref[...]
+            pair_ref[1] = out_ref[...]
 
 
 def early_block(tile, params, own, other, normed):
@@ -177,12 +177,13 @@
 
 
 def detector_block(number, tile, params, own, other, *before):
-    shape = (2,) + tile.shape if before else tile.shape
+    out_shape = [pltpu.VMEM((2,) + tile.shape, jnp.bfloat16)] * len(before)
+    out_shape += [pltpu.VMEM(tile.shape, jnp.bfloat16)]
     return pl.pallas_call(
         functools.partial(block_body, number=number),
-        out_shape=pltpu.VMEM(shape, jnp.bfloat16),
+        out_shape=out_shape,
         in_specs=[VMEM] * (4 + len(before)),
-        out_specs=VMEM,
+        out_specs=[VMEM] * len(out_shape),
         scratch_shapes=[pltpu.VMEM(tile.shape, jnp.bfloat16)] + conv_scratch(tile),
         compiler_params=LIMITED,
         name="detector_block",
@@ -226,7 +227,7 @@
 
 
 def pick_body(ints_ref, *refs):
-    pairs, out_refs = refs[:3], refs[3:]
+    pairs, far_refs, out_refs = refs[:2], refs[2:4], refs[4:]
 
     @pl.when(active(len(out_refs) - 1))
     def _():
@@ -243,7 +244,14 @@
             away = (source == 1) | (source == 3)
             micro = entry(0)
             chosen = selection(entry(1), entry(2))
-            for pair, wanted in zip(pairs, (same_chip, ~away, away & ~same_chip)):
+            for index, far_ref in enumerate(far_refs):
+
+                @pl.when(away & ~same_chip & (micro == index))
+                def _(chosen=chosen, far_ref=far_ref, out_ref=out_ref):
+                    rows = jnp.dot(chosen, far_ref[...], preferred_element_type=jnp.float32)
+                    out_ref[...] = rows.astype(jnp.bfloat16)
+
+            for pair, wanted in zip(pairs, (same_chip, ~away)):
 
                 @pl.when(wanted)
                 def _(chosen=chosen, pair=pair, micro=micro, out_ref=out_ref):
@@ -252,7 +260,7 @@
 
 
 def pick_crops(ints, pairs, slots):
-    width = pairs[0].shape[2]
+    width = pairs[-1].shape[1]
     return pl.pallas_call(
         pick_body,
         out_shape=[pltpu.VMEM((PADDED, width), jnp.bfloat16)] * slots,
@@ -516,7 +524,9 @@
     tiles = [start[0], start[1]]
     early = early_norm(tiles[0], params)
     every = jnp.concatenate([ints, below, above])
-    plane = after(plane, every, early, *cut)
+    source = lax.dynamic_index_in_dim(slot_from[0], section, 0)
+    source = jnp.broadcast_to(source[None], (1, cls_gain.shape[1]))
+    plane, source = lax.optimization_barrier((plane, source, every, early, *cut))[:2]
     cut = lax.optimization_barrier((*cut, plane))[:3]
     beyond = [(index, index + 1) for index in range(1, count - 1, 2)]
     beyond += [(target, origin) for origin, target in beyond]
@@ -529,21 +539,20 @@
             first = early_block(tiles[0], params, own, other, early)
         else:
             tile = after(tiles[0], *pixels) if number == 1 else tiles[0]
-            first = detector_block(number, tile, params, own, other)
+            (first,) = detector_block(number, tile, params, own, other)
         before = (first,) if number == last else ()
-        second = detector_block(number, after(tiles[1], first), params, own, other, *before)
+        *pair, second = detector_block(number, after(tiles[1], first), params, own, other, *before)
         if number < last:
             tiles = [lax.ppermute(tile, "section", [(number, number + 1)]) for tile in (first, second)]
 
     within = [(last * count + origin, last * count + target) for origin, target in swap]
     across = [(last * count + origin, last * count + target) for origin, target in beyond]
-    far = lax.ppermute(second, ("section",) + REP, across)
-    near = lax.ppermute(second, ("section",) + REP, within)
-    crops = pick_crops(after(every, weights), (near, second, far), sections)
+    far_first = lax.ppermute(first, ("section",) + REP, across)
+    far_second = lax.ppermute(after(second, far_first), ("section",) + REP, across)
+    near = lax.ppermute(pair[0], ("section",) + REP, within)
+    crops = pick_crops(after(every, weights), (near, pair[0], far_first, far_second), sections)
     feats = [lax.ppermute(crops[slot], "section", [(last, slot)]) for slot in range(last)] + [crops[last]]
     weights, base = staged(after(ints, *crops), pixels, weights)
-    source = lax.dynamic_index_in_dim(slot_from[0], section, 0)
-    source = jnp.broadcast_to(source[None], (1, cls_gain.shape[1]))
     result = classify(source, feats, base, weights, cls_gain)
     return result[None]
 

time: 158 us -> 157 us (level)
  starting transfers between devices: 32.1 us -> 29.5 us
    ppermute x1, starting transfers between devices: 5.75 us -> 1.96 us  [per_device(): above = lax.ppermute(ints, REP, downward)]
    ppermute x1, waiting for transfers between devices: 12.5 us -> 15.2 us  [per_device(): above = lax.ppermute(ints, REP, downward)]
    ppermute x3, waiting for transfers between devices: 23.6 us -> 21.5 us  [per_device(): lax.ppermute(crops[slot], 'section', [(last, slot)])]
  transfers between devices with their start and end apart: 18 -> 19, of which waited for: 7 -> 7; matrix products, arithmetic and copies ran while one was open for 2% -> 3% of each run, Pallas kernels for 9% -> 10%
where the time goes in v8:
time: 157 us; the launch traced here: 156 us
  waiting for transfers between devices  64.8 us (41%)
  starting transfers between devices  29.5 us (19%)
  Pallas kernels  21.8 us (14%)
  blocking collectives  20.6 us (13%)
  between operations  13.8 us (9%)
  local copies, waits for them, and re-layouts  5.32 us (3%)
    ppermute x3, waiting for transfers between devices, per_device(): lax.ppermute(crops[slot], 'section', [(last, slot)])  21.5 us
    all_to_all x1, blocking collectives, spread_in_groups(): return lax.all_to_all(copies, REP, 0, 0, axis_index_groups=groups)  20.6 us
    ppermute x6, waiting for transfers between devices, per_device(): lax.ppermute(tile, 'section', [(number, number + 1)])  16.2 us
    ppermute x1, waiting for transfers between devices, per_device(): above = lax.ppermute(ints, REP, downward)  15.2 us
    pallas_call x7, Pallas kernels, detector_block(): pl.pallas_call(functools.partial(block_body, number=number), out_shape=ou...  8.25 us
    all_to_all x1, starting transfers between devices, spread_in_groups(): return lax.all_to_all(copies, REP, 0, 0, axis_index_groups=groups)  7.69 us
    ppermute x1, waiting for transfers between devices, per_device(): lax.ppermute(cut[2], REP, beyond)  7.04 us
    ppermute x6, starting transfers between devices, per_device(): lax.ppermute(tile, 'section', [(number, number + 1)])  6.54 us
  transfers between devices with their start and end apart: 19, of which 7 were waited for; matrix products, arithmetic and copies ran while one was open for 3% of the time, Pallas kernels for 10%

profile of v8, /device:TPU:12, one launch (start us, length us, event | category | flops | bytes accessed | tf_op | source)
XLA Modules:
  0.0 156.0 jit_solution(16024637835949415061)
XLA Ops:
  6.5 0.0 all-gather.3.cloned.1.call-start
  6.5 2.2 %pack_weights.1 = bf16[3584,128]{1,0:T(8,128)(2,1)} custom-call(s32[1]{0:T(128)} %bitcast.2.parity_ref, bf16[768,256]{1,0:T(8,128)(2,1)} %embed.1, bf16[512,256]{1,0:T(8,128)(2,1)} %merge.1, bf16[196,256]{1,0:T(8,128)(2,1)} %pos.1, bf16[3,1024,128]{2,1,0:T(8,128)(2,1)} %bitcast.35, bf16[128,1024]{1,0:T(8,128)(2,1)} %out.1), custom_call_target="tpu_custom_call" | custom-call | tf_op jit(solution)/shard_map/pack_weights/pallas_call | solution.py:312
  8.7 0.0 all-gather.3.cloned.1.call-update
  8.8 0.0 copy-done.7
  8.8 20.6 %all_to_all.10 = bf16[8,2,16,512]{3,2,1,0:T(8,128)(2,1)S(1)} all-to-all(bf16[8,2,16,512]{3,2,1,0:T(8,128)(2,1)S(1)} %broadcast_in_dim.13), channel_id=1, replica_groups={{0,2,4,6,8,10,12,14},{16,18,20,22,24,26,28,30},{32,34,36,38,40,42,44,46..., dimensions={0} | all-to-all | bytes 524288 | tf_op jit(solution)/shard_map/all_to_all | solution.py:48
  29.4 1.7 %broadcast_in_dim.28 = bf16[8,8,2,16,512]{4,3,2,1,0:T(8,128)(2,1)} broadcast(bf16[8,2,16,512]{3,2,1,0:T(8,128)(2,1)S(1)} %all_to_all.10), dimensions={1,2,3,4} | broadcast | bytes 2359296 | tf_op jit(solution)/shard_map/broadcast_in_dim | solution.py:47
  31.1 0.0 copy-start.10
  31.1 0.0 copy-start.11
  31.1 7.7 %all-to-all-start.1 = ((bf16[8,8,2,16,512]{4,3,2,1,0:T(8,128)(2,1)}), bf16[8,8,2,16,512]{4,3,2,1,0:T(8,128)(2,1)S(1)}, u32[]{:S(2)}, u32[]{:S(2)}) async-start(bf16[8,8,2,16,512]{4,3,2,1,0:T(8,128)(2,1)} %broadcast_in_dim.28), calls=%async_computation.1 | async-start | bytes 4194304 | tf_op jit(solution)/shard_map/all_to_all | solution.py:48
  38.8 0.1 copy.17
  38.9 0.1 reshape.36
  39.0 0.1 pad_add_fusion.ints_ref
  39.1 2.0 %collective-permute-start.1 = (s32[42]{0:T(128)S(1)}, s32[42]{0:T(128)S(1)}, u32[]{:S(2)}, u32[]{:S(2)}) collective-permute-start(s32[42]{0:T(128)S(1)} %pad_add_fusion.ints_ref), channel_id=1, source_target_pairs={{1,0},{2,1},{3,2},{4,3},{5,4},{6,5},{7,6},{8,7},{9,8},{10,9},{11,1... | collective-permute-start | bytes 512 | tf_op jit(solution)/shard_map/ppermute | solution.py:518
  41.1 2.4 %collective-permute-start = (s32[42]{0:T(128)S(1)}, s32[42]{0:T(128)S(1)}, u32[]{:S(2)}, u32[]{:S(2)}) collective-permute-start(s32[42]{0:T(128)S(1)} %pad_add_fusion.ints_ref), channel_id=1, source_target_pairs={{0,1},{1,2},{2,3},{3,4},{4,5},{5,6},{6,7},{7,8},{8,9},{9,10},{10,1... | collective-permute-start | bytes 512 | tf_op jit(solution)/shard_map/ppermute | solution.py:517
  43.4 0.7 constant_dynamic-slice_fusion
  44.1 2.0 %cut_pixels.1 = (bf16[208,768]{1,0:T(8,128)(2,1)S(1)}, bf16[208,768]{1,0:T(8,128)(2,1)S(1)}, bf16[208,768]{1,0:T(8,128)(2,1)S(1)}) custom-call(s32[42]{0:T(128)S(1)} %pad_add_fusion.ints_ref, bf16[2,256,768]{2,1,0:T(8,128)(2,1)S(1)} %bitcast.33), custom_call_target="tpu_custom_call" | custom-call | tf_op jit(solution)/shard_map/cut_pixels/pallas_call | solution.py:218
  46.1 0.0 copy-start.1
  46.1 0.0 copy-start.3
  46.2 0.1 pad.5.clone
  46.2 0.1 maximum_bitcast_fusion.param_ref
  46.3 1.1 fusion
  47.5 15.2 %collective-permute-done.1 = s32[42]{0:T(128)S(1)} collective-permute-done((s32[42]{0:T(128)S(1)}, s32[42]{0:T(128)S(1)}, u32[]{:S(2)}, u32[]{:S(2)}) %collective-permute-start.1) | collective-permute-done | bytes 200 | tf_op jit(solution)/shard_map/ppermute | solution.py:518
  62.7 0.0 collective-permute-done
  62.7 0.1 concatenate.18.ints_ref
  62.8 4.8 %all-to-all-done.1 = bf16[8,8,2,16,512]{4,3,2,1,0:T(8,128)(2,1)S(1)} async-done(((bf16[8,8,2,16,512]{4,3,2,1,0:T(8,128)(2,1)}), bf16[8,8,2,16,512]{4,3,2,1,0:T(8,128)(2,1)S(1)}, u32[]{:S(2)}, u32[]{:S(2)}) %all-to-all-start.1) | async-done | bytes 2097184 | tf_op jit(solution)/shard_map/all_to_all | solution.py:48
  67.5 0.7 broadcast_in_dim.30.refs_7_
  68.2 1.9 %collective-permute-start.2 = (bf16[64,2,16,512]{3,2,1,0:T(8,128)(2,1)S(1)}, bf16[64,2,16,512]{3,2,1,0:T(8,128)(2,1)S(1)}, u32[]{:S(2)}, u32[]{:S(2)}) collective-permute-start(bf16[64,2,16,512]{3,2,1,0:T(8,128)(2,1)S(1)} %bitcast.21), channel_id=1, source_target_pairs={{0,1},{1,0},{2,3},{3,2},{4,5},{5,4},{6,7},{7,6},{8,9},{9,8},{10,11... | collective-permute-start | bytes 6291464 | tf_op jit(solution)/shard_map/ppermute | solution.py:535
  70.2 2.4 %collective-permute-start.5 = (bf16[208,768]{1,0:T(8,128)(2,1)}, bf16[208,768]{1,0:T(8,128)(2,1)S(1)}, u32[]{:S(2)}, u32[]{:S(2)}) collective-permute-start(bf16[208,768]{1,0:T(8,128)(2,1)} %copy-done.3), channel_id=1, source_target_pairs={{0,1},{1,0},{2,3},{3,2},{4,5},{5,4},{6,7},{7,6},{8,9},{9,8},{10,11... | collective-permute-start | bytes 958472 | tf_op jit(solution)/shard_map/ppermute | solution.py:533
  72.6 1.9 %collective-permute-start.6 = (bf16[208,768]{1,0:T(8,128)(2,1)S(1)}, bf16[208,768]{1,0:T(8,128)(2,1)S(1)}, u32[]{:S(2)}, u32[]{:S(2)}) collective-permute-start(bf16[208,768]{1,0:T(8,128)(2,1)S(1)} %get-tuple-element.39), channel_id=1, source_target_pairs={{1,2},{3,4},{5,6},{7,8},{9,10},{11,12},{13,14},{15,16},{17,18},{19... | collective-permute-start | bytes 958472 | tf_op jit(solution)/shard_map/ppermute | solution.py:533
  74.5 0.0 collective-permute-done.2.other_ref
  74.5 0.7 collective-permute-start.4
  75.3 0.7 collective-permute-start.3
  75.9 0.0 collective-permute-done.5.pix_near
  76.0 7.0 %collective-permute-done.6.pix_far = bf16[208,768]{1,0:T(8,128)(2,1)S(1)} collective-permute-done((bf16[208,768]{1,0:T(8,128)(2,1)S(1)}, bf16[208,768]{1,0:T(8,128)(2,1)S(1)}, u32[]{:S(2)}, u32[]{:S(2)}) %collective-permute-start.6) | collective-permute-done | bytes 319520 | tf_op jit(solution)/shard_map/ppermute | solution.py:533
  83.0 0.0 collective-permute-done.4.tile_ref
  83.0 0.7 copy-done.5
  83.8 1.3 collective-permute-start.8
  85.0 0.0 collective-permute-done.3.tile_ref
  85.1 1.3 collective-permute-start.7
  86.4 11.1 %collective-permute-done.8.tile_ref = bf16[256,512]{1,0:T(8,128)(2,1)S(1)} collective-permute-done((bf16[256,512]{1,0:T(8,128)(2,1)S(1)}, bf16[256,512]{1,0:T(8,128)(2,1)S(1)}, u32[]{:S(2)}, u32[]{:S(2)}) %collective-permute-start.8) | collective-permute-done | bytes 262176 | tf_op jit(solution)/shard_map/ppermute | solution.py:546
  97.5 4.1 %detector_block.10 = bf16[256,512]{1,0:T(8,128)(2,1)S(1)} custom-call(bf16[256,512]{1,0:T(8,128)(2,1)S(1)} %collective-permute-done.8.tile_ref, f32[4,56,128]{2,1,0:T(8,128)S(1)} %maximum_bitcast_fusion.param_ref, bf16[64,2,16,512]{3,2,1,0:T(8,128)(2,1)S(1)} %bitcast.26, bf16[64,2,16,512]{3,2,1,0:T(8,128)(2,1)S(1)} %collective-permute-done.2.other_ref), custom_call_target="tpu_custom_call" | custom-call | tf_op jit(solution)/shard_map/detector_block/pallas_call | solution.py:182
  101.6 1.3 collective-permute-start.10
  102.9 0.4 collective-permute-done.7.tile_ref
  103.3 4.1 %detector_block.11 = bf16[256,512]{1,0:T(8,128)(2,1)S(1)} custom-call(bf16[256,512]{1,0:T(8,128)(2,1)S(1)} %collective-permute-done.7.tile_ref, f32[4,56,128]{2,1,0:T(8,128)S(1)} %maximum_bitcast_fusion.param_ref, bf16[64,2,16,512]{3,2,1,0:T(8,128)(2,1)S(1)} %bitcast.27, bf16[64,2,16,512]{3,2,1,0:T(8,128)(2,1)S(1)} %collective-permute-done.2.other_ref), custom_call_target="tpu_custom_call" | custom-call | tf_op jit(solution)/shard_map/detector_block/pallas_call | solution.py:182
  107.4 1.3 collective-permute-start.9
  108.7 0.0 collective-permute-done.10.tile_ref
  108.8 0.7 collective-permute-start.12
  109.5 4.7 %collective-permute-done.9.tile_ref = bf16[256,512]{1,0:T(8,128)(2,1)S(1)} collective-permute-done((bf16[256,512]{1,0:T(8,128)(2,1)S(1)}, bf16[256,512]{1,0:T(8,128)(2,1)S(1)}, u32[]{:S(2)}, u32[]{:S(2)}) %collective-permute-start.9) | collective-permute-done | bytes 262176 | tf_op jit(solution)/shard_map/ppermute | solution.py:546
  114.2 0.7 collective-permute-start.11
  114.8 0.0 collective-permute-done.12.refs_2_
  114.9 0.7 collective-permute-start.13
  115.5 0.0 all-gather.3.cloned.1.call-done
  115.6 0.0 collective-permute-done.13.refs_3_
  115.6 0.0 collective-permute-done.11.refs_0_
  115.6 0.6 pick_crops.1
  116.2 0.7 collective-permute-start.14
  116.8 0.7 collective-permute-start.15
  117.5 1.3 collective-permute-start.16
  118.8 0.0 copy-start.2
  118.8 4.8 %stage_weights.1 = (bf16[8,3584,128]{2,1,0:T(8,128)(2,1)S(1)}, f32[208,1024]{1,0:T(8,128)S(1)}) custom-call(s32[42]{0:T(128)S(1)} %pad_add_fusion.ints_ref, bf16[208,768]{1,0:T(8,128)(2,1)} %copy-done.4, bf16[208,768]{1,0:T(8,128)(2,1)} %copy-done.1, bf16[208,768]{1,0:T(8,128)(2,1)} %copy-done.5, bf16[8,3584,128]{2,1,0:T(8,128)(2,1)} %bitcast.34), custom_call_target="tpu_custom_call" | custom-call | tf_op jit(solution)/shard_map/stage_weights/pallas_call | solution.py:368
  123.6 0.0 collective-permute-done.14.refs_0_
  123.6 0.0 collective-permute-done.15.refs_1_
  123.6 21.5 %collective-permute-done.16.refs_2_ = bf16[208,512]{1,0:T(8,128)(2,1)S(1)} collective-permute-done((bf16[208,512]{1,0:T(8,128)(2,1)S(1)}, bf16[208,512]{1,0:T(8,128)(2,1)S(1)}, u32[]{:S(2)}, u32[]{:S(2)}) %collective-permute-start.16) | collective-permute-done | bytes 213024 | tf_op jit(solution)/shard_map/ppermute | solution.py:554
  145.1 4.0 %classify.1 = f32[1,1024]{1,0:T(1,128)} custom-call(bf16[208,512]{1,0:T(8,128)(2,1)S(1)} %collective-permute-done.14.refs_0_, bf16[208,512]{1,0:T(8,128)(2,1)S(1)} %collective-permute-done.15.refs_1_, bf16[208,512]{1,0:T(8,128)(2,1)S(1)} %collective-permute-done.16.refs_2_, bf16[208,512]{1,0:T(8,128)(2,1)S(1)} %get-tuple-element.50.refs_3_, ...), custom_call_target="tpu_custom_call" | custom-call | tf_op jit(solution)/shard_map/classify/pallas_call | solution.py:466
  (30 shorter events, 0.2 us)
Async XLA Ops:
  6.5 2.2 %copy-start.7 = (bf16[1,16,512]{2,1,0:T(8,128)(2,1)S(1)}, bf16[1,16,512]{2,1,0:T(8,128)(2,1)}, u32[]{:S(2)}) copy-start(bf16[1,16,512]{2,1,0:T(8,128)(2,1)} %param.20) | copy-start | bytes 49156
  6.5 2.2 %copy-start.8 = (bf16[1,512,16]{1,2,0:T(8,128)(2,1)S(1)}, bf16[1,512,16]{1,2,0:T(8,128)(2,1)}, u32[]{:S(2)}) copy-start(bf16[1,512,16]{1,2,0:T(8,128)(2,1)} %param.19) | copy-start | bytes 49156
  6.5 109.0 %all-gather.3.cloned.1.call-start = ((), (), s32[]{:S(2)}) async-start(), calls=%async_computation.2 | async-start | bytes 8257536 | tf_op jit(solution)/shard_map/all_gather | solution.py:511
  31.1 7.7 %copy-start.9 = (s32[1,4,3,3]{1,0,3,2:T(1,128)S(1)}, s32[1,4,3,3]{1,0,3,2:T(1,128)}, u32[]{:S(2)}) copy-start(s32[1,4,3,3]{1,0,3,2:T(1,128)} %param.28) | copy-start | bytes 436
  31.1 7.9 %copy-start.12 = (s32[1,4]{1,0:T(1,128)S(1)}, s32[1,4]{1,0:T(1,128)}, u32[]{:S(2)}) copy-start(s32[1,4]{1,0:T(1,128)} %param.29) | copy-start | bytes 52
  31.1 13.0 %copy-start.6 = (f32[1,7,7,512]{3,0,2,1:T(1,128)S(1)}, f32[1,7,7,512]{3,0,2,1:T(1,128)}, u32[]{:S(2)}) copy-start(f32[1,7,7,512]{3,0,2,1:T(1,128)} %param.17) | copy-start | bytes 301060
  31.1 13.0 %copy-start = (bf16[2,16,16,768]{3,2,1,0:T(8,128)(2,1)S(1)}, bf16[2,16,16,768]{3,2,1,0:T(8,128)(2,1)}, u32[]{:S(2)}) copy-start(bf16[2,16,16,768]{3,2,1,0:T(8,128)(2,1)} %param.16) | copy-start | bytes 2359300
  31.1 15.2 %copy-start.10 = (f32[1,512]{1,0:T(1,128)S(1)}, f32[1,512]{1,0:T(1,128)}, u32[]{:S(2)}) copy-start(f32[1,512]{1,0:T(1,128)} %param.21) | copy-start | bytes 6148
  31.1 15.1 %copy-start.11 = (f32[1,512]{1,0:T(1,128)S(1)}, f32[1,512]{1,0:T(1,128)}, u32[]{:S(2)}) copy-start(f32[1,512]{1,0:T(1,128)} %param.18) | copy-start | bytes 6148
  31.1 36.4 %all-to-all-start.1 = ((bf16[8,8,2,16,512]{4,3,2,1,0:T(8,128)(2,1)}), bf16[8,8,2,16,512]{4,3,2,1,0:T(8,128)(2,1)S(1)}, u32[]{:S(2)}, u32[]{:S(2)}) async-start(bf16[8,8,2,16,512]{4,3,2,1,0:T(8,128)(2,1)} %broadcast_in_dim.28), calls=%async_computation.1 | async-start | bytes 4194304 | tf_op jit(solution)/shard_map/all_to_all | solution.py:48
  39.1 23.6 %collective-permute-start.1 = (s32[42]{0:T(128)S(1)}, s32[42]{0:T(128)S(1)}, u32[]{:S(2)}, u32[]{:S(2)}) collective-permute-start(s32[42]{0:T(128)S(1)} %pad_add_fusion.ints_ref), channel_id=1, source_target_pairs={{1,0},{2,1},{3,2},{4,3},{5,4},{6,5},{7,6},{8,7},{9,8},{10,9},{11,1... | collective-permute-start | bytes 512 | tf_op jit(solution)/shard_map/ppermute | solution.py:518
  41.1 21.6 %collective-permute-start = (s32[42]{0:T(128)S(1)}, s32[42]{0:T(128)S(1)}, u32[]{:S(2)}, u32[]{:S(2)}) collective-permute-start(s32[42]{0:T(128)S(1)} %pad_add_fusion.ints_ref), channel_id=1, source_target_pairs={{0,1},{1,2},{2,3},{3,4},{4,5},{5,6},{6,7},{7,8},{8,9},{9,10},{10,1... | collective-permute-start | bytes 512 | tf_op jit(solution)/shard_map/ppermute | solution.py:517
  46.1 1.3 copy-start.1
  46.1 16.5 %copy-start.3 = (bf16[208,768]{1,0:T(8,128)(2,1)}, bf16[208,768]{1,0:T(8,128)(2,1)S(1)}, u32[]{:S(2)}) copy-start(bf16[208,768]{1,0:T(8,128)(2,1)S(1)} %get-tuple-element.37) | copy-start | bytes 958468
  68.2 6.3 %collective-permute-start.2 = (bf16[64,2,16,512]{3,2,1,0:T(8,128)(2,1)S(1)}, bf16[64,2,16,512]{3,2,1,0:T(8,128)(2,1)S(1)}, u32[]{:S(2)}, u32[]{:S(2)}) collective-permute-start(bf16[64,2,16,512]{3,2,1,0:T(8,128)(2,1)S(1)} %bitcast.21), channel_id=1, source_target_pairs={{0,1},{1,0},{2,3},{3,2},{4,5},{5,4},{6,7},{7,6},{8,9},{9,8},{10,11... | collective-permute-start | bytes 6291464 | tf_op jit(solution)/shard_map/ppermute | solution.py:535
  70.2 5.8 %collective-permute-start.5 = (bf16[208,768]{1,0:T(8,128)(2,1)}, bf16[208,768]{1,0:T(8,128)(2,1)S(1)}, u32[]{:S(2)}, u32[]{:S(2)}) collective-permute-start(bf16[208,768]{1,0:T(8,128)(2,1)} %copy-done.3), channel_id=1, source_target_pairs={{0,1},{1,0},{2,3},{3,2},{4,5},{5,4},{6,7},{7,6},{8,9},{9,8},{10,11... | collective-permute-start | bytes 958472 | tf_op jit(solution)/shard_map/ppermute | solution.py:533
  72.6 10.4 %collective-permute-start.6 = (bf16[208,768]{1,0:T(8,128)(2,1)S(1)}, bf16[208,768]{1,0:T(8,128)(2,1)S(1)}, u32[]{:S(2)}, u32[]{:S(2)}) collective-permute-start(bf16[208,768]{1,0:T(8,128)(2,1)S(1)} %get-tuple-element.39), channel_id=1, source_target_pairs={{1,2},{3,4},{5,6},{7,8},{9,10},{11,12},{13,14},{15,16},{17,18},{19... | collective-permute-start | bytes 958472 | tf_op jit(solution)/shard_map/ppermute | solution.py:533
  74.5 8.5 %collective-permute-start.4 = (bf16[256,512]{1,0:T(8,128)(2,1)S(1)}, bf16[256,512]{1,0:T(8,128)(2,1)S(1)}, u32[]{:S(2)}, u32[]{:S(2)}) collective-permute-start(bf16[256,512]{1,0:T(8,128)(2,1)S(1)} %early_block.1), channel_id=1, source_target_pairs={{0,128},{1,129},{2,130},{3,131},{4,132},{5,133},{6,134},{7,135},{8... | collective-permute-start | bytes 786440 | tf_op jit(solution)/shard_map/ppermute | solution.py:546
  75.3 9.8 %collective-permute-start.3 = (bf16[256,512]{1,0:T(8,128)(2,1)S(1)}, bf16[256,512]{1,0:T(8,128)(2,1)S(1)}, u32[]{:S(2)}, u32[]{:S(2)}) collective-permute-start(bf16[256,512]{1,0:T(8,128)(2,1)S(1)} %detector_block.7), channel_id=1, source_target_pairs={{0,128},{1,129},{2,130},{3,131},{4,132},{5,133},{6,134},{7,135},{8... | collective-permute-start | bytes 786440 | tf_op jit(solution)/shard_map/ppermute | solution.py:546
  76.0 7.1 %copy-start.4 = (bf16[208,768]{1,0:T(8,128)(2,1)}, bf16[208,768]{1,0:T(8,128)(2,1)S(1)}, u32[]{:S(2)}) copy-start(bf16[208,768]{1,0:T(8,128)(2,1)S(1)} %collective-permute-done.5.pix_near) | copy-start | bytes 958468
  83.0 0.8 copy-start.5
  83.8 13.8 %collective-permute-start.8 = (bf16[256,512]{1,0:T(8,128)(2,1)S(1)}, bf16[256,512]{1,0:T(8,128)(2,1)S(1)}, u32[]{:S(2)}, u32[]{:S(2)}) collective-permute-start(bf16[256,512]{1,0:T(8,128)(2,1)S(1)} %detector_block.8), channel_id=1, source_target_pairs={{128,256},{129,257},{130,258},{131,259},{132,260},{133,261},{134,2... | collective-permute-start | bytes 786440 | tf_op jit(solution)/shard_map/ppermute | solution.py:546
  85.1 18.2 %collective-permute-start.7 = (bf16[256,512]{1,0:T(8,128)(2,1)S(1)}, bf16[256,512]{1,0:T(8,128)(2,1)S(1)}, u32[]{:S(2)}, u32[]{:S(2)}) collective-permute-start(bf16[256,512]{1,0:T(8,128)(2,1)S(1)} %detector_block.9), channel_id=1, source_target_pairs={{128,256},{129,257},{130,258},{131,259},{132,260},{133,261},{134,2... | collective-permute-start | bytes 786440 | tf_op jit(solution)/shard_map/ppermute | solution.py:546
  101.6 7.1 %collective-permute-start.10 = (bf16[256,512]{1,0:T(8,128)(2,1)S(1)}, bf16[256,512]{1,0:T(8,128)(2,1)S(1)}, u32[]{:S(2)}, u32[]{:S(2)}) collective-permute-start(bf16[256,512]{1,0:T(8,128)(2,1)S(1)} %detector_block.10), channel_id=1, source_target_pairs={{256,384},{257,385},{258,386},{259,387},{260,388},{261,389},{262,3... | collective-permute-start | bytes 786440 | tf_op jit(solution)/shard_map/ppermute | solution.py:546
  107.4 6.7 %collective-permute-start.9 = (bf16[256,512]{1,0:T(8,128)(2,1)S(1)}, bf16[256,512]{1,0:T(8,128)(2,1)S(1)}, u32[]{:S(2)}, u32[]{:S(2)}) collective-permute-start(bf16[256,512]{1,0:T(8,128)(2,1)S(1)} %detector_block.11), channel_id=1, source_target_pairs={{256,384},{257,385},{258,386},{259,387},{260,388},{261,389},{262,3... | collective-permute-start | bytes 786440 | tf_op jit(solution)/shard_map/ppermute | solution.py:546
  108.8 6.1 %collective-permute-start.12 = (bf16[256,512]{1,0:T(8,128)(2,1)S(1)}, bf16[256,512]{1,0:T(8,128)(2,1)S(1)}, u32[]{:S(2)}, u32[]{:S(2)}) collective-permute-start(bf16[256,512]{1,0:T(8,128)(2,1)S(1)} %detector_block.12.refs_0_), channel_id=1, source_target_pairs={{385,386},{387,388},{389,390},{391,392},{393,394},{395,396},{397,3... | collective-permute-start | bytes 786440 | tf_op jit(solution)/shard_map/ppermute | solution.py:550
  114.2 1.4 collective-permute-start.11
  114.9 0.7 collective-permute-start.13
  116.2 7.4 %collective-permute-start.14 = (bf16[208,512]{1,0:T(8,128)(2,1)S(1)}, bf16[208,512]{1,0:T(8,128)(2,1)S(1)}, u32[]{:S(2)}, u32[]{:S(2)}) collective-permute-start(bf16[208,512]{1,0:T(8,128)(2,1)S(1)} %get-tuple-element.47), channel_id=1, source_target_pairs={{384,0},{385,1},{386,2},{387,3},{388,4},{389,5},{390,6},{391,7},{3... | collective-permute-start | bytes 638984 | tf_op jit(solution)/shard_map/ppermute | solution.py:554
  116.8 6.8 %collective-permute-start.15 = (bf16[208,512]{1,0:T(8,128)(2,1)S(1)}, bf16[208,512]{1,0:T(8,128)(2,1)S(1)}, u32[]{:S(2)}, u32[]{:S(2)}) collective-permute-start(bf16[208,512]{1,0:T(8,128)(2,1)S(1)} %get-tuple-element.48), channel_id=1, source_target_pairs={{384,128},{385,129},{386,130},{387,131},{388,132},{389,133},{390,1... | collective-permute-start | bytes 638984 | tf_op jit(solution)/shard_map/ppermute | solution.py:554
  117.5 27.6 %collective-permute-start.16 = (bf16[208,512]{1,0:T(8,128)(2,1)S(1)}, bf16[208,512]{1,0:T(8,128)(2,1)S(1)}, u32[]{:S(2)}, u32[]{:S(2)}) collective-permute-start(bf16[208,512]{1,0:T(8,128)(2,1)S(1)} %get-tuple-element.49), channel_id=1, source_target_pairs={{384,256},{385,257},{386,258},{387,259},{388,260},{389,261},{390,2... | collective-permute-start | bytes 638984 | tf_op jit(solution)/shard_map/ppermute | solution.py:554
  118.8 26.3 %copy-start.2 = (f32[2,1024]{1,0:T(2,128)S(1)}, f32[2,1024]{1,0:T(2,128)}, u32[]{:S(2)}) copy-start(f32[2,1024]{1,0:T(2,128)} %refs_6_.1) | copy-start | bytes 24580
Sparse Core Ops, SparseCore 0:
  9.5 54.0 all-gather.2

commit v9 on v8

--- a/solution.py
+++ b/solution.py
@@ -337,6 +337,8 @@
             copies.append(
                 pltpu.make_async_copy(packed.at[place], weights.at[place], sems.at[1 + len(copies)])
             )
+    for copy in copies:
+        copy.start()
     core = ints_ref[CORE_AT]
     same_chip = ((source == 1) & (core == 1)) | ((source == 3) & (core == 0))
     away = (source == 1) | (source == 3)
@@ -348,8 +350,6 @@
             copy.start()
             copy.wait()
 
-    for copy in copies:
-        copy.start()
     for copy in copies[: 2 * sections]:
         copy.wait()
     rows = pix[...]

time: 157 us -> 157 us (level)
  transfers between devices with their start and end apart: 19 -> 19, of which waited for: 7 -> 7; matrix products, arithmetic and copies ran while one was open for 3% -> 3% of each run, Pallas kernels for 10% -> 9%
where the time goes in v9:
time: 157 us; the launch traced here: 156 us
  waiting for transfers between devices  65.1 us (41%)
  starting transfers between devices  29.5 us (19%)
  Pallas kernels  21.4 us (14%)
  blocking collectives  20.6 us (13%)
  between operations  13.8 us (9%)
  local copies, waits for them, and re-layouts  5.32 us (3%)
    ppermute x3, waiting for transfers between devices, per_device(): lax.ppermute(crops[slot], 'section', [(last, slot)])  21.9 us
    all_to_all x1, blocking collectives, spread_in_groups(): return lax.all_to_all(copies, REP, 0, 0, axis_index_groups=groups)  20.6 us
    ppermute x6, waiting for transfers between devices, per_device(): lax.ppermute(tile, 'section', [(number, number + 1)])  16.2 us
    ppermute x1, waiting for transfers between devices, per_device(): above = lax.ppermute(ints, REP, downward)  15.2 us
    pallas_call x7, Pallas kernels, detector_block(): pl.pallas_call(functools.partial(block_body, number=number), out_shape=ou...  8.25 us
    all_to_all x1, starting transfers between devices, spread_in_groups(): return lax.all_to_all(copies, REP, 0, 0, axis_index_groups=groups)  7.69 us
    ppermute x1, waiting for transfers between devices, per_device(): lax.ppermute(cut[2], REP, beyond)  7.04 us
    ppermute x6, starting transfers between devices, per_device(): lax.ppermute(tile, 'section', [(number, number + 1)])  6.54 us
  transfers between devices with their start and end apart: 19, of which 7 were waited for; matrix products, arithmetic and copies ran while one was open for 3% of the time, Pallas kernels for 9%

profile of v9, /device:TPU:12, one launch (start us, length us, event | category | flops | bytes accessed | tf_op | source)
XLA Modules:
  0.0 156.0 jit_solution(8792017949828408091)
XLA Ops:
  6.5 0.0 all-gather.3.cloned.1.call-start
  6.5 2.2 %pack_weights.1 = bf16[3584,128]{1,0:T(8,128)(2,1)} custom-call(s32[1]{0:T(128)} %bitcast.2.parity_ref, bf16[768,256]{1,0:T(8,128)(2,1)} %embed.1, bf16[512,256]{1,0:T(8,128)(2,1)} %merge.1, bf16[196,256]{1,0:T(8,128)(2,1)} %pos.1, bf16[3,1024,128]{2,1,0:T(8,128)(2,1)} %bitcast.35, bf16[128,1024]{1,0:T(8,128)(2,1)} %out.1), custom_call_target="tpu_custom_call" | custom-call | tf_op jit(solution)/shard_map/pack_weights/pallas_call | solution.py:312
  8.7 0.0 all-gather.3.cloned.1.call-update
  8.8 20.6 %all_to_all.10 = bf16[8,2,16,512]{3,2,1,0:T(8,128)(2,1)S(1)} all-to-all(bf16[8,2,16,512]{3,2,1,0:T(8,128)(2,1)S(1)} %broadcast_in_dim.13), channel_id=1, replica_groups={{0,2,4,6,8,10,12,14},{16,18,20,22,24,26,28,30},{32,34,36,38,40,42,44,46..., dimensions={0} | all-to-all | bytes 524288 | tf_op jit(solution)/shard_map/all_to_all | solution.py:48
  29.4 1.7 %broadcast_in_dim.28 = bf16[8,8,2,16,512]{4,3,2,1,0:T(8,128)(2,1)} broadcast(bf16[8,2,16,512]{3,2,1,0:T(8,128)(2,1)S(1)} %all_to_all.10), dimensions={1,2,3,4} | broadcast | bytes 2359296 | tf_op jit(solution)/shard_map/broadcast_in_dim | solution.py:47
  31.1 0.0 copy-start.10
  31.1 0.0 copy-start.11
  31.1 7.7 %all-to-all-start.1 = ((bf16[8,8,2,16,512]{4,3,2,1,0:T(8,128)(2,1)}), bf16[8,8,2,16,512]{4,3,2,1,0:T(8,128)(2,1)S(1)}, u32[]{:S(2)}, u32[]{:S(2)}) async-start(bf16[8,8,2,16,512]{4,3,2,1,0:T(8,128)(2,1)} %broadcast_in_dim.28), calls=%async_computation.1 | async-start | bytes 4194304 | tf_op jit(solution)/shard_map/all_to_all | solution.py:48
  38.8 0.1 copy.17
  38.9 0.1 reshape.36
  39.0 0.1 pad_add_fusion.ints_ref
  39.1 2.0 %collective-permute-start.1 = (s32[42]{0:T(128)S(1)}, s32[42]{0:T(128)S(1)}, u32[]{:S(2)}, u32[]{:S(2)}) collective-permute-start(s32[42]{0:T(128)S(1)} %pad_add_fusion.ints_ref), channel_id=1, source_target_pairs={{1,0},{2,1},{3,2},{4,3},{5,4},{6,5},{7,6},{8,7},{9,8},{10,9},{11,1... | collective-permute-start | bytes 512 | tf_op jit(solution)/shard_map/ppermute | solution.py:518
  41.1 2.4 %collective-permute-start = (s32[42]{0:T(128)S(1)}, s32[42]{0:T(128)S(1)}, u32[]{:S(2)}, u32[]{:S(2)}) collective-permute-start(s32[42]{0:T(128)S(1)} %pad_add_fusion.ints_ref), channel_id=1, source_target_pairs={{0,1},{1,2},{2,3},{3,4},{4,5},{5,6},{6,7},{7,8},{8,9},{9,10},{10,1... | collective-permute-start | bytes 512 | tf_op jit(solution)/shard_map/ppermute | solution.py:517
  43.4 0.7 constant_dynamic-slice_fusion
  44.1 0.0 copy-done.6
  44.1 2.0 %cut_pixels.1 = (bf16[208,768]{1,0:T(8,128)(2,1)S(1)}, bf16[208,768]{1,0:T(8,128)(2,1)S(1)}, bf16[208,768]{1,0:T(8,128)(2,1)S(1)}) custom-call(s32[42]{0:T(128)S(1)} %pad_add_fusion.ints_ref, bf16[2,256,768]{2,1,0:T(8,128)(2,1)S(1)} %bitcast.33), custom_call_target="tpu_custom_call" | custom-call | tf_op jit(solution)/shard_map/cut_pixels/pallas_call | solution.py:218
  46.2 0.1 pad.5.clone
  46.2 0.1 maximum_bitcast_fusion.param_ref
  46.3 1.1 fusion
  47.5 15.2 %collective-permute-done.1 = s32[42]{0:T(128)S(1)} collective-permute-done((s32[42]{0:T(128)S(1)}, s32[42]{0:T(128)S(1)}, u32[]{:S(2)}, u32[]{:S(2)}) %collective-permute-start.1) | collective-permute-done | bytes 200 | tf_op jit(solution)/shard_map/ppermute | solution.py:518
  62.7 0.0 copy-done.3
  62.7 0.0 collective-permute-done
  62.7 0.1 concatenate.18.ints_ref
  62.8 4.8 %all-to-all-done.1 = bf16[8,8,2,16,512]{4,3,2,1,0:T(8,128)(2,1)S(1)} async-done(((bf16[8,8,2,16,512]{4,3,2,1,0:T(8,128)(2,1)}), bf16[8,8,2,16,512]{4,3,2,1,0:T(8,128)(2,1)S(1)}, u32[]{:S(2)}, u32[]{:S(2)}) %all-to-all-start.1) | async-done | bytes 2097184 | tf_op jit(solution)/shard_map/all_to_all | solution.py:48
  67.5 0.7 broadcast_in_dim.30.refs_7_
  68.2 1.9 %collective-permute-start.2 = (bf16[64,2,16,512]{3,2,1,0:T(8,128)(2,1)S(1)}, bf16[64,2,16,512]{3,2,1,0:T(8,128)(2,1)S(1)}, u32[]{:S(2)}, u32[]{:S(2)}) collective-permute-start(bf16[64,2,16,512]{3,2,1,0:T(8,128)(2,1)S(1)} %bitcast.21), channel_id=1, source_target_pairs={{0,1},{1,0},{2,3},{3,2},{4,5},{5,4},{6,7},{7,6},{8,9},{9,8},{10,11... | collective-permute-start | bytes 6291464 | tf_op jit(solution)/shard_map/ppermute | solution.py:535
  70.2 2.4 %collective-permute-start.5 = (bf16[208,768]{1,0:T(8,128)(2,1)}, bf16[208,768]{1,0:T(8,128)(2,1)S(1)}, u32[]{:S(2)}, u32[]{:S(2)}) collective-permute-start(bf16[208,768]{1,0:T(8,128)(2,1)} %copy-done.3), channel_id=1, source_target_pairs={{0,1},{1,0},{2,3},{3,2},{4,5},{5,4},{6,7},{7,6},{8,9},{9,8},{10,11... | collective-permute-start | bytes 958472 | tf_op jit(solution)/shard_map/ppermute | solution.py:533
  72.6 1.9 %collective-permute-start.6 = (bf16[208,768]{1,0:T(8,128)(2,1)S(1)}, bf16[208,768]{1,0:T(8,128)(2,1)S(1)}, u32[]{:S(2)}, u32[]{:S(2)}) collective-permute-start(bf16[208,768]{1,0:T(8,128)(2,1)S(1)} %get-tuple-element.39), channel_id=1, source_target_pairs={{1,2},{3,4},{5,6},{7,8},{9,10},{11,12},{13,14},{15,16},{17,18},{19... | collective-permute-start | bytes 958472 | tf_op jit(solution)/shard_map/ppermute | solution.py:533
  74.5 0.0 collective-permute-done.2.other_ref
  74.5 0.7 collective-permute-start.4
  75.3 0.7 collective-permute-start.3
  75.9 0.0 collective-permute-done.5.pix_near
  76.0 0.0 copy-start.4
  76.0 7.0 %collective-permute-done.6.pix_far = bf16[208,768]{1,0:T(8,128)(2,1)S(1)} collective-permute-done((bf16[208,768]{1,0:T(8,128)(2,1)S(1)}, bf16[208,768]{1,0:T(8,128)(2,1)S(1)}, u32[]{:S(2)}, u32[]{:S(2)}) %collective-permute-start.6) | collective-permute-done | bytes 319520 | tf_op jit(solution)/shard_map/ppermute | solution.py:533
  83.0 0.0 collective-permute-done.4.tile_ref
  83.0 0.7 copy-done.5
  83.8 1.3 collective-permute-start.8
  85.0 0.0 collective-permute-done.3.tile_ref
  85.1 1.3 collective-permute-start.7
  86.4 11.1 %collective-permute-done.8.tile_ref = bf16[256,512]{1,0:T(8,128)(2,1)S(1)} collective-permute-done((bf16[256,512]{1,0:T(8,128)(2,1)S(1)}, bf16[256,512]{1,0:T(8,128)(2,1)S(1)}, u32[]{:S(2)}, u32[]{:S(2)}) %collective-permute-start.8) | collective-permute-done | bytes 262176 | tf_op jit(solution)/shard_map/ppermute | solution.py:546
  97.5 4.1 %detector_block.10 = bf16[256,512]{1,0:T(8,128)(2,1)S(1)} custom-call(bf16[256,512]{1,0:T(8,128)(2,1)S(1)} %collective-permute-done.8.tile_ref, f32[4,56,128]{2,1,0:T(8,128)S(1)} %maximum_bitcast_fusion.param_ref, bf16[64,2,16,512]{3,2,1,0:T(8,128)(2,1)S(1)} %bitcast.26, bf16[64,2,16,512]{3,2,1,0:T(8,128)(2,1)S(1)} %collective-permute-done.2.other_ref), custom_call_target="tpu_custom_call" | custom-call | tf_op jit(solution)/shard_map/detector_block/pallas_call | solution.py:182
  101.6 1.3 collective-permute-start.10
  102.9 0.4 collective-permute-done.7.tile_ref
  103.3 4.1 %detector_block.11 = bf16[256,512]{1,0:T(8,128)(2,1)S(1)} custom-call(bf16[256,512]{1,0:T(8,128)(2,1)S(1)} %collective-permute-done.7.tile_ref, f32[4,56,128]{2,1,0:T(8,128)S(1)} %maximum_bitcast_fusion.param_ref, bf16[64,2,16,512]{3,2,1,0:T(8,128)(2,1)S(1)} %bitcast.27, bf16[64,2,16,512]{3,2,1,0:T(8,128)(2,1)S(1)} %collective-permute-done.2.other_ref), custom_call_target="tpu_custom_call" | custom-call | tf_op jit(solution)/shard_map/detector_block/pallas_call | solution.py:182
  107.4 1.3 collective-permute-start.9
  108.7 0.0 collective-permute-done.10.tile_ref
  108.8 0.7 collective-permute-start.12
  109.5 4.7 %collective-permute-done.9.tile_ref = bf16[256,512]{1,0:T(8,128)(2,1)S(1)} collective-permute-done((bf16[256,512]{1,0:T(8,128)(2,1)S(1)}, bf16[256,512]{1,0:T(8,128)(2,1)S(1)}, u32[]{:S(2)}, u32[]{:S(2)}) %collective-permute-start.9) | collective-permute-done | bytes 262176 | tf_op jit(solution)/shard_map/ppermute | solution.py:546
  114.2 0.7 collective-permute-start.11
  114.8 0.0 collective-permute-done.12.refs_2_
  114.9 0.7 collective-permute-start.13
  115.5 0.0 all-gather.3.cloned.1.call-done
  115.6 0.0 collective-permute-done.13.refs_3_
  115.6 0.0 collective-permute-done.11.refs_0_
  115.6 0.6 pick_crops.1
  116.2 0.7 collective-permute-start.14
  116.8 0.7 collective-permute-start.15
  117.5 1.3 collective-permute-start.16
  118.8 0.0 copy-start.2
  118.8 4.4 %stage_weights.1 = (bf16[8,3584,128]{2,1,0:T(8,128)(2,1)S(1)}, f32[208,1024]{1,0:T(8,128)S(1)}) custom-call(s32[42]{0:T(128)S(1)} %pad_add_fusion.ints_ref, bf16[208,768]{1,0:T(8,128)(2,1)} %copy-done.4, bf16[208,768]{1,0:T(8,128)(2,1)} %copy-done.1, bf16[208,768]{1,0:T(8,128)(2,1)} %copy-done.5, bf16[8,3584,128]{2,1,0:T(8,128)(2,1)} %bitcast.34), custom_call_target="tpu_custom_call" | custom-call | tf_op jit(solution)/shard_map/stage_weights/pallas_call | solution.py:368
  123.2 0.0 collective-permute-done.14.refs_0_
  123.2 0.0 collective-permute-done.15.refs_1_
  123.2 21.9 %collective-permute-done.16.refs_2_ = bf16[208,512]{1,0:T(8,128)(2,1)S(1)} collective-permute-done((bf16[208,512]{1,0:T(8,128)(2,1)S(1)}, bf16[208,512]{1,0:T(8,128)(2,1)S(1)}, u32[]{:S(2)}, u32[]{:S(2)}) %collective-permute-start.16) | collective-permute-done | bytes 213024 | tf_op jit(solution)/shard_map/ppermute | solution.py:554
  145.1 4.0 %classify.1 = f32[1,1024]{1,0:T(1,128)} custom-call(bf16[208,512]{1,0:T(8,128)(2,1)S(1)} %collective-permute-done.14.refs_0_, bf16[208,512]{1,0:T(8,128)(2,1)S(1)} %collective-permute-done.15.refs_1_, bf16[208,512]{1,0:T(8,128)(2,1)S(1)} %collective-permute-done.16.refs_2_, bf16[208,512]{1,0:T(8,128)(2,1)S(1)} %get-tuple-element.50.refs_3_, ...), custom_call_target="tpu_custom_call" | custom-call | tf_op jit(solution)/shard_map/classify/pallas_call | solution.py:466
  (30 shorter events, 0.2 us)
Async XLA Ops:
  6.5 2.2 %copy-start.7 = (bf16[1,16,512]{2,1,0:T(8,128)(2,1)S(1)}, bf16[1,16,512]{2,1,0:T(8,128)(2,1)}, u32[]{:S(2)}) copy-start(bf16[1,16,512]{2,1,0:T(8,128)(2,1)} %param.20) | copy-start | bytes 49156
  6.5 2.2 %copy-start.8 = (bf16[1,512,16]{1,2,0:T(8,128)(2,1)S(1)}, bf16[1,512,16]{1,2,0:T(8,128)(2,1)}, u32[]{:S(2)}) copy-start(bf16[1,512,16]{1,2,0:T(8,128)(2,1)} %param.19) | copy-start | bytes 49156
  6.5 109.0 %all-gather.3.cloned.1.call-start = ((), (), s32[]{:S(2)}) async-start(), calls=%async_computation.2 | async-start | bytes 8257536 | tf_op jit(solution)/shard_map/all_gather | solution.py:511
  31.1 7.7 %copy-start.9 = (s32[1,4,3,3]{1,0,3,2:T(1,128)S(1)}, s32[1,4,3,3]{1,0,3,2:T(1,128)}, u32[]{:S(2)}) copy-start(s32[1,4,3,3]{1,0,3,2:T(1,128)} %param.28) | copy-start | bytes 436
  31.1 7.9 %copy-start.12 = (s32[1,4]{1,0:T(1,128)S(1)}, s32[1,4]{1,0:T(1,128)}, u32[]{:S(2)}) copy-start(s32[1,4]{1,0:T(1,128)} %param.29) | copy-start | bytes 52
  31.1 13.0 %copy-start.6 = (f32[1,7,7,512]{3,0,2,1:T(1,128)S(1)}, f32[1,7,7,512]{3,0,2,1:T(1,128)}, u32[]{:S(2)}) copy-start(f32[1,7,7,512]{3,0,2,1:T(1,128)} %param.17) | copy-start | bytes 301060
  31.1 13.0 %copy-start = (bf16[2,16,16,768]{3,2,1,0:T(8,128)(2,1)S(1)}, bf16[2,16,16,768]{3,2,1,0:T(8,128)(2,1)}, u32[]{:S(2)}) copy-start(bf16[2,16,16,768]{3,2,1,0:T(8,128)(2,1)} %param.16) | copy-start | bytes 2359300
  31.1 15.2 %copy-start.10 = (f32[1,512]{1,0:T(1,128)S(1)}, f32[1,512]{1,0:T(1,128)}, u32[]{:S(2)}) copy-start(f32[1,512]{1,0:T(1,128)} %param.21) | copy-start | bytes 6148
  31.1 15.1 %copy-start.11 = (f32[1,512]{1,0:T(1,128)S(1)}, f32[1,512]{1,0:T(1,128)}, u32[]{:S(2)}) copy-start(f32[1,512]{1,0:T(1,128)} %param.18) | copy-start | bytes 6148
  31.1 36.4 %all-to-all-start.1 = ((bf16[8,8,2,16,512]{4,3,2,1,0:T(8,128)(2,1)}), bf16[8,8,2,16,512]{4,3,2,1,0:T(8,128)(2,1)S(1)}, u32[]{:S(2)}, u32[]{:S(2)}) async-start(bf16[8,8,2,16,512]{4,3,2,1,0:T(8,128)(2,1)} %broadcast_in_dim.28), calls=%async_computation.1 | async-start | bytes 4194304 | tf_op jit(solution)/shard_map/all_to_all | solution.py:48
  39.1 23.6 %collective-permute-start.1 = (s32[42]{0:T(128)S(1)}, s32[42]{0:T(128)S(1)}, u32[]{:S(2)}, u32[]{:S(2)}) collective-permute-start(s32[42]{0:T(128)S(1)} %pad_add_fusion.ints_ref), channel_id=1, source_target_pairs={{1,0},{2,1},{3,2},{4,3},{5,4},{6,5},{7,6},{8,7},{9,8},{10,9},{11,1... | collective-permute-start | bytes 512 | tf_op jit(solution)/shard_map/ppermute | solution.py:518
  41.1 21.6 %collective-permute-start = (s32[42]{0:T(128)S(1)}, s32[42]{0:T(128)S(1)}, u32[]{:S(2)}, u32[]{:S(2)}) collective-permute-start(s32[42]{0:T(128)S(1)} %pad_add_fusion.ints_ref), channel_id=1, source_target_pairs={{0,1},{1,2},{2,3},{3,4},{4,5},{5,6},{6,7},{7,8},{8,9},{9,10},{10,1... | collective-permute-start | bytes 512 | tf_op jit(solution)/shard_map/ppermute | solution.py:517
  46.1 1.3 copy-start.1
  46.1 16.5 %copy-start.3 = (bf16[208,768]{1,0:T(8,128)(2,1)}, bf16[208,768]{1,0:T(8,128)(2,1)S(1)}, u32[]{:S(2)}) copy-start(bf16[208,768]{1,0:T(8,128)(2,1)S(1)} %get-tuple-element.37) | copy-start | bytes 958468
  68.2 6.3 %collective-permute-start.2 = (bf16[64,2,16,512]{3,2,1,0:T(8,128)(2,1)S(1)}, bf16[64,2,16,512]{3,2,1,0:T(8,128)(2,1)S(1)}, u32[]{:S(2)}, u32[]{:S(2)}) collective-permute-start(bf16[64,2,16,512]{3,2,1,0:T(8,128)(2,1)S(1)} %bitcast.21), channel_id=1, source_target_pairs={{0,1},{1,0},{2,3},{3,2},{4,5},{5,4},{6,7},{7,6},{8,9},{9,8},{10,11... | collective-permute-start | bytes 6291464 | tf_op jit(solution)/shard_map/ppermute | solution.py:535
  70.2 5.8 %collective-permute-start.5 = (bf16[208,768]{1,0:T(8,128)(2,1)}, bf16[208,768]{1,0:T(8,128)(2,1)S(1)}, u32[]{:S(2)}, u32[]{:S(2)}) collective-permute-start(bf16[208,768]{1,0:T(8,128)(2,1)} %copy-done.3), channel_id=1, source_target_pairs={{0,1},{1,0},{2,3},{3,2},{4,5},{5,4},{6,7},{7,6},{8,9},{9,8},{10,11... | collective-permute-start | bytes 958472 | tf_op jit(solution)/shard_map/ppermute | solution.py:533
  72.6 10.4 %collective-permute-start.6 = (bf16[208,768]{1,0:T(8,128)(2,1)S(1)}, bf16[208,768]{1,0:T(8,128)(2,1)S(1)}, u32[]{:S(2)}, u32[]{:S(2)}) collective-permute-start(bf16[208,768]{1,0:T(8,128)(2,1)S(1)} %get-tuple-element.39), channel_id=1, source_target_pairs={{1,2},{3,4},{5,6},{7,8},{9,10},{11,12},{13,14},{15,16},{17,18},{19... | collective-permute-start | bytes 958472 | tf_op jit(solution)/shard_map/ppermute | solution.py:533
  74.5 8.5 %collective-permute-start.4 = (bf16[256,512]{1,0:T(8,128)(2,1)S(1)}, bf16[256,512]{1,0:T(8,128)(2,1)S(1)}, u32[]{:S(2)}, u32[]{:S(2)}) collective-permute-start(bf16[256,512]{1,0:T(8,128)(2,1)S(1)} %early_block.1), channel_id=1, source_target_pairs={{0,128},{1,129},{2,130},{3,131},{4,132},{5,133},{6,134},{7,135},{8... | collective-permute-start | bytes 786440 | tf_op jit(solution)/shard_map/ppermute | solution.py:546
  75.3 9.8 %collective-permute-start.3 = (bf16[256,512]{1,0:T(8,128)(2,1)S(1)}, bf16[256,512]{1,0:T(8,128)(2,1)S(1)}, u32[]{:S(2)}, u32[]{:S(2)}) collective-permute-start(bf16[256,512]{1,0:T(8,128)(2,1)S(1)} %detector_block.7), channel_id=1, source_target_pairs={{0,128},{1,129},{2,130},{3,131},{4,132},{5,133},{6,134},{7,135},{8... | collective-permute-start | bytes 786440 | tf_op jit(solution)/shard_map/ppermute | solution.py:546
  76.0 7.1 %copy-start.4 = (bf16[208,768]{1,0:T(8,128)(2,1)}, bf16[208,768]{1,0:T(8,128)(2,1)S(1)}, u32[]{:S(2)}) copy-start(bf16[208,768]{1,0:T(8,128)(2,1)S(1)} %collective-permute-done.5.pix_near) | copy-start | bytes 958468
  83.0 0.8 copy-start.5
  83.8 13.8 %collective-permute-start.8 = (bf16[256,512]{1,0:T(8,128)(2,1)S(1)}, bf16[256,512]{1,0:T(8,128)(2,1)S(1)}, u32[]{:S(2)}, u32[]{:S(2)}) collective-permute-start(bf16[256,512]{1,0:T(8,128)(2,1)S(1)} %detector_block.8), channel_id=1, source_target_pairs={{128,256},{129,257},{130,258},{131,259},{132,260},{133,261},{134,2... | collective-permute-start | bytes 786440 | tf_op jit(solution)/shard_map/ppermute | solution.py:546
  85.1 18.2 %collective-permute-start.7 = (bf16[256,512]{1,0:T(8,128)(2,1)S(1)}, bf16[256,512]{1,0:T(8,128)(2,1)S(1)}, u32[]{:S(2)}, u32[]{:S(2)}) collective-permute-start(bf16[256,512]{1,0:T(8,128)(2,1)S(1)} %detector_block.9), channel_id=1, source_target_pairs={{128,256},{129,257},{130,258},{131,259},{132,260},{133,261},{134,2... | collective-permute-start | bytes 786440 | tf_op jit(solution)/shard_map/ppermute | solution.py:546
  101.6 7.1 %collective-permute-start.10 = (bf16[256,512]{1,0:T(8,128)(2,1)S(1)}, bf16[256,512]{1,0:T(8,128)(2,1)S(1)}, u32[]{:S(2)}, u32[]{:S(2)}) collective-permute-start(bf16[256,512]{1,0:T(8,128)(2,1)S(1)} %detector_block.10), channel_id=1, source_target_pairs={{256,384},{257,385},{258,386},{259,387},{260,388},{261,389},{262,3... | collective-permute-start | bytes 786440 | tf_op jit(solution)/shard_map/ppermute | solution.py:546
  107.4 6.7 %collective-permute-start.9 = (bf16[256,512]{1,0:T(8,128)(2,1)S(1)}, bf16[256,512]{1,0:T(8,128)(2,1)S(1)}, u32[]{:S(2)}, u32[]{:S(2)}) collective-permute-start(bf16[256,512]{1,0:T(8,128)(2,1)S(1)} %detector_block.11), channel_id=1, source_target_pairs={{256,384},{257,385},{258,386},{259,387},{260,388},{261,389},{262,3... | collective-permute-start | bytes 786440 | tf_op jit(solution)/shard_map/ppermute | solution.py:546
  108.8 6.1 %collective-permute-start.12 = (bf16[256,512]{1,0:T(8,128)(2,1)S(1)}, bf16[256,512]{1,0:T(8,128)(2,1)S(1)}, u32[]{:S(2)}, u32[]{:S(2)}) collective-permute-start(bf16[256,512]{1,0:T(8,128)(2,1)S(1)} %detector_block.12.refs_0_), channel_id=1, source_target_pairs={{385,386},{387,388},{389,390},{391,392},{393,394},{395,396},{397,3... | collective-permute-start | bytes 786440 | tf_op jit(solution)/shard_map/ppermute | solution.py:550
  114.2 1.4 collective-permute-start.11
  114.9 0.7 collective-permute-start.13
  116.2 7.1 %collective-permute-start.14 = (bf16[208,512]{1,0:T(8,128)(2,1)S(1)}, bf16[208,512]{1,0:T(8,128)(2,1)S(1)}, u32[]{:S(2)}, u32[]{:S(2)}) collective-permute-start(bf16[208,512]{1,0:T(8,128)(2,1)S(1)} %get-tuple-element.47), channel_id=1, source_target_pairs={{384,0},{385,1},{386,2},{387,3},{388,4},{389,5},{390,6},{391,7},{3... | collective-permute-start | bytes 638984 | tf_op jit(solution)/shard_map/ppermute | solution.py:554
  116.8 6.4 %collective-permute-start.15 = (bf16[208,512]{1,0:T(8,128)(2,1)S(1)}, bf16[208,512]{1,0:T(8,128)(2,1)S(1)}, u32[]{:S(2)}, u32[]{:S(2)}) collective-permute-start(bf16[208,512]{1,0:T(8,128)(2,1)S(1)} %get-tuple-element.48), channel_id=1, source_target_pairs={{384,128},{385,129},{386,130},{387,131},{388,132},{389,133},{390,1... | collective-permute-start | bytes 638984 | tf_op jit(solution)/shard_map/ppermute | solution.py:554
  117.5 27.6 %collective-permute-start.16 = (bf16[208,512]{1,0:T(8,128)(2,1)S(1)}, bf16[208,512]{1,0:T(8,128)(2,1)S(1)}, u32[]{:S(2)}, u32[]{:S(2)}) collective-permute-start(bf16[208,512]{1,0:T(8,128)(2,1)S(1)} %get-tuple-element.49), channel_id=1, source_target_pairs={{384,256},{385,257},{386,258},{387,259},{388,260},{389,261},{390,2... | collective-permute-start | bytes 638984 | tf_op jit(solution)/shard_map/ppermute | solution.py:554
  118.8 26.3 %copy-start.2 = (f32[2,1024]{1,0:T(2,128)S(1)}, f32[2,1024]{1,0:T(2,128)}, u32[]{:S(2)}) copy-start(f32[2,1024]{1,0:T(2,128)} %refs_6_.1) | copy-start | bytes 24580
Sparse Core Ops, SparseCore 0:
  9.5 54.0 all-gather.2
